TPU v7x, 32 devices: a whole 2x2x4 slice. The times are simulated.
32 devices in a mesh: dp: 8 (over y, x, core), seq: 4 (over z).
Axes of the slice: x: 2, y: 2, z: 4, core: 2. Of those that a mesh axis runs over, the one named last changes fastest.
Arguments:
- inputs: bfloat16 [16, 2048, 1024], P('dp', 'seq'), may hold values from -6 to 6
- cotangent: bfloat16 [16, 2048, 1024], P('dp', 'seq'), may hold values from -6 to 6
- segment_ids: int32 [16, 2048], P('dp'), may hold values from 0 to 21, as said below
- query_weight: bfloat16 [1024, 1024], P(('dp', 'seq')), may hold values from -0.1875 to 0.1875
- key_weight: bfloat16 [1024, 1024], P(('dp', 'seq')), may hold values from -0.1875 to 0.1875
- value_weight: bfloat16 [1024, 1024], P(('dp', 'seq')), may hold values from -0.1875 to 0.1875
- output_weight: bfloat16 [1024, 1024], P(('dp', 'seq')), may hold values from -0.1875 to 0.1875
- up_weight: bfloat16 [1024, 4096], P(('dp', 'seq')), may hold values from -0.1875 to 0.1875
- down_weight: bfloat16 [4096, 1024], P(('dp', 'seq')), may hold values from -0.09375 to 0.09375
- first_gain: float32 [1024], replicated, may hold values from 0.25 to 1.75
- first_shift: float32 [1024], replicated, may hold values from -1 to 1
- query_bias: float32 [1024], replicated, may hold values from -1 to 1
- value_bias: float32 [1024], replicated, may hold values from -1 to 1
- head_scale: float32 [16], replicated, may hold values from 0.3 to 3
- output_bias: float32 [1024], replicated, may hold values from -1 to 1
- post_gain: float32 [1024], replicated, may hold values from 0.25 to 1.75
- post_shift: float32 [1024], replicated, may hold values from -1 to 1
- second_gain: float32 [1024], replicated, may hold values from 0.25 to 1.75
- second_shift: float32 [1024], replicated, may hold values from -1 to 1
- up_bias: float32 [4096], replicated, may hold values from -1 to 1
- middle_gain: float32 [4096], replicated, may hold values from 0.25 to 1.75
- middle_shift: float32 [4096], replicated, may hold values from -1 to 1
- down_bias: float32 [1024], replicated, may hold values from -1 to 1
Outputs:
- layer_output: bfloat16 [16, 2048, 1024], P('dp', 'seq')
- input_grad: bfloat16 [16, 2048, 1024], P('dp', 'seq')
- query_weight_grad: float32 [1024, 1024], P(('dp', 'seq'))
- key_weight_grad: float32 [1024, 1024], P(('dp', 'seq'))
- value_weight_grad: float32 [1024, 1024], P(('dp', 'seq'))
- output_weight_grad: float32 [1024, 1024], P(('dp', 'seq'))
- up_weight_grad: float32 [1024, 4096], P(('dp', 'seq'))
- down_weight_grad: float32 [4096, 1024], P(('dp', 'seq'))
- first_gain_grad: float32 [1024], replicated
- first_shift_grad: float32 [1024], replicated
- query_bias_grad: float32 [1024], replicated
- value_bias_grad: float32 [1024], replicated
- head_scale_grad: float32 [16], replicated
- output_bias_grad: float32 [1024], replicated
- post_gain_grad: float32 [1024], replicated
- post_shift_grad: float32 [1024], replicated
- second_gain_grad: float32 [1024], replicated
- second_shift_grad: float32 [1024], replicated
- up_bias_grad: float32 [4096], replicated
- middle_gain_grad: float32 [4096], replicated
- middle_shift_grad: float32 [4096], replicated
- down_bias_grad: float32 [1024], replicated
Inputs may be any that keep to these rules, and one draw needn't show every extreme that they name: `segment_ids`: along each sequence the ids start at 0 and never fall; each document (a run of equal ids) has 60 to 800 positions, except the last of a sequence, which the sequence's end may cut short; in each sequence the first or the second document has exactly 800 positions; the last sequence reaches the largest id.
All inputs are finite; a program needn't handle non-finite values.
Results may differ from a plain program's by a relative error of at most 0.014.
Values may be sent and summed in bfloat16 or wider, within the bound.
A program may use at most 184 MiB of HBM per device.

v0:
```python
import jax
import jax.numpy as jnp
from jax import lax
from jax.sharding import PartitionSpec as P

EPSILON = 1e-05
MASKED = -1e30


def layer_norm(values, gain_vec, shift_vec):
    row_mean = jnp.mean(values, -1, keepdims=True)
    centred = values - row_mean
    spread = jnp.mean(centred * centred, -1, keepdims=True)
    return centred * lax.rsqrt(spread + EPSILON) * gain_vec + shift_vec


def exact_gelu(values):
    return jax.nn.gelu(values, approximate=False)


def matmul(left_side, right_side):
    return jnp.dot(left_side, right_side, preferred_element_type=jnp.float32)


def contract_rows(left_side, right_side):
    return lax.dot_general(
        left_side, right_side, (((0,), (0,)), ((), ())), preferred_element_type=jnp.float32
    )


def contract_last(left_side, right_side):
    return lax.dot_general(
        left_side, right_side, (((1,), (1,)), ((), ())), preferred_element_type=jnp.float32
    )


def split_heads(matrix, head_count):
    return matrix.reshape(matrix.shape[0], head_count, -1).transpose(1, 0, 2)


def join_heads(stacked):
    return stacked.transpose(1, 0, 2).reshape(stacked.shape[1], -1)


def head_scores(single_query_head, single_key_head, allowed, logit_scale_factor):
    score_matrix = contract_last(single_query_head, single_key_head) * logit_scale_factor
    return jnp.where(allowed, score_matrix, MASKED)


def local(
    inputs,
    cotangent,
    segment_ids,
    query_weight,
    key_weight,
    value_weight,
    output_weight,
    up_weight,
    down_weight,
    first_gain,
    first_shift,
    query_bias,
    value_bias,
    head_scale,
    output_bias,
    post_gain,
    post_shift,
    second_gain,
    second_shift,
    up_bias,
    middle_gain,
    middle_shift,
    down_bias,
):
    micro_count, row_count, model_width = inputs.shape
    hidden_width = up_bias.shape[0]
    head_count = head_scale.shape[0]
    logit_scale_factor = (model_width // head_count) ** (-0.5)
    seq_ranks = lax.axis_size("seq")
    rank_index = lax.axis_index("seq")
    length = row_count * seq_ranks
    query_place = rank_index * row_count + jnp.arange(row_count)
    causal = jnp.arange(length)[None, :] <= query_place[:, None]
    square = (model_width, model_width)
    matrix_sums = [
        jnp.zeros(square, jnp.float32),
        jnp.zeros(square, jnp.float32),
        jnp.zeros(square, jnp.float32),
        jnp.zeros(square, jnp.float32),
        jnp.zeros((model_width, hidden_width), jnp.float32),
        jnp.zeros((hidden_width, model_width), jnp.float32),
    ]
    vectors = (
        first_gain,
        first_shift,
        query_bias,
        value_bias,
        head_scale,
        output_bias,
        post_gain,
        post_shift,
        second_gain,
        second_shift,
        up_bias,
        middle_gain,
        middle_shift,
        down_bias,
    )
    vector_sums = [jnp.zeros_like(tensor) for tensor in vectors]
    outputs = []
    input_grads = []
    for micro_step in range(micro_count):
        tokens = inputs[micro_step].astype(jnp.float32)
        segment_row = segment_ids[micro_step]
        segment_query = lax.dynamic_slice_in_dim(segment_row, rank_index * row_count, row_count)
        attention_full = (
            lax.all_gather(query_weight, ("dp", "seq"), axis=0, tiled=True),
            lax.all_gather(key_weight, ("dp", "seq"), axis=0, tiled=True),
            lax.all_gather(value_weight, ("dp", "seq"), axis=0, tiled=True),
            lax.all_gather(output_weight, ("dp", "seq"), axis=0, tiled=True),
        )
        query_full, key_full, value_full, output_full = attention_full
        normed, first_back = jax.vjp(layer_norm, tokens, first_gain, first_shift)
        normed_low = normed.astype(jnp.bfloat16)
        query_low = (matmul(normed_low, query_full) + query_bias).astype(jnp.bfloat16)
        key_low = matmul(normed_low, key_full).astype(jnp.bfloat16)
        value_low = (matmul(normed_low, value_full) + value_bias).astype(jnp.bfloat16)
        key_all, value_all = (
            lax.all_gather(key_low, "seq", axis=0, tiled=True),
            lax.all_gather(value_low, "seq", axis=0, tiled=True),
        )
        allowed = causal & (segment_row[None, :] == segment_query[:, None])
        query_heads = split_heads(query_low, head_count)
        key_heads = split_heads(key_all, head_count)
        value_heads = split_heads(value_all, head_count)

        def attend(packed):
            single_query_head, single_key_head, single_value_head = packed
            score_matrix = head_scores(
                single_query_head, single_key_head, allowed, logit_scale_factor
            )
            largest = jnp.max(score_matrix, -1, keepdims=True)
            exponent = jnp.exp(score_matrix - largest)
            row_total = jnp.sum(exponent, -1, keepdims=True)
            weights_low = (exponent / row_total).astype(jnp.bfloat16)
            return (matmul(weights_low, single_value_head), (largest + jnp.log(row_total))[:, 0])

        attended, logsums = lax.map(attend, (query_heads, key_heads, value_heads))
        scaled_low = join_heads(attended * head_scale[:, None, None]).astype(jnp.bfloat16)
        branch = matmul(scaled_low, output_full) + output_bias
        posted, post_back = jax.vjp(layer_norm, branch, post_gain, post_shift)
        middle = tokens + posted
        feedforward_full = (
            lax.all_gather(up_weight, ("dp", "seq"), axis=0, tiled=True),
            lax.all_gather(down_weight, ("dp", "seq"), axis=0, tiled=True),
        )
        up_full, down_full = feedforward_full
        normed_two, second_back = jax.vjp(layer_norm, middle, second_gain, second_shift)
        second_low = normed_two.astype(jnp.bfloat16)
        upper_pre = matmul(second_low, up_full) + up_bias
        activated, gelu_back = jax.vjp(exact_gelu, upper_pre)
        mixed, middle_back = jax.vjp(layer_norm, activated, middle_gain, middle_shift)
        mixed_low = mixed.astype(jnp.bfloat16)
        output = middle + matmul(mixed_low, down_full) + down_bias
        outputs.append(output.astype(jnp.bfloat16))
        query_full, key_full, value_full, output_full = (
            lax.all_gather(query_weight, ("dp", "seq"), axis=0, tiled=True),
            lax.all_gather(key_weight, ("dp", "seq"), axis=0, tiled=True),
            lax.all_gather(value_weight, ("dp", "seq"), axis=0, tiled=True),
            lax.all_gather(output_weight, ("dp", "seq"), axis=0, tiled=True),
        )
        up_full, down_full = (
            lax.all_gather(up_weight, ("dp", "seq"), axis=0, tiled=True),
            lax.all_gather(down_weight, ("dp", "seq"), axis=0, tiled=True),
        )
        grad_low = cotangent[micro_step]
        grad_out = grad_low.astype(jnp.float32)
        grad_mixed = contract_last(grad_low, down_full)
        grad_activated, middle_gain_term, middle_shift_term = middle_back(grad_mixed)
        (grad_upper,) = gelu_back(grad_activated)
        upper_low = grad_upper.astype(jnp.bfloat16)
        grad_second = contract_last(upper_low, up_full)
        grad_middle_part, second_gain_term, second_shift_term = second_back(grad_second)
        grad_middle = grad_out + grad_middle_part
        grad_branch, post_gain_term, post_shift_term = post_back(grad_middle)
        branch_low = grad_branch.astype(jnp.bfloat16)
        grad_scaled = split_heads(contract_last(branch_low, output_full), head_count)
        head_term = jnp.sum(grad_scaled * attended, axis=(1, 2))
        grad_attended = (grad_scaled * head_scale[:, None, None]).astype(jnp.bfloat16)

        def attend_back(packed):
            single_query_head, single_key_head, single_value_head, grad_head, logsum = packed
            score_matrix = head_scores(
                single_query_head, single_key_head, allowed, logit_scale_factor
            )
            attention_probabilities = jnp.exp(score_matrix - logsum[:, None])
            weights_low = attention_probabilities.astype(jnp.bfloat16)
            grad_weights = contract_last(grad_head, single_value_head)
            grad_value = contract_rows(weights_low, grad_head)
            row_inner = jnp.sum(attention_probabilities * grad_weights, -1, keepdims=True)
            grad_scores = (attention_probabilities * (grad_weights - row_inner)).astype(
                jnp.bfloat16
            )
            grad_query = matmul(grad_scores, single_key_head) * logit_scale_factor
            grad_key = contract_rows(grad_scores, single_query_head) * logit_scale_factor
            return (grad_query, grad_key, grad_value)

        grad_queries, grad_keys, grad_values = lax.map(
            attend_back, (query_heads, key_heads, value_heads, grad_attended, logsums)
        )
        query_grad_low = join_heads(grad_queries).astype(jnp.bfloat16)
        key_sum, value_sum = (
            lax.psum_scatter(
                join_heads(grad_keys).astype(jnp.bfloat16), "seq", scatter_dimension=0, tiled=True
            ).astype(jnp.float32),
            lax.psum_scatter(
                join_heads(grad_values).astype(jnp.bfloat16), "seq", scatter_dimension=0, tiled=True
            ).astype(jnp.float32),
        )
        key_grad_low = key_sum.astype(jnp.bfloat16)
        value_grad_low = value_sum.astype(jnp.bfloat16)
        grad_normed = (
            contract_last(query_grad_low, query_full)
            + contract_last(key_grad_low, key_full)
            + contract_last(value_grad_low, value_full)
        )
        grad_tokens, first_gain_term, first_shift_term = first_back(grad_normed)
        input_grads.append((grad_middle + grad_tokens).astype(jnp.bfloat16))
        matrix_terms = (
            contract_rows(normed_low, query_grad_low),
            contract_rows(normed_low, key_grad_low),
            contract_rows(normed_low, value_grad_low),
            contract_rows(scaled_low, branch_low),
            contract_rows(second_low, upper_low),
            contract_rows(mixed_low, grad_low),
        )
        matrix_sums = [running + adding for running, adding in zip(matrix_sums, matrix_terms)]
        vector_terms = (
            first_gain_term,
            first_shift_term,
            jnp.sum(query_grad_low.astype(jnp.float32), 0),
            jnp.sum(value_grad_low.astype(jnp.float32), 0),
            head_term,
            jnp.sum(branch_low.astype(jnp.float32), 0),
            post_gain_term,
            post_shift_term,
            second_gain_term,
            second_shift_term,
            jnp.sum(upper_low.astype(jnp.float32), 0),
            middle_gain_term,
            middle_shift_term,
            jnp.sum(grad_out, 0),
        )
        vector_sums = [running + adding for running, adding in zip(vector_sums, vector_terms)]
    weight_parts = (
        lax.psum_scatter(matrix_sums[0], ("dp", "seq"), scatter_dimension=0, tiled=True),
        lax.psum_scatter(matrix_sums[1], ("dp", "seq"), scatter_dimension=0, tiled=True),
        lax.psum_scatter(matrix_sums[2], ("dp", "seq"), scatter_dimension=0, tiled=True),
        lax.psum_scatter(matrix_sums[3], ("dp", "seq"), scatter_dimension=0, tiled=True),
        lax.psum_scatter(matrix_sums[4], ("dp", "seq"), scatter_dimension=0, tiled=True),
        lax.psum_scatter(matrix_sums[5], ("dp", "seq"), scatter_dimension=0, tiled=True),
    )
    vector_parts = lax.psum(
        (
            vector_sums[0],
            vector_sums[1],
            vector_sums[2],
            vector_sums[3],
            vector_sums[4],
            vector_sums[5],
            vector_sums[6],
            vector_sums[7],
            vector_sums[8],
            vector_sums[9],
            vector_sums[10],
            vector_sums[11],
            vector_sums[12],
            vector_sums[13],
        ),
        ("dp", "seq"),
    )
    return (
        jnp.stack(outputs),
        jnp.stack(input_grads),
        weight_parts[0],
        weight_parts[1],
        weight_parts[2],
        weight_parts[3],
        weight_parts[4],
        weight_parts[5],
        vector_parts[0],
        vector_parts[1],
        vector_parts[2],
        vector_parts[3],
        vector_parts[4],
        vector_parts[5],
        vector_parts[6],
        vector_parts[7],
        vector_parts[8],
        vector_parts[9],
        vector_parts[10],
        vector_parts[11],
        vector_parts[12],
        vector_parts[13],
    )


def solution(mesh):
    in_specs = (
        P("dp", "seq", None),
        P("dp", "seq", None),
        P("dp", None),
        P(("dp", "seq"), None),
        P(("dp", "seq"), None),
        P(("dp", "seq"), None),
        P(("dp", "seq"), None),
        P(("dp", "seq"), None),
        P(("dp", "seq"), None),
        P(),
        P(),
        P(),
        P(),
        P(),
        P(),
        P(),
        P(),
        P(),
        P(),
        P(),
        P(),
        P(),
        P(),
    )
    out_specs = (
        P("dp", "seq", None),
        P("dp", "seq", None),
        P(("dp", "seq"), None),
        P(("dp", "seq"), None),
        P(("dp", "seq"), None),
        P(("dp", "seq"), None),
        P(("dp", "seq"), None),
        P(("dp", "seq"), None),
        P(),
        P(),
        P(),
        P(),
        P(),
        P(),
        P(),
        P(),
        P(),
        P(),
        P(),
        P(),
        P(),
        P(),
    )
    return jax.shard_map(local, mesh=mesh, in_specs=in_specs, out_specs=out_specs, check_vma=False)
```

profile of v0, /device:TPU:0, one launch (start us, length us, event | category | flops | bytes accessed | tf_op | source)
XLA Modules:
  0.0 2929.4 jit_solution(12358509383623044732)
XLA Ops:
  12.2 57.9 %all-gather.13.cloned.1.call-done = bf16[1024,1024]{1,0:T(8,128)(2,1)} async-done(((bf16[32,1024]{1,0:T(8,128)(2,1)}), bf16[1024,1024]{1,0:T(8,128)(2,1)}) %all-gather.13.cloned.1.call-update) | async-done | bytes 2097168 | tf_op jit(solution)/shard_map/all_gather | solution.py:118
  74.1 54.2 %all-gather.17.cloned.1.call-done = bf16[1024,1024]{1,0:T(8,128)(2,1)} async-done(((bf16[32,1024]{1,0:T(8,128)(2,1)}), bf16[1024,1024]{1,0:T(8,128)(2,1)}) %all-gather.17.cloned.1.call-update) | async-done | bytes 2097168 | tf_op jit(solution)/shard_map/all_gather | solution.py:119
  143.7 42.7 %all-gather.11.cloned.1.call-done = bf16[1024,1024]{1,0:T(8,128)(2,1)} async-done(((bf16[32,1024]{1,0:T(8,128)(2,1)}), bf16[1024,1024]{1,0:T(8,128)(2,1)}) %all-gather.11.cloned.1.call-update) | async-done | bytes 2097168 | tf_op jit(solution)/shard_map/all_gather | solution.py:117
  202.6 64.8 %all-gather.15.cloned.1.call-done = bf16[2048,1024]{1,0:T(8,128)(2,1)} async-done(((bf16[512,1024]{1,0:T(8,128)(2,1)}), bf16[2048,1024]{1,0:T(8,128)(2,1)}) %all-gather.15.cloned.1.call-update) | async-done | bytes 4194320 | tf_op jit(solution)/shard_map/all_gather | solution.py:129
  282.4 65.8 %all-gather.19.cloned.1.call-done = bf16[2048,1024]{1,0:T(8,128)(2,1)} async-done(((bf16[512,1024]{1,0:T(8,128)(2,1)}), bf16[2048,1024]{1,0:T(8,128)(2,1)}) %all-gather.19.cloned.1.call-update) | async-done | bytes 4194320 | tf_op jit(solution)/shard_map/all_gather | solution.py:130
  364.8 94.9 %while.56 = (s32[]{:T(128)}, f32[16,512,64]{1,2,0:T(8,128)}, f32[16,512]{1,0:T(8,128)S(1)}, bf16[16,512,64]{2,1,0:T(8,128)(2,1)}, bf16[16,2048,64]{2,1,0:T(8,128...) while((s32[]{:T(128)}, f32[16,512,64]{1,2,0:T(8,128)}, ...), condition=%wide.region_5.6_spmd.clone, body=%wide.region_2.5_spmd.clone.sunk | while | flops 279969280 | bytes 13928569 | solution.py:148
  474.7 34.9 %all-gather.29.cloned.1.call-done = bf16[2048,1024]{1,0:T(8,128)(2,1)} async-done(((bf16[512,1024]{1,0:T(8,128)(2,1)}), bf16[2048,1024]{1,0:T(8,128)(2,1)}) %all-gather.29.cloned.1.call-update) | async-done | bytes 4194320 | tf_op jit(solution)/shard_map/all_gather | solution.py:130
  526.2 95.1 %while.57 = (s32[]{:T(128)}, f32[16,512,64]{1,2,0:T(8,128)}, f32[16,512]{1,0:T(8,128)S(1)}, bf16[16,512,64]{2,1,0:T(8,128)(2,1)}, bf16[16,2048,64]{2,1,0:T(8,128...) while((s32[]{:T(128)}, f32[16,512,64]{1,2,0:T(8,128)}, ...), condition=%wide.region_17.18_spmd.clone, body=%wide.region_14.17_spmd.clone.sunk | while | flops 279969280 | bytes 13928569 | solution.py:148
  654.2 49.0 %fusion.197 = (f32[512]{0:T(512)S(1)}, f32[512,4096]{1,0:T(8,128)}, f32[512,4096]{1,0:T(8,128)}, f32[512]{0:T(512)S(1)}, f32[512,4096]{1,0:T(8,128)}, /*index=5*/f32[512,4096]{1,0:T(8,128)}, f32[512,4096]{1,0:T(8,128)}) fusion(f32[4096]{0:T(1024)S(1)} %copy-done.107, f32[512,4096]{1,0:T(8,128)S(1)} %fusion.178, ...), kind=kOutput, calls=%fused_computation.343 | convolution fusion | flops 4574411776 | bytes 60850176 | tf_op jit(solution)/shard_map/dot_general | solution.py:22
  703.3 21.7 all-gather.25.cloned.1.call-done
  736.5 17.3 multiply_reduce_fusion.5
  769.0 24.0 convert_reduce_fusion
  834.1 178.3 %while.59 = (s32[]{:T(128)}, bf16[16,512,64]{1,2,0:T(8,128)(2,1)S(1)}, bf16[16,2048,64]{1,2,0:T(8,128)(2,1)}, bf16[16,2048,64]{1,2,0:T(8,128)(2,1)}, bf16[16,512...) while((s32[]{:T(128)}, ...), condition=%wide.region_45.46_spmd.clone, body=%wide.region_43.45_spmd.clone.sunk | while | flops 683834880 | bytes 34630792 | solution.py:208
  1017.5 178.0 %while.58 = (s32[]{:T(128)}, bf16[16,512,64]{1,2,0:T(8,128)(2,1)S(1)}, bf16[16,2048,64]{1,2,0:T(8,128)(2,1)}, bf16[16,2048,64]{1,2,0:T(8,128)(2,1)}, bf16[16,512...) while((s32[]{:T(128)}, ...), condition=%wide.region_32.33_spmd.clone, body=%wide.region_30.32_spmd.clone.sunk | while | flops 683834880 | bytes 34630792 | solution.py:208
  1233.7 37.4 %reduce-scatter.11.cloned.1.call-done = bf16[512,1024]{0,1:T(8,128)(2,1)} async-done(((bf16[2048,1024]{0,1:T(8,128)(2,1)}), bf16[512,1024]{0,1:T(8,128)(2,1)}) %reduce-scatter.11.cloned.1.call-update) | async-done | bytes 1048592 | tf_op jit(solution)/shard_map/reduce_scatter | solution.py:213
  1275.6 75.1 %reduce-scatter.17.cloned.1.call-done = bf16[512,1024]{0,1:T(8,128)(2,1)} async-done(((bf16[2048,1024]{0,1:T(8,128)(2,1)}), bf16[512,1024]{0,1:T(8,128)(2,1)}) %reduce-scatter.17.cloned.1.call-update) | async-done | bytes 1048592 | tf_op jit(solution)/shard_map/reduce_scatter | solution.py:216
  1356.5 73.7 %reduce-scatter.13.cloned.1.call-done = bf16[512,1024]{0,1:T(8,128)(2,1)} async-done(((bf16[2048,1024]{0,1:T(8,128)(2,1)}), bf16[512,1024]{0,1:T(8,128)(2,1)}) %reduce-scatter.13.cloned.1.call-update) | async-done | bytes 1048592 | tf_op jit(solution)/shard_map/reduce_scatter | solution.py:216
  1538.7 43.8 %reduce-scatter.19.cloned.1.call-done = f32[32,1024]{1,0:T(8,128)} async-done(((f32[1024,1024]{1,0:T(8,128)}), f32[32,1024]{1,0:T(8,128)}) %reduce-scatter.19.cloned.1.call-update) | async-done | bytes 131088 | tf_op jit(solution)/shard_map/reduce_scatter | solution.py:256
  1582.5 150.5 %reduce-scatter.25.cloned.1.call-done = f32[32,1024]{1,0:T(8,128)} async-done(((f32[1024,1024]{1,0:T(8,128)}), f32[32,1024]{1,0:T(8,128)}) %reduce-scatter.25.cloned.1.call-update) | async-done | bytes 131088 | tf_op jit(solution)/shard_map/reduce_scatter | solution.py:259
  1733.1 140.5 %all-reduce.3.cloned.1.call-done = (f32[1024]{0:T(1024)}, f32[1024]{0:T(1024)}, f32[1024]{0:T(1024)}, f32[1024]{0:T(1024)}, f32[16]{0:T(128)}, /*index=5*/f32[10...) async-done(((f32[1024]{0:T(1024)}, f32[1024]{0:T(1024)}, ...) | async-done | bytes 90192 | tf_op jit(solution)/shard_map/psum | solution.py:263
  1873.6 153.3 %reduce-scatter.21.cloned.1.call-done = f32[32,1024]{1,0:T(8,128)} async-done(((f32[1024,1024]{1,0:T(8,128)}), f32[32,1024]{1,0:T(8,128)}) %reduce-scatter.21.cloned.1.call-update) | async-done | bytes 131088 | tf_op jit(solution)/shard_map/reduce_scatter | solution.py:257
  2026.9 150.5 %reduce-scatter.23.cloned.1.call-done = f32[32,1024]{1,0:T(8,128)} async-done(((f32[1024,1024]{1,0:T(8,128)}), f32[32,1024]{1,0:T(8,128)}) %reduce-scatter.23.cloned.1.call-update) | async-done | bytes 131088 | tf_op jit(solution)/shard_map/reduce_scatter | solution.py:258
  2177.4 362.3 %reduce-scatter.27.cloned.1.call-done = f32[32,4096]{1,0:T(8,128)} async-done(((f32[1024,4096]{1,0:T(8,128)}), f32[32,4096]{1,0:T(8,128)}) %reduce-scatter.27.cloned.1.call-update) | async-done | bytes 524304 | tf_op jit(solution)/shard_map/reduce_scatter | solution.py:260
  2539.8 364.8 %reduce-scatter.29.cloned.1.call-done = f32[128,1024]{1,0:T(8,128)} async-done(((f32[4096,1024]{1,0:T(8,128)}), f32[128,1024]{1,0:T(8,128)}) %reduce-scatter.29.cloned.1.call-update) | async-done | bytes 524304 | tf_op jit(solution)/shard_map/reduce_scatter | solution.py:261
  (840 shorter events, 927.2 us)
Async XLA Ops:
  7.2 62.9 %all-gather.13.cloned.1.call-start = ((), (), s32[]{:S(2)}) async-start(), calls=%async_computation.11 | async-start | bytes 2162688 | tf_op jit(solution)/shard_map/all_gather | solution.py:118
  7.9 120.3 %all-gather.17.cloned.1.call-start = ((), (), s32[]{:S(2)}) async-start(), calls=%async_computation.13 | async-start | bytes 2162688 | tf_op jit(solution)/shard_map/all_gather | solution.py:119
  8.7 177.7 %all-gather.11.cloned.1.call-start = ((), (), s32[]{:S(2)}) async-start(), calls=%async_computation.10 | async-start | bytes 2162688 | tf_op jit(solution)/shard_map/all_gather | solution.py:117
  9.4 258.0 %all-gather.15.cloned.1.call-start = ((), (), s32[]{:S(2)}) async-start(), calls=%async_computation.12 | async-start | bytes 5242880 | tf_op jit(solution)/shard_map/all_gather | solution.py:129
  11.4 183.9 %copy-start.53 = (f32[512]{0:T(512)}, f32[512]{0:T(512)S(1)}, u32[]{:S(2)}) copy-start(f32[512]{0:T(512)S(1)} %get-tuple-element.588) | copy-start | bytes 6148
  74.0 274.1 %all-gather.19.cloned.1.call-start = ((), (), s32[]{:S(2)}) async-start(), calls=%async_computation.14 | async-start | bytes 5242880 | tf_op jit(solution)/shard_map/all_gather | solution.py:130
  132.1 327.6 %all-gather.27.cloned.1.call-start = ((), (), s32[]{:S(2)}) async-start(), calls=%async_computation.18 | async-start | bytes 5242880 | tf_op jit(solution)/shard_map/all_gather | solution.py:129
  136.1 373.5 %all-gather.29.cloned.1.call-start = ((), (), s32[]{:S(2)}) async-start(), calls=%async_computation.19 | async-start | bytes 5242880 | tf_op jit(solution)/shard_map/all_gather | solution.py:130
  140.2 485.7 %all-gather.21.cloned.1.call-start = ((), (), s32[]{:S(2)}) async-start(), calls=%async_computation.15 | async-start | bytes 2162688 | tf_op jit(solution)/shard_map/all_gather | solution.py:120
  140.9 505.4 %all-gather.23.cloned.1.call-start = ((), (), s32[]{:S(2)}) async-start(), calls=%async_computation.16 | async-start | bytes 8650752 | tf_op jit(solution)/shard_map/all_gather | solution.py:154
  141.7 583.3 %all-gather.25.cloned.1.call-start = ((), (), s32[]{:S(2)}) async-start(), calls=%async_computation.17 | async-start | bytes 8650752 | tf_op jit(solution)/shard_map/all_gather | solution.py:155
  142.3 1086.9 %reduce-scatter.15.cloned.1.call-start = ((), (), s32[]{:S(2)}) async-start(), calls=%async_computation.22 | async-start | bytes 5242880 | tf_op jit(solution)/shard_map/reduce_scatter | solution.py:213
  634.1 179.6 %copy-start.95 = (f32[512]{0:T(512)}, f32[512]{0:T(512)S(1)}, u32[]{:S(2)}) copy-start(f32[512]{0:T(512)S(1)} %broadcast_multiply_fusion.5) | copy-start | bytes 6148
  635.7 178.0 %copy-start.115 = (f32[512]{0:T(512)}, f32[512]{0:T(512)S(1)}, u32[]{:S(2)}) copy-start(f32[512]{0:T(512)S(1)} %fusion.168) | copy-start | bytes 6148
  1012.4 258.7 %reduce-scatter.11.cloned.1.call-start = ((), (), s32[]{:S(2)}) async-start(), calls=%async_computation.20 | async-start | bytes 5242880 | tf_op jit(solution)/shard_map/reduce_scatter | solution.py:213
  1196.5 154.2 %reduce-scatter.17.cloned.1.call-start = ((), (), s32[]{:S(2)}) async-start(), calls=%async_computation.23 | async-start | bytes 5242880 | tf_op jit(solution)/shard_map/reduce_scatter | solution.py:216
  1197.2 233.0 %reduce-scatter.13.cloned.1.call-start = ((), (), s32[]{:S(2)}) async-start(), calls=%async_computation.21 | async-start | bytes 5242880 | tf_op jit(solution)/shard_map/reduce_scatter | solution.py:216
  1197.8 384.7 %reduce-scatter.19.cloned.1.call-start = ((), (), s32[]{:S(2)}) async-start(), calls=%async_computation.24 | async-start | bytes 4325376 | tf_op jit(solution)/shard_map/reduce_scatter | solution.py:256
  1205.2 527.8 %reduce-scatter.25.cloned.1.call-start = ((), (), s32[]{:S(2)}) async-start(), calls=%async_computation.27 | async-start | bytes 4325376 | tf_op jit(solution)/shard_map/reduce_scatter | solution.py:259
  1211.7 661.9 %all-reduce.3.cloned.1.call-start = ((), (), s32[]{:S(2)}) async-start(), calls=%async_computation.30 | async-start | bytes 181248 | tf_op jit(solution)/shard_map/psum | solution.py:263
  1440.9 586.0 %reduce-scatter.21.cloned.1.call-start = ((), (), s32[]{:S(2)}) async-start(), calls=%async_computation.25 | async-start | bytes 4325376 | tf_op jit(solution)/shard_map/reduce_scatter | solution.py:257
  1447.7 729.7 %reduce-scatter.23.cloned.1.call-start = ((), (), s32[]{:S(2)}) async-start(), calls=%async_computation.26 | async-start | bytes 4325376 | tf_op jit(solution)/shard_map/reduce_scatter | solution.py:258
  1454.1 1085.6 %reduce-scatter.27.cloned.1.call-start = ((), (), s32[]{:S(2)}) async-start(), calls=%async_computation.28 | async-start | bytes 17301504 | tf_op jit(solution)/shard_map/reduce_scatter | solution.py:260
  1480.2 1424.4 %reduce-scatter.29.cloned.1.call-start = ((), (), s32[]{:S(2)}) async-start(), calls=%async_computation.29 | async-start | bytes 17301504 | tf_op jit(solution)/shard_map/reduce_scatter | solution.py:261
  (131 other events, 2037.9 us)
Sparse Core Ops, SparseCore 0:
  10.9 59.0 all-gather.12
  73.0 55.1 all-gather.16
  131.2 55.1 all-gather.10
  187.8 79.5 all-gather.14
  268.9 79.2 all-gather.18
  349.5 79.2 all-gather.26
  430.4 79.2 all-gather.28
  512.6 54.8 all-gather.20
  570.4 75.9 all-gather.22
  649.1 75.7 all-gather.24
  1012.5 75.4 reduce-scatter.14
  1195.7 75.3 reduce-scatter.10
  1273.4 77.3 reduce-scatter.16
  1352.9 77.2 reduce-scatter.12
  1432.9 149.5 reduce-scatter.18
  1585.2 147.7 reduce-scatter.24
  1740.5 133.0 all-reduce.2
  1876.3 150.5 reduce-scatter.20
  2029.7 147.6 reduce-scatter.22
  2180.1 359.5 reduce-scatter.26
  2542.6 361.9 reduce-scatter.28
where the time goes:
time: 2950 us; the launch traced here: 2930 us
  waiting for transfers between devices  1910 us (65%)
  matrix products  750 us (25%)
  local copies, waits for them, and re-layouts  137 us (5%)
  other arithmetic  113 us (4%)
    reduce_scatter x1, waiting for transfers between devices, local(): lax.psum_scatter(matrix_sums[5], ('dp', 'seq'), scatter_dimension=0, tile...  365 us
    reduce_scatter x1, waiting for transfers between devices, local(): lax.psum_scatter(matrix_sums[4], ('dp', 'seq'), scatter_dimension=0, tile...  362 us
    dot_general x108, matrix products, contract_last(): lax.dot_general(left_side, right_side, (((1,), (1,)), ((), ())), preferre...  309 us
    dot_general x76, matrix products, matmul(): return jnp.dot(left_side, right_side, preferred_element_type=jnp.float32)  254 us
    dot_general x76, matrix products, contract_rows(): lax.dot_general(left_side, right_side, (((0,), (0,)), ((), ())), preferre...  187 us
    reduce_scatter x1, waiting for transfers between devices, local(): lax.psum_scatter(matrix_sums[1], ('dp', 'seq'), scatter_dimension=0, tile...  153 us
    reduce_scatter x1, waiting for transfers between devices, local(): lax.psum_scatter(matrix_sums[2], ('dp', 'seq'), scatter_dimension=0, tile...  151 us
    reduce_scatter x1, waiting for transfers between devices, local(): lax.psum_scatter(matrix_sums[3], ('dp', 'seq'), scatter_dimension=0, tile...  151 us
  transfers between devices with their start and end apart: 21, of which 18 were waited for; matrix products, arithmetic and copies ran while one was open for 23% of the time, Pallas kernels for 0%

commit v1 on v0

v1 whole, which is shorter than its diff:
```python
import functools

import jax
import jax.numpy as jnp
from jax import lax
from jax.experimental import pallas as pl
from jax.experimental.pallas import tpu as pltpu
from jax.sharding import PartitionSpec as P

EPSILON = 1e-05
MASKED = -1e30
DOCUMENT_MAX = 800
BLOCK = 256
LANES = 256
BOTH = ("dp", "seq")


def dot_nn(a, b):
    return lax.dot_general(a, b, (((1,), (0,)), ((), ())), preferred_element_type=jnp.float32)


def dot_nt(a, b):
    return lax.dot_general(a, b, (((1,), (1,)), ((), ())), preferred_element_type=jnp.float32)


def dot_tn(a, b):
    return lax.dot_general(a, b, (((0,), (0,)), ((), ())), preferred_element_type=jnp.float32)


def moments(values):
    row_mean = jnp.mean(values, -1, keepdims=True)
    centred = values - row_mean
    spread = jnp.mean(centred * centred, -1, keepdims=True)
    scale = lax.rsqrt(spread + EPSILON)
    return centred * scale, scale


def norm_back(hat, scale, gain, grad):
    weighted = gain * grad
    first = jnp.mean(weighted, -1, keepdims=True)
    second = jnp.mean(weighted * hat, -1, keepdims=True)
    return scale * (weighted - first - hat * second)


def pick_lanes(block, head, width):
    lane = lax.broadcasted_iota(jnp.int32, block.shape, 1)
    inside = (lane >= head * width) & (lane < (head + 1) * width)
    return jnp.where(inside, block, jnp.zeros_like(block))


def key_blocks(rows, hops):
    blocks = []
    for block in range(rows // BLOCK):
        blocks.append((0, block * BLOCK, BLOCK, block * BLOCK))
    place = 0
    for hop, hop_rows in enumerate(hops):
        place -= hop_rows
        if hop_rows % BLOCK == 0:
            for block in reversed(range(hop_rows // BLOCK)):
                blocks.append((hop + 1, block * BLOCK, BLOCK, place + block * BLOCK))
        else:
            blocks.append((hop + 1, 0, hop_rows, place))
    return blocks


def mask_scores(scores, first_key, start_row, first_query, diagonal):
    place = first_key + lax.broadcasted_iota(jnp.int32, scores.shape, 0)
    ok = place >= start_row
    if diagonal:
        ok = ok & (place <= first_query + lax.broadcasted_iota(jnp.int32, scores.shape, 1))
    return jnp.where(ok, scores, MASKED)


def attend_kernel(pieces, hops, heads, width, factor, first_ref, scale_ref, q_ref, *refs):
    keys, values = refs[:pieces], refs[pieces : 2 * pieces]
    start_ref, out_ref, lse_ref, qh_ref, m_ref, l_ref, acc_ref = refs[2 * pieces :]
    sequence, group = pl.program_id(0), pl.program_id(1)
    rows = q_ref.shape[1]
    blocks = key_blocks(rows, hops)
    for qi in range(rows // BLOCK):
        first_query = qi * BLOCK
        first = first_ref[sequence, qi]
        start_row = start_ref[0, :, first_query : first_query + BLOCK]
        q_block = q_ref[0, first_query : first_query + BLOCK, :] * factor
        for head in range(heads):
            qh_ref[head] = pick_lanes(q_block, head, width)

        def body(piece, offset, count, place, fresh):
            key = keys[piece][0, offset : offset + count, :]
            value_t = values[piece][0, offset : offset + count, :].T
            for head in range(heads):
                scores = dot_nt(key, qh_ref[head])
                scores = mask_scores(scores, place, start_row, first_query, fresh)
                top = jnp.max(scores, 0, keepdims=True)
                lanes = slice(head * width, (head + 1) * width)
                if fresh:
                    weights = jnp.exp(scores - top)
                    l_ref[head : head + 1] = jnp.sum(weights, 0, keepdims=True)
                    acc_ref[lanes] = dot_nn(value_t[lanes], weights.astype(jnp.bfloat16))
                    m_ref[head : head + 1] = top
                else:
                    before = m_ref[head : head + 1]
                    top = jnp.maximum(before, top)
                    fade = jnp.exp(before - top)
                    weights = jnp.exp(scores - top)
                    l_ref[head : head + 1] = l_ref[head : head + 1] * fade + jnp.sum(weights, 0, keepdims=True)
                    acc_ref[lanes] = acc_ref[lanes] * fade + dot_nn(value_t[lanes], weights.astype(jnp.bfloat16))
                    m_ref[head : head + 1] = top

        body(*blocks[qi], True)
        for block in reversed(blocks[:qi]):
            pl.when(first < block[3] + block[2])(functools.partial(body, *block, False))
        for block in blocks[rows // BLOCK :]:
            pl.when(first < block[3] + block[2])(functools.partial(body, *block, False))
        total = l_ref[...]
        lse_ref[0, 0, :, first_query : first_query + BLOCK] = m_ref[...] + jnp.log(total)
        for head in range(heads):
            lanes = slice(head * width, (head + 1) * width)
            acc_ref[lanes] = acc_ref[lanes] * (scale_ref[group * heads + head] / total[head : head + 1])
        out_ref[0, first_query : first_query + BLOCK, :] = acc_ref[...].T.astype(jnp.bfloat16)


def attend(first, head_scale, query, keys, values, start, hops):
    sequences, rows, model = query.shape
    head_count = head_scale.shape[0]
    width = model // head_count
    heads = LANES // width
    groups = model // LANES
    pieces = len(keys)
    wide = lambda count: pl.BlockSpec((1, count, LANES), lambda s, g, *_: (s, 0, g))
    counts = [k.shape[1] for k in keys]
    kernel = functools.partial(attend_kernel, pieces, hops, heads, width, width ** (-0.5))
    return pl.pallas_call(
        kernel,
        grid_spec=pltpu.PrefetchScalarGridSpec(
            num_scalar_prefetch=2,
            grid=(sequences, groups),
            in_specs=[wide(rows)] + [wide(c) for c in counts] * 2
            + [pl.BlockSpec((1, 1, rows), lambda s, g, *_: (s, 0, 0))],
            out_specs=[wide(rows), pl.BlockSpec((1, 1, heads, rows), lambda s, g, *_: (s, g, 0, 0))],
            scratch_shapes=[
                pltpu.VMEM((heads, BLOCK, LANES), jnp.bfloat16),
                pltpu.VMEM((heads, BLOCK), jnp.float32),
                pltpu.VMEM((heads, BLOCK), jnp.float32),
                pltpu.VMEM((LANES, BLOCK), jnp.float32),
            ],
        ),
        out_shape=[
            jax.ShapeDtypeStruct((sequences, rows, model), jnp.bfloat16),
            jax.ShapeDtypeStruct((sequences, groups, heads, rows), jnp.float32),
        ],
        name="attend",
    )(first, head_scale, query, *keys, *values, start)


def attend_back_kernel(pieces, hops, heads, width, factor, first_ref, scale_ref, q_ref, *refs):
    keys, values = refs[:pieces], refs[pieces : 2 * pieces]
    start_ref, lse_ref, out_ref, grad_ref = refs[2 * pieces : 2 * pieces + 4]
    dq_ref = refs[2 * pieces + 4]
    dkeys = refs[2 * pieces + 5 : 3 * pieces + 5]
    dvalues = refs[3 * pieces + 5 : 4 * pieces + 5]
    qh_ref, gh_ref, delta_ref, p_ref, ds_ref, dq_acc, dk_acc, dv_acc = refs[4 * pieces + 5 :]
    sequence, group = pl.program_id(0), pl.program_id(1)
    rows = q_ref.shape[1]
    query_blocks = rows // BLOCK
    for qi in range(query_blocks):
        here = slice(qi * BLOCK, (qi + 1) * BLOCK)
        q_block = q_ref[0, here, :] * factor
        grad = grad_ref[0, here, :]
        product = (grad.astype(jnp.float32) * out_ref[0, here, :].astype(jnp.float32)).T
        for head in range(heads):
            lanes = slice(head * width, (head + 1) * width)
            spot = slice(head * BLOCK, (head + 1) * BLOCK)
            qh_ref[qi, spot] = pick_lanes(q_block, head, width)
            gh_ref[qi, spot] = pick_lanes(grad, head, width)
            delta_ref[head : head + 1, here] = jnp.sum(product[lanes], 0, keepdims=True) / scale_ref[group * heads + head]
    dq_acc[...] = jnp.zeros_like(dq_acc)
    for piece, offset, count, place in key_blocks(rows, hops):
        key = keys[piece][0, offset : offset + count, :]
        key_t = key.T
        value = values[piece][0, offset : offset + count, :]
        dk_acc[:count] = jnp.zeros((count, LANES), jnp.float32)
        dv_acc[:count] = jnp.zeros((count, LANES), jnp.float32)
        for qi in range(query_blocks):
            first_query = qi * BLOCK
            if place > first_query:
                continue

            def body():
                here = slice(first_query, first_query + BLOCK)
                start_row = start_ref[0, :, here]
                for head in range(heads):
                    lanes = slice(head * width, (head + 1) * width)
                    spot = slice(head * BLOCK, (head + 1) * BLOCK)
                    scores = dot_nt(key, qh_ref[qi, spot])
                    scores = mask_scores(scores, place, start_row, first_query, place == first_query)
                    weights = jnp.exp(scores - lse_ref[0, 0, head : head + 1, here])
                    dweights = dot_nt(value, gh_ref[qi, spot])
                    dscores = (weights * (dweights - delta_ref[head : head + 1, here])).astype(jnp.bfloat16)
                    p_ref[:count, spot] = weights.astype(jnp.bfloat16)
                    ds_ref[:count, spot] = dscores
                    dq_acc[lanes, here] += dot_nn(key_t[lanes], dscores)
                dv_acc[:count] += dot_nn(p_ref[:count], gh_ref[qi])
                dk_acc[:count] += dot_nn(ds_ref[:count], qh_ref[qi])

            if place == first_query:
                body()
            else:
                pl.when(first_ref[sequence, qi] < place + count)(body)
        dkeys[piece][0, offset : offset + count, :] = dk_acc[:count].astype(jnp.bfloat16)
        dvalues[piece][0, offset : offset + count, :] = dv_acc[:count].astype(jnp.bfloat16)
    for qi in range(query_blocks):
        here = slice(qi * BLOCK, (qi + 1) * BLOCK)
        dq_ref[0, here, :] = (dq_acc[:, here] * factor).T.astype(jnp.bfloat16)


def attend_back(first, head_scale, query, keys, values, start, lse, scaled, grad, hops):
    sequences, rows, model = query.shape
    head_count = head_scale.shape[0]
    width = model // head_count
    heads = LANES // width
    groups = model // LANES
    pieces = len(keys)
    wide = lambda count: pl.BlockSpec((1, count, LANES), lambda s, g, *_: (s, 0, g))
    counts = [k.shape[1] for k in keys]
    most = max([BLOCK] + [c for c in counts if c % BLOCK])
    kernel = functools.partial(attend_back_kernel, pieces, hops, heads, width, width ** (-0.5))
    shape = lambda count: jax.ShapeDtypeStruct((sequences, count, model), jnp.bfloat16)
    results = pl.pallas_call(
        kernel,
        grid_spec=pltpu.PrefetchScalarGridSpec(
            num_scalar_prefetch=2,
            grid=(sequences, groups),
            in_specs=[wide(rows)] + [wide(c) for c in counts] * 2
            + [
                pl.BlockSpec((1, 1, rows), lambda s, g, *_: (s, 0, 0)),
                pl.BlockSpec((1, 1, heads, rows), lambda s, g, *_: (s, g, 0, 0)),
                wide(rows),
                wide(rows),
            ],
            out_specs=[wide(rows)] + [wide(c) for c in counts] * 2,
            scratch_shapes=[
                pltpu.VMEM((rows // BLOCK, heads * BLOCK, LANES), jnp.bfloat16),
                pltpu.VMEM((rows // BLOCK, heads * BLOCK, LANES), jnp.bfloat16),
                pltpu.VMEM((heads, rows), jnp.float32),
                pltpu.VMEM((most, heads * BLOCK), jnp.bfloat16),
                pltpu.VMEM((most, heads * BLOCK), jnp.bfloat16),
                pltpu.VMEM((LANES, rows), jnp.float32),
                pltpu.VMEM((most, LANES), jnp.float32),
                pltpu.VMEM((most, LANES), jnp.float32),
            ],
        ),
        out_shape=[shape(rows)] + [shape(c) for c in counts] * 2,
        name="attend_back",
    )(first, head_scale, query, *keys, *values, start, lse, scaled, grad)
    return results[0], results[1 : 1 + pieces], results[1 + pieces :]


def halo_rows(rows, ranks):
    hops, left = [], DOCUMENT_MAX - 1
    for _ in range(ranks - 1):
        if left <= 0:
            break
        hops.append(min(rows, -(-left // 32) * 32))
        left -= rows
    return hops


def local(
    inputs,
    cotangent,
    segment_ids,
    query_weight,
    key_weight,
    value_weight,
    output_weight,
    up_weight,
    down_weight,
    first_gain,
    first_shift,
    query_bias,
    value_bias,
    head_scale,
    output_bias,
    post_gain,
    post_shift,
    second_gain,
    second_shift,
    up_bias,
    middle_gain,
    middle_shift,
    down_bias,
):
    sequences, rows, model = inputs.shape
    hidden = up_bias.shape[0]
    head_count = head_scale.shape[0]
    ranks = lax.axis_size("seq")
    rank = lax.axis_index("seq")
    hops = halo_rows(rows, ranks)
    upward = [(i, i + 1) for i in range(ranks - 1)]
    downward = [(i + 1, i) for i in range(ranks - 1)]

    halos, moving = [], inputs
    for hop_rows in hops:
        moving = lax.ppermute(moving[:, rows - hop_rows :], "seq", upward)
        halos.append(moving)

    inward = jnp.concatenate([query_weight, key_weight, value_weight], 1)
    inward = lax.all_gather(inward, BOTH, axis=0, tiled=True)
    outward = lax.all_gather(jnp.concatenate([output_weight, up_weight], 1), BOTH, axis=0, tiled=True)
    down_full = lax.all_gather(down_weight, BOTH, axis=0, tiled=True)
    output_full, up_full = outward[:, :model], outward[:, model:]

    own_ids = lax.dynamic_slice_in_dim(segment_ids, rank * rows, rows, 1)
    start = jnp.sum((segment_ids[:, None, :] < own_ids[:, :, None]).astype(jnp.int32), -1) - rank * rows
    first = start[:, ::BLOCK]
    start = start[:, None, :]

    flat = lambda array: array.reshape(-1, array.shape[-1])
    tokens = flat(inputs).astype(jnp.float32)
    hat_one, scale_one = moments(tokens)
    normed = (hat_one * first_gain + first_shift).astype(jnp.bfloat16)
    projected = dot_nn(normed, inward)
    stacked = lambda array: array.reshape(sequences, -1, array.shape[-1])
    query = stacked((projected[:, :model] + query_bias).astype(jnp.bfloat16))
    keys = [stacked(projected[:, model : 2 * model].astype(jnp.bfloat16))]
    values = [stacked((projected[:, 2 * model :] + value_bias).astype(jnp.bfloat16))]
    normed_pieces = [normed]
    for halo in halos:
        hat, _ = moments(flat(halo).astype(jnp.float32))
        piece = (hat * first_gain + first_shift).astype(jnp.bfloat16)
        normed_pieces.append(piece)
        both = dot_nn(piece, inward[:, model:])
        keys.append(stacked(both[:, :model].astype(jnp.bfloat16)))
        values.append(stacked((both[:, model:] + value_bias).astype(jnp.bfloat16)))
    scaled, lse = attend(first, head_scale, query, keys, values, start, hops)

    scaled_low = flat(scaled)
    branch = dot_nn(scaled_low, output_full) + output_bias
    hat_post, scale_post = moments(branch)
    middle = tokens + hat_post * post_gain + post_shift
    hat_two, scale_two = moments(middle)
    second = (hat_two * second_gain + second_shift).astype(jnp.bfloat16)
    upper = dot_nn(second, up_full) + up_bias
    phi = 0.5 * (1.0 + lax.erf(upper * 0.7071067811865476))
    hat_middle, scale_middle = moments(upper * phi)
    mixed = (hat_middle * middle_gain + middle_shift).astype(jnp.bfloat16)
    layer_output = (middle + dot_nn(mixed, down_full) + down_bias).astype(jnp.bfloat16)

    grad_low = flat(cotangent)
    grad_out = grad_low.astype(jnp.float32)
    grad_mixed = dot_nt(grad_low, down_full)
    slope = phi + upper * (0.3989422804014327 * jnp.exp(-0.5 * upper * upper))
    grad_upper = (norm_back(hat_middle, scale_middle, middle_gain, grad_mixed) * slope).astype(jnp.bfloat16)
    grad_second = dot_nt(grad_upper, up_full)
    grad_middle = grad_out + norm_back(hat_two, scale_two, second_gain, grad_second)
    grad_branch = norm_back(hat_post, scale_post, post_gain, grad_middle).astype(jnp.bfloat16)
    grad_scaled = dot_nt(grad_branch, output_full)
    grad_attended = (grad_scaled * jnp.repeat(head_scale, model // head_count)).astype(jnp.bfloat16)
    head_columns = jnp.sum(grad_scaled * scaled_low.astype(jnp.float32), 0)
    head_term = jnp.sum(head_columns.reshape(head_count, -1), -1) / head_scale

    early_vectors = lax.psum(
        jnp.concatenate(
            [
                head_term,
                jnp.sum(grad_branch.astype(jnp.float32), 0),
                jnp.sum(grad_middle * hat_post, 0),
                jnp.sum(grad_middle, 0),
                jnp.sum(grad_second * hat_two, 0),
                jnp.sum(grad_second, 0),
                jnp.sum(grad_upper.astype(jnp.float32), 0),
                jnp.sum(grad_mixed * hat_middle, 0),
                jnp.sum(grad_mixed, 0),
                jnp.sum(grad_out, 0),
            ]
        ),
        BOTH,
    )
    scatter = lambda array: lax.psum_scatter(array, BOTH, scatter_dimension=0, tiled=True)
    down_part = scatter(dot_tn(mixed, grad_low).astype(jnp.bfloat16))
    outward_part = scatter(
        jnp.concatenate([dot_tn(scaled_low, grad_branch), dot_tn(second, grad_upper)], 1).astype(jnp.bfloat16)
    )

    dquery, dkeys, dvalues = attend_back(
        first, head_scale, query, keys, values, start, lse, scaled, stacked(grad_attended), hops
    )
    carried = None
    for hop in reversed(range(len(hops))):
        partial = stacked(
            dot_nt(flat(dkeys[hop + 1]), inward[:, model : 2 * model])
            + dot_nt(flat(dvalues[hop + 1]), inward[:, 2 * model :])
        )
        if carried is not None:
            partial = partial + jnp.pad(carried, ((0, 0), (partial.shape[1] - carried.shape[1], 0), (0, 0)))
        carried = lax.ppermute(partial.astype(jnp.bfloat16), "seq", downward).astype(jnp.float32)
    query_low, key_low, value_low = flat(dquery), flat(dkeys[0]), flat(dvalues[0])
    grad_normed = (
        dot_nt(query_low, inward[:, :model])
        + dot_nt(key_low, inward[:, model : 2 * model])
        + dot_nt(value_low, inward[:, 2 * model :])
    )
    if carried is not None:
        grad_normed = grad_normed + flat(jnp.pad(carried, ((0, 0), (rows - carried.shape[1], 0), (0, 0))))
    input_grad = (grad_middle + norm_back(hat_one, scale_one, first_gain, grad_normed)).astype(jnp.bfloat16)

    value_bias_term = sum(jnp.sum(d.astype(jnp.float32), (0, 1)) for d in dvalues)
    late_vectors = lax.psum(
        jnp.concatenate(
            [
                jnp.sum(grad_normed * hat_one, 0),
                jnp.sum(grad_normed, 0),
                jnp.sum(query_low.astype(jnp.float32), 0),
                value_bias_term,
            ]
        ),
        BOTH,
    )
    key_matrix = sum(dot_tn(n, flat(d)) for n, d in zip(normed_pieces, dkeys))
    value_matrix = sum(dot_tn(n, flat(d)) for n, d in zip(normed_pieces, dvalues))
    inward_part = scatter(
        jnp.concatenate([dot_tn(normed, query_low), key_matrix, value_matrix], 1).astype(jnp.bfloat16)
    )
    inward_part = inward_part.astype(jnp.float32)
    outward_part = outward_part.astype(jnp.float32)
    late = late_vectors.reshape(4, model)
    early = early_vectors[head_count:]
    five = early[: 5 * model].reshape(5, model)
    three = early[5 * model : 5 * model + 3 * hidden].reshape(3, hidden)
    return (
        stacked(layer_output),
        stacked(input_grad),
        inward_part[:, :model],
        inward_part[:, model : 2 * model],
        inward_part[:, 2 * model :],
        outward_part[:, :model],
        outward_part[:, model:],
        down_part.astype(jnp.float32),
        late[0],
        late[1],
        late[2],
        late[3],
        early_vectors[:head_count],
        five[0],
        five[1],
        five[2],
        five[3],
        five[4],
        three[0],
        three[1],
        three[2],
        early[5 * model + 3 * hidden :],
    )


def solution(mesh):
    sharded, matrix = P("dp", "seq", None), P(BOTH, None)
    in_specs = (sharded, sharded, P("dp", None)) + (matrix,) * 6 + (P(),) * 14
    out_specs = (sharded, sharded) + (matrix,) * 6 + (P(),) * 14
    return jax.shard_map(local, mesh=mesh, in_specs=in_specs, out_specs=out_specs, check_vma=False)
```

time: 2950 us -> 1060 us (0.36)
  waiting for transfers between devices: 1910 us -> 578 us
  matrix products: 750 us -> 189 us
  local copies, waits for them, and re-layouts: 137 us -> 38.7 us
  Pallas kernels: 0 us -> 75.1 us
  blocking collectives: 0 us -> 40 us
    reduce_scatter x10 -> x2, waiting for transfers between devices: 1410 us -> 305 us  [local(): lax.psum_scatter(array, BOTH, scatter_dimension=0, tiled=True)]
    dot_general x260 -> x26, matrix products: 750 us -> 189 us  [the longest x10 77.1 us: dot_nt(): lax.dot_general(a, b, (((1,), (1,)), ((), ())), preferred_element_type=jn...]
    all_gather x10 -> x3, waiting for transfers between devices: 353 us -> 42.8 us  [the longest x1 41.3 us: local(): down_full = lax.all_gather(down_weight, BOTH, axis=0, tiled=True)]
    ppermute x0 -> x4, waiting for transfers between devices: none -> 229 us  [the longest x2 155 us: local(): lax.ppermute(partial.astype(jnp.bfloat16), 'seq', downward)]
    psum x1, waiting for transfers between devices: 141 us -> 0.01 us  [local(): lax.psum(jnp.concatenate([head_term, jnp.sum(grad_branch.astype(jnp.float...]
    pallas_call x0 -> x2, Pallas kernels: none -> 75.1 us  [the longest x1 44.7 us: attend_back(): pl.pallas_call(kernel, grid_spec=pltpu.PrefetchScalarGridSpec(num_scalar_...]
    unnamed x289 -> x145, local copies, waits for them, and re-layouts: 69 us -> 16.9 us
    psum x0 -> x1, blocking collectives: none -> 40 us  [local(): lax.psum(jnp.concatenate([jnp.sum(grad_normed * hat_one, 0), jnp.sum(grad...]
  transfers between devices with their start and end apart: 21 -> 11, of which waited for: 18 -> 8; matrix products, arithmetic and copies ran while one was open for 23% -> 23% of each run, Pallas kernels for 0% -> 7%
where the time goes in v1:
time: 1060 us
  waiting for transfers between devices  578 us (55%)
  matrix products  189 us (18%)
  other arithmetic  99.6 us (9%)
  Pallas kernels  75.1 us (7%)
  blocking collectives  40 us (4%)
  local copies, waits for them, and re-layouts  38.7 us (4%)
  starting transfers between devices  19.5 us (2%)
  between operations  15.5 us (1%)
    reduce_scatter x2, waiting for transfers between devices, local(): lax.psum_scatter(array, BOTH, scatter_dimension=0, tiled=True)  305 us
    ppermute x2, waiting for transfers between devices, local(): lax.ppermute(partial.astype(jnp.bfloat16), 'seq', downward)  155 us
    dot_general x10, matrix products, dot_nt(): lax.dot_general(a, b, (((1,), (1,)), ((), ())), preferred_element_type=jn...  77.1 us
    ppermute x2, waiting for transfers between devices, local(): moving = lax.ppermute(moving[:, rows - hop_rows:], 'seq', upward)  74.9 us
    dot_general x10, matrix products, dot_tn(): lax.dot_general(a, b, (((0,), (0,)), ((), ())), preferred_element_type=jn...  58.8 us
    dot_general x6, matrix products, dot_nn(): lax.dot_general(a, b, (((1,), (0,)), ((), ())), preferred_element_type=jn...  52.8 us
    pallas_call x1, Pallas kernels, attend_back(): pl.pallas_call(kernel, grid_spec=pltpu.PrefetchScalarGridSpec(num_scalar_...  44.7 us
    all_gather x1, waiting for transfers between devices, local(): down_full = lax.all_gather(down_weight, BOTH, axis=0, tiled=True)  41.3 us
  transfers between devices with their start and end apart: 11, of which 8 were waited for; matrix products, arithmetic and copies ran while one was open for 23% of the time, Pallas kernels for 7%

profile of v1, /device:TPU:0, one launch (start us, length us, event | category | flops | bytes accessed | tf_op | source)
XLA Modules:
  0.0 1055.4 jit_solution(5681126852786947262)
XLA Ops:
  28.2 57.1 %collective-permute-done = bf16[2,512,1024]{2,1,0:T(8,128)(2,1)} collective-permute-done((bf16[2,512,1024]{2,1,0:T(8,128)(2,1)}, bf16[2,512,1024]{2,1,0:T(8,128)(2,1)}, u32[]{:S(2)}, u32[]{:S(2)}) %collective-permute-start) | collective-permute-done | bytes 2097184 | tf_op jit(solution)/shard_map/ppermute | solution.py:305
  86.6 9.5 collective-permute-start.1
  105.6 17.8 %collective-permute-done.1 = bf16[2,288,1024]{2,1,0:T(8,128)(2,1)S(1)} collective-permute-done((bf16[2,288,1024]{2,1,0:T(8,128)(2,1)S(1)}, bf16[2,288,1024]{2,1,0:T(8,128)(2,1)S(1)}, u32[]{:S(2)}, u32[]{:S(2)}) %collective-permute-start.1) | collective-permute-done | bytes 1179680 | tf_op jit(solution)/shard_map/ppermute | solution.py:305
  132.3 6.7 fusion.85
  141.3 6.3 fusion.41
  154.0 30.5 %attend.1 = (bf16[2,512,1024]{2,1,0:T(8,128)(2,1)}, f32[2,4,4,512]{3,2,1,0:T(4,128)}) custom-call(s32[2,2]{1,0:T(2,128)} %slice.136.first_ref, f32[16]{0:T(128)} %scale_ref.3, bf16[2,512,1024]{2,1,0:T(8,128)(2,1)} %bitcast.146, bf16[2,512,1024]{2,1,0:T(8,128)(2,1)} %bitcast.150, bf16[2,512,1024]{2,1,0:T(8,128)(2,1)} %bitcast.152, ...), custom_call_target="tpu_custom_call" | custom-call | tf_op jit(solution)/shard_map/attend/pallas_call | solution.py:133
  195.7 20.0 %fusion.78 = (f32[1024]{0:T(1024)S(1)}, f32[1024,4096]{1,0:T(8,128)}, f32[1024,4096]{1,0:T(8,128)}) fusion(f32[4096]{0:T(1024)S(1)} %copy-done.40, bf16[1024,5120]{1,0:T(8,128)(2,1)} %all-gather.6.cloned.1.call-done, f32[1024,1024]{1,0:T(8,128)} %copy-done.4, f32[1024]{0:T(1024)S(1)} %copy-done.59, f32[1024]{0:T(1024)S(1)} %copy-done.48, ...), kind=kOutput, calls=%fused_computation.166 | convolution fusion | flops 8620342272 | bytes 46174208 | tf_op jit(solution)/shard_map/dot_general | solution.py:19
  215.6 7.6 multiply_reduce_fusion.2
  223.2 41.3 %all-gather.8.cloned.1.call-done = bf16[4096,1024]{1,0:T(8,128)(2,1)} async-done(((bf16[128,1024]{1,0:T(8,128)(2,1)}), bf16[4096,1024]{1,0:T(8,128)(2,1)}) %all-gather.8.cloned.1.call-update) | async-done | bytes 8388624 | tf_op jit(solution)/shard_map/all_gather | solution.py:311
  264.6 20.9 %multiply_reduce_fusion = (f32[4096]{0:T(1024)S(1)}, f32[1024]{0:T(1024)S(1)}, f32[1024]{0:T(1024)S(1)}, f32[4096]{0:T(1024)S(1)}, f32[1024,4096]{1,0:T(8,128)}) fusion(f32[1024,4096]{1,0:T(8,128)} %get-tuple-element.128, f32[1024]{0:T(1024)S(1)} %add_rsqrt_fusion, f32[1024]{0:T(1024)S(1)} %broadcast_multiply_fusion.2, f32[4096]{0:T(1024)S(1)} %copy-done.41, ...), kind=kOutput, calls=%fused_computation.7 | convolution fusion | flops 8627673088 | bytes 44105728 | tf_op jit(solution)/shard_map/dot_general | solution.py:23
  285.5 26.7 %convert_reduce_fusion = (f32[4096]{0:T(1024)S(1)}, bf16[1024,4096]{1,0:T(8,128)(2,1)}, bf16[1024,4096]{1,0:T(8,128)(2,1)}) fusion(f32[1024,4096]{1,0:T(8,128)} %get-tuple-element.165, f32[4096]{0:T(1024)S(1)} %copy-done.40, f32[1024]{0:T(1024)S(1)} %get-tuple-element.169, f32[1024,4096]{1,0:T(8,128)} %get-tuple-element.128, ...), kind=kLoop, calls=%fused_computation.8 | loop fusion | flops 96464896 | bytes 67190784 | tf_op jit(solution)/shard_map/reduce_sum | solution.py:372
  312.2 15.1 %multiply_reduce_fusion.4 = (f32[1024]{0:T(1024)S(1)}, f32[1024]{0:T(1024)S(1)}, f32[1024]{0:T(1024)S(1)}, f32[1024]{0:T(1024)S(1)}, f32[1024,1024]{1,0:T(8,128)S(1)}) fusion(f32[1024,1024]{1,0:T(8,128)S(1)} %copy-done.5, f32[1024]{0:T(1024)S(1)} %add_rsqrt_fusion.1, f32[1024]{0:T(1024)S(1)} %broadcast_multiply_fusion.9, f32[1024]{0:T(1024)S(1)} %copy-done.48, ...), kind=kOutput, calls=%fused_computation.71 | convolution fusion | flops 8599367680 | bytes 25194496 | tf_op jit(solution)/shard_map/dot_general | solution.py:23
  341.8 44.7 %attend_back.1 = (bf16[2,512,1024]{2,1,0:T(8,128)(2,1)}, bf16[2,512,1024]{2,1,0:T(8,128)(2,1)}, bf16[2,512,1024]{2,1,0:T(8,128)(2,1)}, bf16[2,288,1024]{2,1,0:T(...) custom-call(s32[2,2]{1,0:T(2,128)} %slice.136.first_ref, ...), custom_call_target="tpu_custom_call" | custom-call | tf_op jit(solution)/shard_map/attend_back/pallas_call | solution.py:229
  410.6 13.4 %pad_maximum_fusion.1 = bf16[1024,3072]{0,1:T(8,128)(2,1)} fusion(bf16[1024,1024]{0,1:T(8,128)(2,1)S(1)} %fusion.13, bf16[1024,1024]{0,1:T(8,128)(2,1)S(1)} %fusion.14, bf16[1024,1024]{0,1:T(8,128)(2,1)S(1)} %bitcast_convert_fusion), kind=kLoop, calls=%fused_computation.24 | loop fusion | flops 18874368 | bytes 12582912 | tf_op jit(solution)/shard_map/concatenate | solution.py:423
  424.0 8.7 copy.77
  432.8 15.4 %convolution_convert_fusion = bf16[4096,1024]{1,0:T(8,128)(2,1)} fusion(bf16[1024,4096]{1,0:T(8,128)(2,1)} %get-tuple-element.131, bf16[1024,1024]{1,0:T(8,128)(2,1)} %bitcast.159), kind=kOutput, calls=%fused_computation.18 | convolution fusion | flops 8594128896 | bytes 18874368 | tf_op jit(solution)/shard_map/dot_general | solution.py:27
  458.2 13.7 %convolution_convert_fusion.1 = bf16[1024,4096]{1,0:T(8,128)(2,1)S(1)} fusion(bf16[1024,4096]{1,0:T(8,128)(2,1)} %get-tuple-element.123, f32[1024,1024]{1,0:T(8,128)} %copy-done.4, f32[1024]{0:T(1024)S(1)} %copy-done.60, f32[1024]{0:T(1024)S(1)} %copy-done.48, f32[1024]{0:T(1024)S(1)} %add_rsqrt_fusion.1, f32[1024]{0:T(1024)S(1)} %broadcast_multiply_fusion.9), kind=kOutput, calls=%fused_computation.19 | convolution fusion | flops 8599371776 | bytes 20987904 | tf_op jit(solution)/shard_map/dot_general | solution.py:27
  505.1 76.5 %collective-permute-done.2 = bf16[2,288,1024]{2,1,0:T(8,128)(2,1)S(1)} collective-permute-done((bf16[2,288,1024]{2,1,0:T(8,128)(2,1)S(1)}, bf16[2,288,1024]{2,1,0:T(8,128)(2,1)S(1)}, u32[]{:S(2)}, u32[]{:S(2)}) %collective-permute-start.2) | collective-permute-done | bytes 1179680 | tf_op jit(solution)/shard_map/ppermute | solution.py:397
  585.2 10.0 add_convert_fusion.3
  599.4 78.0 %collective-permute-done.3 = bf16[2,512,1024]{2,1,0:T(8,128)(2,1)} collective-permute-done((bf16[2,512,1024]{2,1,0:T(8,128)(2,1)}, bf16[2,512,1024]{2,1,0:T(8,128)(2,1)}, u32[]{:S(2)}, u32[]{:S(2)}) %collective-permute-start.3) | collective-permute-done | bytes 2097184 | tf_op jit(solution)/shard_map/ppermute | solution.py:397
  677.4 10.6 %fusion.37 = (f32[1024]{0:T(1024)S(1)}, f32[1024]{0:T(1024)S(1)}, f32[1024]{0:T(1024)S(1)}, f32[1024]{0:T(1024)S(1)}, f32[1024,1024]{1,0:T(8,128)}) fusion(bf16[2,512,1024]{2,1,0:T(8,128)(2,1)S(1)} %copy-done.2, f32[1024]{0:T(1024)S(1)} %bitcast.172, f32[1024]{0:T(1024)S(1)} %bitcast.175, f32[1024]{0:T(1024)S(1)} %copy-done.24, ...), kind=kOutput, calls=%fused_computation.68 | convolution fusion | flops 2162159616 | bytes 21000192 | tf_op jit(solution)/shard_map/dot_general | solution.py:23
  688.0 40.0 %psum.14 = f32[4096]{0:T(1024)S(1)} all-reduce(f32[4096]{0:T(1024)S(1)} %pad_maximum_fusion.4), channel_id=1, replica_groups=mesh['dp'=8,'seq'=4] {'dp','seq'}, use_global_device_ids=true, to_apply=%region_30.0 | all-reduce | flops 4096 | bytes 32768 | tf_op jit(solution)/shard_map/psum | solution.py:409
  737.8 76.8 %reduce-scatter.8.cloned.1.call-done = bf16[128,1024]{1,0:T(8,128)(2,1)} async-done(((bf16[4096,1024]{1,0:T(8,128)(2,1)}), bf16[128,1024]{1,0:T(8,128)(2,1)}) %reduce-scatter.8.cloned.1.call-update) | async-done | bytes 262160 | tf_op jit(solution)/shard_map/reduce_scatter | solution.py:380
  816.4 228.6 %reduce-scatter.6.cloned.1.call-done = bf16[32,5120]{1,0:T(8,128)(2,1)} async-done(((bf16[1024,5120]{1,0:T(8,128)(2,1)}), bf16[32,5120]{1,0:T(8,128)(2,1)}) %reduce-scatter.6.cloned.1.call-update) | async-done | bytes 327696 | tf_op jit(solution)/shard_map/reduce_scatter | solution.py:380
  (257 shorter events, 164.2 us)
Async XLA Ops:
  7.2 118.6 %all-gather.4.cloned.1.call-start = ((), (), s32[]{:S(2)}) async-start(), calls=%async_computation.3 | async-start | bytes 6488064 | tf_op jit(solution)/shard_map/all_gather | solution.py:309
  9.0 177.0 %all-gather.6.cloned.1.call-start = ((), (), s32[]{:S(2)}) async-start(), calls=%async_computation.4 | async-start | bytes 10813440 | tf_op jit(solution)/shard_map/all_gather | solution.py:310
  10.8 253.8 %all-gather.8.cloned.1.call-start = ((), (), s32[]{:S(2)}) async-start(), calls=%async_computation.5 | async-start | bytes 8650752 | tf_op jit(solution)/shard_map/all_gather | solution.py:311
  11.5 583.7 %all-reduce.3.cloned.1.call-start = ((), (), s32[]{:S(2)}) async-start(), calls=%async_computation.8 | async-start | bytes 155648 | tf_op jit(solution)/shard_map/psum | solution.py:363
  11.6 73.7 %collective-permute-start = (bf16[2,512,1024]{2,1,0:T(8,128)(2,1)}, bf16[2,512,1024]{2,1,0:T(8,128)(2,1)}, u32[]{:S(2)}, u32[]{:S(2)}) collective-permute-start(bf16[2,512,1024]{2,1,0:T(8,128)(2,1)} %param.23), channel_id=1, source_target_pairs={{0,1},{1,2},{2,3},{4,5},{5,6},{6,7},{8,9},{9,10},{10,11},{12,13},{... | collective-permute-start | bytes 6291464 | tf_op jit(solution)/shard_map/ppermute | solution.py:305
  24.8 76.2 %copy-start.25 = (f32[1,4,2,128]{3,1,2,0:T(4,128)}, f32[1,4,2,128]{3,1,2,0:T(4,128)S(1)}, u32[]{:S(2)}) copy-start(f32[1,4,2,128]{3,1,2,0:T(4,128)S(1)} %copy.80) | copy-start | bytes 12292
  24.8 76.2 %copy-start.27 = (f32[1,4,2,128]{3,1,2,0:T(4,128)}, f32[1,4,2,128]{3,1,2,0:T(4,128)S(1)}, u32[]{:S(2)}) copy-start(f32[1,4,2,128]{3,1,2,0:T(4,128)S(1)} %copy.79) | copy-start | bytes 12292
  25.6 75.5 %copy-start.23 = (f32[1024]{0:T(1024)S(1)}, f32[1024]{0:T(1024)}, u32[]{:S(2)}) copy-start(f32[1024]{0:T(1024)} %param.32) | copy-start | bytes 12292
  25.6 75.5 %copy-start.32 = (f32[1024]{0:T(1024)S(1)}, f32[1024]{0:T(1024)}, u32[]{:S(2)}) copy-start(f32[1024]{0:T(1024)} %param.33) | copy-start | bytes 12292
  86.6 36.7 %collective-permute-start.1 = (bf16[2,288,1024]{2,1,0:T(8,128)(2,1)S(1)}, bf16[2,288,1024]{2,1,0:T(8,128)(2,1)S(1)}, u32[]{:S(2)}, u32[]{:S(2)}) collective-permute-start(bf16[2,288,1024]{2,1,0:T(8,128)(2,1)S(1)} %slice.174), channel_id=1, source_target_pairs={{0,1},{1,2},{2,3},{4,5},{5,6},{6,7},{8,9},{9,10},{10,11},{12,13},{... | collective-permute-start | bytes 3538952 | tf_op jit(solution)/shard_map/ppermute | solution.py:305
  215.6 48.9 %copy-start.41 = (f32[4096]{0:T(1024)S(1)}, f32[4096]{0:T(1024)}, u32[]{:S(2)}) copy-start(f32[4096]{0:T(1024)} %param.43) | copy-start | bytes 49156
  341.7 392.1 %reduce-scatter.10.cloned.1.call-start = ((), (), s32[]{:S(2)}) async-start(), calls=%async_computation.9 | async-start | bytes 6488064
  432.7 381.9 %reduce-scatter.8.cloned.1.call-start = ((), (), s32[]{:S(2)}) async-start(), calls=%async_computation.7 | async-start | bytes 8650752 | tf_op jit(solution)/shard_map/reduce_scatter | solution.py:380
  448.1 596.9 %reduce-scatter.6.cloned.1.call-start = ((), (), s32[]{:S(2)}) async-start(), calls=%async_computation.6 | async-start | bytes 10813440 | tf_op jit(solution)/shard_map/reduce_scatter | solution.py:380
  483.1 98.5 %collective-permute-start.2 = (bf16[2,288,1024]{2,1,0:T(8,128)(2,1)S(1)}, bf16[2,288,1024]{2,1,0:T(8,128)(2,1)S(1)}, u32[]{:S(2)}, u32[]{:S(2)}) collective-permute-start(bf16[2,288,1024]{2,1,0:T(8,128)(2,1)S(1)} %bitcast.186), channel_id=1, source_target_pairs={{1,0},{2,1},{3,2},{5,4},{6,5},{7,6},{9,8},{10,9},{11,10},{13,12},{... | collective-permute-start | bytes 3538952 | tf_op jit(solution)/shard_map/ppermute | solution.py:397
  499.5 85.6 %slice-start = ((s8[8388608]{0:T(1024)(128)(4,1)}), s8[4194304]{0:T(1024)(128)(4,1)S(1)}, s32[]{:S(2)}) async-start(s8[8388608]{0:T(1024)(128)(4,1)} %bitcast.160), calls=%async_computation.10 | async-start | bytes 8388608
  499.5 85.7 %slice-start.2 = ((s8[8388608]{0:T(1024)(128)(4,1)}), s8[4194304]{0:T(1024)(128)(4,1)S(1)}, s32[]{:S(2)}) async-start(s8[8388608]{0:T(1024)(128)(4,1)} %bitcast.179), calls=%async_computation.12 | async-start | bytes 8388608
  499.5 85.7 %slice-start.1 = ((s8[8388608]{0:T(1024)(128)(4,1)}), s8[4194304]{0:T(1024)(128)(4,1)S(1)}, s32[]{:S(2)}) async-start(s8[8388608]{0:T(1024)(128)(4,1)} %bitcast.160), calls=%async_computation.11 | async-start | bytes 8388608
  499.5 85.7 %slice-start.3 = ((s8[8388608]{0:T(1024)(128)(4,1)}), s8[4194304]{0:T(1024)(128)(4,1)S(1)}, s32[]{:S(2)}) async-start(s8[8388608]{0:T(1024)(128)(4,1)} %bitcast.179), calls=%async_computation.13 | async-start | bytes 8388608
  505.1 80.1 %copy-start.6 = (f32[1024,1024]{1,0:T(8,128)S(1)}, f32[1024,1024]{1,0:T(8,128)}, u32[]{:S(2)}) copy-start(f32[1024,1024]{1,0:T(8,128)} %copy-done.4) | copy-start | bytes 12582916
  505.1 80.1 %copy-start.61 = (f32[1024]{0:T(1024)S(1)}, f32[1024]{0:T(1024)}, u32[]{:S(2)}) copy-start(f32[1024]{0:T(1024)} %param.45) | copy-start | bytes 12292
  583.5 93.9 %copy-start.26 = (f32[1,4,2,128]{3,1,2,0:T(4,128)S(1)}, f32[1,4,2,128]{3,1,2,0:T(4,128)}, u32[]{:S(2)}) copy-start(f32[1,4,2,128]{3,1,2,0:T(4,128)} %copy-done.25) | copy-start | bytes 12292
  583.5 93.9 %copy-start.28 = (f32[1,4,2,128]{3,1,2,0:T(4,128)S(1)}, f32[1,4,2,128]{3,1,2,0:T(4,128)}, u32[]{:S(2)}) copy-start(f32[1,4,2,128]{3,1,2,0:T(4,128)} %copy-done.27) | copy-start | bytes 12292
  583.5 93.9 %collective-permute-start.3 = (bf16[2,512,1024]{2,1,0:T(8,128)(2,1)}, bf16[2,512,1024]{2,1,0:T(8,128)(2,1)}, u32[]{:S(2)}, u32[]{:S(2)}) collective-permute-start(bf16[2,512,1024]{2,1,0:T(8,128)(2,1)} %add_convert_fusion.2), channel_id=1, source_target_pairs={{1,0},{2,1},{3,2},{5,4},{6,5},{7,6},{9,8},{10,9},{11,10},{13,12},{... | collective-permute-start | bytes 6291464 | tf_op jit(solution)/shard_map/ppermute | solution.py:397
  (55 other events, 501.8 us)
Sparse Core Ops, SparseCore 0:
  11.5 80.6 all-gather.3
  95.5 90.4 all-gather.5
  188.9 75.6 all-gather.7
  341.9 119.5 all-reduce.2
  466.9 137.9 reduce-scatter.9
  607.1 207.5 reduce-scatter.7
  816.9 228.0 reduce-scatter.5

commit v2 on v1

--- a/solution.py
+++ b/solution.py
@@ -266,6 +266,36 @@
     return hops
 
 
+def bits_of(axis):
+    return [(axis, bit) for bit in range(lax.axis_size(axis).bit_length() - 1)]
+
+
+def exchange(array, axis, bit):
+    return lax.ppermute(array, axis, [(i, i ^ (1 << bit)) for i in range(lax.axis_size(axis))])
+
+
+def reduce_rows(array, order):
+    left = bits_of("dp")[::-1] + bits_of("seq")[::-1]
+    columns = array.shape[-1]
+    for axis, bit in order:
+        at = left.index((axis, bit))
+        left.pop(at)
+        split = array.reshape(1 << at, 2, -1, columns)
+        mine = (lax.axis_index(axis) >> bit) & 1
+        gone = lax.dynamic_index_in_dim(split, 1 - mine, 1, keepdims=False)
+        kept = lax.dynamic_index_in_dim(split, mine, 1, keepdims=False)
+        came = exchange(gone.reshape(-1, columns), axis, bit).reshape(kept.shape)
+        total = kept.astype(jnp.float32) + came.astype(jnp.float32)
+        array = total.astype(array.dtype) if left else total
+    return array.reshape(-1, columns)
+
+
+def reduce_all(vector):
+    for axis, bit in bits_of("dp") + bits_of("seq"):
+        vector = vector + exchange(vector, axis, bit)
+    return vector
+
+
 def local(
     inputs,
     cotangent,
@@ -360,7 +390,7 @@
     head_columns = jnp.sum(grad_scaled * scaled_low.astype(jnp.float32), 0)
     head_term = jnp.sum(head_columns.reshape(head_count, -1), -1) / head_scale
 
-    early_vectors = lax.psum(
+    early_vectors = reduce_all(
         jnp.concatenate(
             [
                 head_term,
@@ -374,13 +404,15 @@
                 jnp.sum(grad_mixed, 0),
                 jnp.sum(grad_out, 0),
             ]
-        ),
-        BOTH,
-    )
-    scatter = lambda array: lax.psum_scatter(array, BOTH, scatter_dimension=0, tiled=True)
-    down_part = scatter(dot_tn(mixed, grad_low).astype(jnp.bfloat16))
-    outward_part = scatter(
-        jnp.concatenate([dot_tn(scaled_low, grad_branch), dot_tn(second, grad_upper)], 1).astype(jnp.bfloat16)
+        )
+    )
+    core, *planes = bits_of("dp")
+    one_way = [core, *reversed(planes), *bits_of("seq")]
+    other_way = [core, *planes, *bits_of("seq")]
+    down_part = reduce_rows(dot_tn(mixed, grad_low).astype(jnp.bfloat16), one_way)
+    outward_part = reduce_rows(
+        jnp.concatenate([dot_tn(scaled_low, grad_branch), dot_tn(second, grad_upper)], 1).astype(jnp.bfloat16),
+        other_way,
     )
 
     dquery, dkeys, dvalues = attend_back(
@@ -406,7 +438,7 @@
     input_grad = (grad_middle + norm_back(hat_one, scale_one, first_gain, grad_normed)).astype(jnp.bfloat16)
 
     value_bias_term = sum(jnp.sum(d.astype(jnp.float32), (0, 1)) for d in dvalues)
-    late_vectors = lax.psum(
+    late_vectors = reduce_all(
         jnp.concatenate(
             [
                 jnp.sum(grad_normed * hat_one, 0),
@@ -414,16 +446,15 @@
                 jnp.sum(query_low.astype(jnp.float32), 0),
                 value_bias_term,
             ]
-        ),
-        BOTH,
+        )
     )
     key_matrix = sum(dot_tn(n, flat(d)) for n, d in zip(normed_pieces, dkeys))
     value_matrix = sum(dot_tn(n, flat(d)) for n, d in zip(normed_pieces, dvalues))
-    inward_part = scatter(
-        jnp.concatenate([dot_tn(normed, query_low), key_matrix, value_matrix], 1).astype(jnp.bfloat16)
-    )
-    inward_part = inward_part.astype(jnp.float32)
-    outward_part = outward_part.astype(jnp.float32)
+    inward_grad = jnp.concatenate([dot_tn(normed, query_low), key_matrix, value_matrix], 1).astype(jnp.bfloat16)
+    half = inward_grad.shape[1] // 2
+    inward_part = jnp.concatenate(
+        [reduce_rows(inward_grad[:, :half], one_way), reduce_rows(inward_grad[:, half:], other_way)], 1
+    )
     late = late_vectors.reshape(4, model)
     early = early_vectors[head_count:]
     five = early[: 5 * model].reshape(5, model)
@@ -436,7 +467,7 @@
         inward_part[:, 2 * model :],
         outward_part[:, :model],
         outward_part[:, model:],
-        down_part.astype(jnp.float32),
+        down_part,
         late[0],
         late[1],
         late[2],

time: 1060 us -> 838 us (0.79)
  waiting for transfers between devices: 578 us -> 282 us
  starting transfers between devices: 19.5 us -> 94.4 us
  blocking collectives: 40 us -> 0 us
  local copies, waits for them, and re-layouts: 38.7 us -> 70.2 us
    reduce_scatter x2 -> x0, waiting for transfers between devices: 305 us -> none  [local(): lax.psum_scatter(array, BOTH, scatter_dimension=0, tiled=True)]
    ppermute x0 -> x30, waiting for transfers between devices: none -> 167 us  [exchange(): lax.ppermute(array, axis, [(i, i ^ 1 << bit) for i in range(lax.axis_size...]
    ppermute x2, waiting for transfers between devices: 155 us -> 0.01 us  [local(): lax.ppermute(partial.astype(jnp.bfloat16), 'seq', downward)]
    ppermute x0 -> x30, starting transfers between devices: none -> 75.7 us  [exchange(): lax.ppermute(array, axis, [(i, i ^ 1 << bit) for i in range(lax.axis_size...]
    psum x1 -> x0, blocking collectives: 40 us -> none  [local(): lax.psum(jnp.concatenate([jnp.sum(grad_normed * hat_one, 0), jnp.sum(grad...]
    dynamic_slice x0 -> x9, local copies, waits for them, and re-layouts: none -> 19.3 us  [the longest x3 18.9 us: reduce_rows(): kept = lax.dynamic_index_in_dim(split, mine, 1, keepdims=False)]
    convert_element_type x1 -> x16, other arithmetic: 1.79 us -> 18.3 us  [reduce_rows(): array = total.astype(array.dtype) if left else total]
  transfers between devices with their start and end apart: 11 -> 37, of which waited for: 8 -> 21; matrix products, arithmetic and copies ran while one was open for 23% -> 32% of each run, Pallas kernels for 7% -> 9%
where the time goes in v2:
time: 838 us; the launch traced here: 833 us
  waiting for transfers between devices  282 us (34%)
  matrix products  187 us (22%)
  other arithmetic  110 us (13%)
  starting transfers between devices  94.4 us (11%)
  Pallas kernels  74.2 us (9%)
  local copies, waits for them, and re-layouts  70.2 us (8%)
  between operations  15.5 us (2%)
    ppermute x30, waiting for transfers between devices, exchange(): lax.ppermute(array, axis, [(i, i ^ 1 << bit) for i in range(lax.axis_size...  167 us
    dot_general x10, matrix products, dot_nt(): lax.dot_general(a, b, (((1,), (1,)), ((), ())), preferred_element_type=jn...  82.2 us
    ppermute x30, starting transfers between devices, exchange(): lax.ppermute(array, axis, [(i, i ^ 1 << bit) for i in range(lax.axis_size...  75.7 us
    ppermute x2, waiting for transfers between devices, local(): moving = lax.ppermute(moving[:, rows - hop_rows:], 'seq', upward)  75 us
    dot_general x6, matrix products, dot_nn(): lax.dot_general(a, b, (((1,), (0,)), ((), ())), preferred_element_type=jn...  53.1 us
    dot_general x10, matrix products, dot_tn(): lax.dot_general(a, b, (((0,), (0,)), ((), ())), preferred_element_type=jn...  51.3 us
    pallas_call x1, Pallas kernels, attend_back(): pl.pallas_call(kernel, grid_spec=pltpu.PrefetchScalarGridSpec(num_scalar_...  44.2 us
    all_gather x1, waiting for transfers between devices, local(): down_full = lax.all_gather(down_weight, BOTH, axis=0, tiled=True)  38.8 us
  transfers between devices with their start and end apart: 37, of which 21 were waited for; matrix products, arithmetic and copies ran while one was open for 32% of the time, Pallas kernels for 9%

profile of v2, /device:TPU:0, one launch (start us, length us, event | category | flops | bytes accessed | tf_op | source)
XLA Modules:
  0.0 833.1 jit_solution(1363821843131955890)
XLA Ops:
  28.1 57.1 %collective-permute-done = bf16[2,512,1024]{2,1,0:T(8,128)(2,1)} collective-permute-done((bf16[2,512,1024]{2,1,0:T(8,128)(2,1)}, bf16[2,512,1024]{2,1,0:T(8,128)(2,1)}, u32[]{:S(2)}, u32[]{:S(2)}) %collective-permute-start) | collective-permute-done | bytes 2097184 | tf_op jit(solution)/shard_map/ppermute | solution.py:335
  86.6 9.5 %collective-permute-start.1 = (bf16[2,288,1024]{2,1,0:T(8,128)(2,1)S(1)}, bf16[2,288,1024]{2,1,0:T(8,128)(2,1)S(1)}, u32[]{:S(2)}, u32[]{:S(2)}) collective-permute-start(bf16[2,288,1024]{2,1,0:T(8,128)(2,1)S(1)} %slice.184), channel_id=1, source_target_pairs={{0,1},{1,2},{2,3},{4,5},{5,6},{6,7},{8,9},{9,10},{10,11},{12,13},{... | collective-permute-start | bytes 3538952 | tf_op jit(solution)/shard_map/ppermute | solution.py:335
  105.4 17.9 %collective-permute-done.1 = bf16[2,288,1024]{2,1,0:T(8,128)(2,1)S(1)} collective-permute-done((bf16[2,288,1024]{2,1,0:T(8,128)(2,1)S(1)}, bf16[2,288,1024]{2,1,0:T(8,128)(2,1)S(1)}, u32[]{:S(2)}, u32[]{:S(2)}) %collective-permute-start.1) | collective-permute-done | bytes 1179680 | tf_op jit(solution)/shard_map/ppermute | solution.py:335
  153.9 30.0 %attend.1 = (bf16[2,512,1024]{2,1,0:T(8,128)(2,1)}, f32[2,4,4,512]{3,2,1,0:T(4,128)}) custom-call(s32[2,2]{1,0:T(2,128)} %slice.144.first_ref, f32[16]{0:T(128)} %scale_ref.3, bf16[2,512,1024]{2,1,0:T(8,128)(2,1)} %bitcast.282, bf16[2,512,1024]{2,1,0:T(8,128)(2,1)} %bitcast.286, bf16[2,512,1024]{2,1,0:T(8,128)(2,1)} %bitcast.288, ...), custom_call_target="tpu_custom_call" | custom-call | tf_op jit(solution)/shard_map/attend/pallas_call | solution.py:133
  197.8 20.1 %fusion.102 = (f32[1024]{0:T(1024)S(1)}, f32[1024,4096]{1,0:T(8,128)}, f32[1024,4096]{1,0:T(8,128)}) fusion(f32[4096]{0:T(1024)S(1)} %copy-done.49, bf16[1024,5120]{1,0:T(8,128)(2,1)} %all-gather.6.cloned.1.call-done, f32[1024,1024]{1,0:T(8,128)} %copy-done.6, f32[1024]{0:T(1024)S(1)} %copy-done.69, f32[1024]{0:T(1024)S(1)} %copy-done.57, ...), kind=kOutput, calls=%fused_computation.234 | convolution fusion | flops 8620342272 | bytes 46174208 | tf_op jit(solution)/shard_map/dot_general | solution.py:19
  225.7 38.8 %all-gather.8.cloned.1.call-done = bf16[4096,1024]{1,0:T(8,128)(2,1)} async-done(((bf16[128,1024]{1,0:T(8,128)(2,1)}), bf16[4096,1024]{1,0:T(8,128)(2,1)}) %all-gather.8.cloned.1.call-update) | async-done | bytes 8388624 | tf_op jit(solution)/shard_map/all_gather | solution.py:341
  264.5 19.9 %multiply_reduce_fusion = (f32[4096]{0:T(1024)S(1)}, f32[1024]{0:T(1024)S(1)}, f32[1024]{0:T(1024)S(1)}, f32[4096]{0:T(1024)S(1)}, f32[1024,4096]{1,0:T(8,128)}) fusion(f32[1024,4096]{1,0:T(8,128)} %get-tuple-element.62, f32[1024]{0:T(1024)S(1)} %add_rsqrt_fusion, f32[1024]{0:T(1024)S(1)} %broadcast_multiply_fusion.2, f32[4096]{0:T(1024)S(1)} %copy-done.50, ...), kind=kOutput, calls=%fused_computation.7 | convolution fusion | flops 8627673088 | bytes 44105728 | tf_op jit(solution)/shard_map/dot_general | solution.py:23
  284.5 26.6 %convert_reduce_fusion = (f32[4096]{0:T(1024)S(1)}, bf16[1024,4096]{1,0:T(8,128)(2,1)}, bf16[1024,4096]{1,0:T(8,128)(2,1)}) fusion(f32[1024,4096]{1,0:T(8,128)} %get-tuple-element.109, f32[4096]{0:T(1024)S(1)} %copy-done.49, f32[1024]{0:T(1024)S(1)} %get-tuple-element.113, f32[1024,4096]{1,0:T(8,128)} %get-tuple-element.62, ...), kind=kLoop, calls=%fused_computation.8 | loop fusion | flops 96464896 | bytes 67190784 | tf_op jit(solution)/shard_map/reduce_sum | solution.py:402
  311.1 15.1 %convolution_convert_fusion.1 = bf16[1024,4096]{1,0:T(8,128)(2,1)} fusion(bf16[1024,4096]{1,0:T(8,128)(2,1)} %get-tuple-element.57, f32[1024,1024]{1,0:T(8,128)S(1)} %copy-done.7, f32[1024]{0:T(1024)S(1)} %copy-done.69, f32[1024]{0:T(1024)S(1)} %copy-done.57, f32[1024]{0:T(1024)S(1)} %add_rsqrt_fusion.1, f32[1024]{0:T(1024)S(1)} %broadcast_multiply_fusion.9), kind=kOutput, calls=%fused_computation.26 | convolution fusion | flops 8599371776 | bytes 20987904 | tf_op jit(solution)/shard_map/dot_general | solution.py:27
  326.2 15.0 %multiply_reduce_fusion.4 = (f32[1024]{0:T(1024)S(1)}, f32[1024]{0:T(1024)S(1)}, f32[1024]{0:T(1024)S(1)}, f32[1024]{0:T(1024)S(1)}, f32[1024,1024]{1,0:T(8,128)S(1)}) fusion(f32[1024,1024]{1,0:T(8,128)S(1)} %copy-done.7, f32[1024]{0:T(1024)S(1)} %add_rsqrt_fusion.1, f32[1024]{0:T(1024)S(1)} %broadcast_multiply_fusion.9, f32[1024]{0:T(1024)S(1)} %copy-done.57, ...), kind=kOutput, calls=%fused_computation.83 | convolution fusion | flops 8599367680 | bytes 25194496 | tf_op jit(solution)/shard_map/dot_general | solution.py:23
  355.7 44.2 %attend_back.1 = (bf16[2,512,1024]{2,1,0:T(8,128)(2,1)}, bf16[2,512,1024]{2,1,0:T(8,128)(2,1)}, bf16[2,512,1024]{2,1,0:T(8,128)(2,1)}, bf16[2,288,1024]{2,1,0:T(...) custom-call(s32[2,2]{1,0:T(2,128)} %slice.144.first_ref, ...), custom_call_target="tpu_custom_call" | custom-call | tf_op jit(solution)/shard_map/attend_back/pallas_call | solution.py:229
  409.0 9.6 %convolution_convert_fusion = bf16[4096,1024]{1,0:T(8,128)(2,1)S(1)} fusion(bf16[1024,4096]{1,0:T(8,128)(2,1)S(1)} %bitcast.305, bf16[1024,1024]{1,0:T(8,128)(2,1)S(1)} %bitcast.297), kind=kOutput, calls=%fused_computation.25 | convolution fusion | flops 8594128896 | bytes 18874368 | tf_op jit(solution)/shard_map/dot_general | solution.py:27
  468.8 10.1 %constant_dynamic-slice_fusion.8 = (bf16[4,1,128,1536]{2,1,0,3:T(2,128)(2,1)}, bf16[4,1,128,1536]{2,1,0,3:T(2,128)(2,1)}) fusion(bf16[4,2,128,1536]{2,1,0,3:T(2,128)(2,1)} %reshape.851, s32[]{:T(128)S(6)} %select_n.80, s32[]{:T(128)S(6)} %select_n.81), kind=kLoop, calls=%fused_computation.202 | loop fusion | bytes 6291464 | tf_op jit(solution)/shard_map/jit(dynamic_index_in_dim)/dynamic_slice | solution.py:286
  487.4 9.9 %fusion.13 = (bf16[4,1,128,5120]{3,2,1,0:T(8,128)(2,1)}, bf16[4,1,128,5120]{3,2,1,0:T(8,128)(2,1)}) fusion(s32[]{:T(128)S(6)} %select_n.80, bf16[4,2,128,4096]{3,2,1,0:T(8,128)(2,1)} %bitcast.300, bf16[4,2,128,1024]{3,2,1,0:T(8,128)(2,1)} %fusion.62, s32[]{:T(128)S(6)} %select_n.81), kind=kLoop, calls=%fused_computation.32 | loop fusion | flops 20971520 | bytes 20971528 | tf_op jit(solution)/shard_map/concatenate | solution.py:414
  509.7 10.1 %add_convert_fusion.3 = bf16[1024,1024]{1,0:T(8,128)(2,1)} fusion(f32[1024,1024]{1,0:T(8,128)S(1)} %copy-done.8, f32[1024]{0:T(1024)S(1)} %copy-done.70, bf16[1024,4096]{1,0:T(8,128)(2,1)S(1)} %bitcast.307, bf16[4096,1024]{1,0:T(8,128)(2,1)S(1)} %bitcast.351), kind=kOutput, calls=%fused_computation.97 | convolution fusion | flops 8593080320 | bytes 23072768 | tf_op jit(solution)/shard_map/dot_general | solution.py:19
  542.8 51.0 %collective-permute-start.32 = (f32[18448]{0:T(1024)S(1)}, f32[18448]{0:T(1024)S(1)}, u32[]{:S(2)}, u32[]{:S(2)}) collective-permute-start(f32[18448]{0:T(1024)S(1)} %add.526), channel_id=1, source_target_pairs={{0,1},{1,0},{2,3},{3,2},{4,5},{5,4},{6,7},{7,6},{8,9},{9,8},{10,11... | collective-permute-start | bytes 221384 | tf_op jit(solution)/shard_map/ppermute | solution.py:274
  620.8 12.5 %collective-permute-done.5 = bf16[256,1536]{1,0:T(8,128)(2,1)S(1)} collective-permute-done((bf16[256,1536]{1,0:T(8,128)(2,1)S(1)}, bf16[256,1536]{1,0:T(8,128)(2,1)S(1)}, u32[]{:S(2)}, u32[]{:S(2)}) %collective-permute-start.5) | collective-permute-done | bytes 786464 | tf_op jit(solution)/shard_map/ppermute | solution.py:274
  647.6 26.5 %collective-permute-done.7 = bf16[64,1536]{1,0:T(8,128)(2,1)S(1)} collective-permute-done((bf16[64,1536]{1,0:T(8,128)(2,1)S(1)}, bf16[64,1536]{1,0:T(8,128)(2,1)S(1)}, u32[]{:S(2)}, u32[]{:S(2)}) %collective-permute-start.7) | collective-permute-done | bytes 196640 | tf_op jit(solution)/shard_map/ppermute | solution.py:274
  691.6 8.5 %fusion.43 = (f32[1024]{0:T(1024)S(1)}, f32[1024]{0:T(1024)S(1)}, f32[1024]{0:T(1024)S(1)}, f32[1024]{0:T(1024)S(1)}, f32[1024,1024]{1,0:T(8,128)S(1)}) fusion(bf16[2,512,1024]{2,1,0:T(8,128)(2,1)S(1)} %copy-done.3, f32[1024]{0:T(1024)S(1)} %bitcast.343, f32[1024]{0:T(1024)S(1)} %bitcast.346, f32[1024]{0:T(1024)S(1)} %copy-done.33, ...), kind=kOutput, calls=%fused_computation.80 | convolution fusion | flops 2162159616 | bytes 21000192 | tf_op jit(solution)/shard_map/dot_general | solution.py:23
  700.1 31.1 %collective-permute-done.20 = bf16[1024,1024]{1,0:T(8,128)(2,1)} collective-permute-done((bf16[1024,1024]{1,0:T(8,128)(2,1)}, bf16[1024,1024]{1,0:T(8,128)(2,1)}, u32[]{:S(2)}, u32[]{:S(2)}) %collective-permute-start.20) | collective-permute-done | bytes 2097184 | tf_op jit(solution)/shard_map/ppermute | solution.py:274
  735.2 14.8 %collective-permute-done.15 = bf16[256,5120]{1,0:T(8,128)(2,1)S(1)} collective-permute-done((bf16[256,5120]{1,0:T(8,128)(2,1)S(1)}, bf16[256,5120]{1,0:T(8,128)(2,1)S(1)}, u32[]{:S(2)}, u32[]{:S(2)}) %collective-permute-start.15) | collective-permute-done | bytes 2621472 | tf_op jit(solution)/shard_map/ppermute | solution.py:274
  754.2 16.4 %collective-permute-done.25 = f32[4096]{0:T(1024)S(1)} collective-permute-done((f32[4096]{0:T(1024)S(1)}, f32[4096]{0:T(1024)S(1)}, u32[]{:S(2)}, u32[]{:S(2)}) %collective-permute-start.25) | collective-permute-done | bytes 16416 | tf_op jit(solution)/shard_map/ppermute | solution.py:274
  789.7 12.0 %collective-permute-done.22 = bf16[256,1024]{1,0:T(8,128)(2,1)S(1)} collective-permute-done((bf16[256,1024]{1,0:T(8,128)(2,1)S(1)}, bf16[256,1024]{1,0:T(8,128)(2,1)S(1)}, u32[]{:S(2)}, u32[]{:S(2)}) %collective-permute-start.22) | collective-permute-done | bytes 524320 | tf_op jit(solution)/shard_map/ppermute | solution.py:274
  802.0 11.1 %collective-permute-done.17 = bf16[64,5120]{1,0:T(8,128)(2,1)S(1)} collective-permute-done((bf16[64,5120]{1,0:T(8,128)(2,1)S(1)}, bf16[64,5120]{1,0:T(8,128)(2,1)S(1)}, u32[]{:S(2)}, u32[]{:S(2)}) %collective-permute-start.17) | collective-permute-done | bytes 655392 | tf_op jit(solution)/shard_map/ppermute | solution.py:274
  (374 shorter events, 299.5 us)
Async XLA Ops:
  7.2 118.5 %all-gather.4.cloned.1.call-start = ((), (), s32[]{:S(2)}) async-start(), calls=%async_computation | async-start | bytes 6488064 | tf_op jit(solution)/shard_map/all_gather | solution.py:339
  9.0 179.0 %all-gather.6.cloned.1.call-start = ((), (), s32[]{:S(2)}) async-start(), calls=%async_computation.1 | async-start | bytes 10813440 | tf_op jit(solution)/shard_map/all_gather | solution.py:340
  10.8 253.7 %all-gather.8.cloned.1.call-start = ((), (), s32[]{:S(2)}) async-start(), calls=%async_computation.2 | async-start | bytes 8650752 | tf_op jit(solution)/shard_map/all_gather | solution.py:341
  11.5 73.7 %collective-permute-start = (bf16[2,512,1024]{2,1,0:T(8,128)(2,1)}, bf16[2,512,1024]{2,1,0:T(8,128)(2,1)}, u32[]{:S(2)}, u32[]{:S(2)}) collective-permute-start(bf16[2,512,1024]{2,1,0:T(8,128)(2,1)} %param.23), channel_id=1, source_target_pairs={{0,1},{1,2},{2,3},{4,5},{5,6},{6,7},{8,9},{9,10},{10,11},{12,13},{... | collective-permute-start | bytes 6291464 | tf_op jit(solution)/shard_map/ppermute | solution.py:335
  86.6 36.7 %collective-permute-start.1 = (bf16[2,288,1024]{2,1,0:T(8,128)(2,1)S(1)}, bf16[2,288,1024]{2,1,0:T(8,128)(2,1)S(1)}, u32[]{:S(2)}, u32[]{:S(2)}) collective-permute-start(bf16[2,288,1024]{2,1,0:T(8,128)(2,1)S(1)} %slice.184), channel_id=1, source_target_pairs={{0,1},{1,2},{2,3},{4,5},{5,6},{6,7},{8,9},{9,10},{10,11},{12,13},{... | collective-permute-start | bytes 3538952 | tf_op jit(solution)/shard_map/ppermute | solution.py:335
  355.4 178.3 %collective-permute-start.29 = (f32[18448]{0:T(1024)S(1)}, f32[18448]{0:T(1024)S(1)}, u32[]{:S(2)}, u32[]{:S(2)}) collective-permute-start(f32[18448]{0:T(1024)S(1)} %concatenate.38), channel_id=1, source_target_pairs={{0,4},{4,0},{8,12},{12,8},{16,20},{20,16},{24,28},{28,24},{1,5},{5... | collective-permute-start | bytes 221384 | tf_op jit(solution)/shard_map/ppermute | solution.py:274
  407.6 209.7 %collective-permute-start.2 = (bf16[2,288,1024]{2,1,0:T(8,128)(2,1)}, bf16[2,288,1024]{2,1,0:T(8,128)(2,1)S(1)}, u32[]{:S(2)}, u32[]{:S(2)}) collective-permute-start(bf16[2,288,1024]{2,1,0:T(8,128)(2,1)} %bitcast.22), channel_id=1, source_target_pairs={{1,0},{2,1},{3,2},{5,4},{6,5},{7,6},{9,8},{10,9},{11,10},{13,12},{... | collective-permute-start | bytes 3538952 | tf_op jit(solution)/shard_map/ppermute | solution.py:429
  423.6 254.9 %collective-permute-start.19 = (bf16[2048,1024]{1,0:T(8,128)(2,1)}, bf16[2048,1024]{1,0:T(8,128)(2,1)}, u32[]{:S(2)}, u32[]{:S(2)}) collective-permute-start(bf16[2048,1024]{1,0:T(8,128)(2,1)} %bitcast.82), channel_id=1, source_target_pairs={{0,4},{4,0},{8,12},{12,8},{16,20},{20,16},{24,28},{28,24},{1,5},{5... | collective-permute-start | bytes 12582920 | tf_op jit(solution)/shard_map/ppermute | solution.py:274
  462.4 148.6 %collective-permute-start.4 = (bf16[512,1536]{1,0:T(8,128)(2,1)}, bf16[512,1536]{1,0:T(8,128)(2,1)}, u32[]{:S(2)}, u32[]{:S(2)}) collective-permute-start(bf16[512,1536]{1,0:T(8,128)(2,1)} %bitcast.31), channel_id=1, source_target_pairs={{0,4},{4,0},{8,12},{12,8},{16,20},{20,16},{24,28},{28,24},{1,5},{5... | collective-permute-start | bytes 4718600 | tf_op jit(solution)/shard_map/ppermute | solution.py:274
  487.1 127.2 %collective-permute-start.9 = (bf16[512,1536]{1,0:T(8,128)(2,1)}, bf16[512,1536]{1,0:T(8,128)(2,1)}, u32[]{:S(2)}, u32[]{:S(2)}) collective-permute-start(bf16[512,1536]{1,0:T(8,128)(2,1)} %bitcast.326), channel_id=1, source_target_pairs={{0,4},{4,0},{8,12},{12,8},{16,20},{20,16},{24,28},{28,24},{1,5},{5... | collective-permute-start | bytes 4718600 | tf_op jit(solution)/shard_map/ppermute | solution.py:274
  542.8 53.4 %collective-permute-start.32 = (f32[18448]{0:T(1024)S(1)}, f32[18448]{0:T(1024)S(1)}, u32[]{:S(2)}, u32[]{:S(2)}) collective-permute-start(f32[18448]{0:T(1024)S(1)} %add.526), channel_id=1, source_target_pairs={{0,1},{1,0},{2,3},{3,2},{4,5},{5,4},{6,7},{7,6},{8,9},{9,8},{10,11... | collective-permute-start | bytes 221384 | tf_op jit(solution)/shard_map/ppermute | solution.py:274
  609.1 76.5 %collective-permute-start.14 = (bf16[512,5120]{1,0:T(8,128)(2,1)}, bf16[512,5120]{1,0:T(8,128)(2,1)}, u32[]{:S(2)}, u32[]{:S(2)}) collective-permute-start(bf16[512,5120]{1,0:T(8,128)(2,1)} %bitcast.312), channel_id=1, source_target_pairs={{0,4},{4,0},{8,12},{12,8},{16,20},{20,16},{24,28},{28,24},{1,5},{5... | collective-permute-start | bytes 15728648 | tf_op jit(solution)/shard_map/ppermute | solution.py:274
  613.3 20.0 %collective-permute-start.5 = (bf16[256,1536]{1,0:T(8,128)(2,1)S(1)}, bf16[256,1536]{1,0:T(8,128)(2,1)S(1)}, u32[]{:S(2)}, u32[]{:S(2)}) collective-permute-start(bf16[256,1536]{1,0:T(8,128)(2,1)S(1)} %dynamic-slice_bitcast_fusion.3), channel_id=1, source_target_pairs={{0,16},{4,20},{8,24},{12,28},{16,0},{20,4},{24,8},{28,12},{1,17},{... | collective-permute-start | bytes 2359304 | tf_op jit(solution)/shard_map/ppermute | solution.py:274
  616.4 20.3 %collective-permute-start.10 = (bf16[256,1536]{1,0:T(8,128)(2,1)S(1)}, bf16[256,1536]{1,0:T(8,128)(2,1)S(1)}, u32[]{:S(2)}, u32[]{:S(2)}) collective-permute-start(bf16[256,1536]{1,0:T(8,128)(2,1)S(1)} %bitcast.333), channel_id=1, source_target_pairs={{0,8},{4,12},{8,0},{12,4},{16,24},{20,28},{24,16},{28,20},{1,9},{5... | collective-permute-start | bytes 2359304 | tf_op jit(solution)/shard_map/ppermute | solution.py:274
  619.3 72.2 %collective-permute-start.3 = (bf16[2,512,1024]{2,1,0:T(8,128)(2,1)}, bf16[2,512,1024]{2,1,0:T(8,128)(2,1)}, u32[]{:S(2)}, u32[]{:S(2)}) collective-permute-start(bf16[2,512,1024]{2,1,0:T(8,128)(2,1)} %add_convert_fusion.2), channel_id=1, source_target_pairs={{1,0},{2,1},{3,2},{5,4},{6,5},{7,6},{9,8},{10,9},{11,10},{13,12},{... | collective-permute-start | bytes 6291464 | tf_op jit(solution)/shard_map/ppermute | solution.py:429
  644.9 29.2 %collective-permute-start.7 = (bf16[64,1536]{1,0:T(8,128)(2,1)S(1)}, bf16[64,1536]{1,0:T(8,128)(2,1)S(1)}, u32[]{:S(2)}, u32[]{:S(2)}) collective-permute-start(bf16[64,1536]{1,0:T(8,128)(2,1)S(1)} %bitcast.338), channel_id=1, source_target_pairs={{0,1},{1,0},{2,3},{3,2},{4,5},{5,4},{6,7},{7,6},{8,9},{9,8},{10,11... | collective-permute-start | bytes 589832 | tf_op jit(solution)/shard_map/ppermute | solution.py:274
  647.5 30.9 %collective-permute-start.12 = (bf16[64,1536]{1,0:T(8,128)(2,1)S(1)}, bf16[64,1536]{1,0:T(8,128)(2,1)S(1)}, u32[]{:S(2)}, u32[]{:S(2)}) collective-permute-start(bf16[64,1536]{1,0:T(8,128)(2,1)S(1)} %bitcast.339), channel_id=1, source_target_pairs={{0,1},{1,0},{2,3},{3,2},{4,5},{5,4},{6,7},{7,6},{8,9},{9,8},{10,11... | collective-permute-start | bytes 589832 | tf_op jit(solution)/shard_map/ppermute | solution.py:274
  684.6 46.6 %collective-permute-start.20 = (bf16[1024,1024]{1,0:T(8,128)(2,1)}, bf16[1024,1024]{1,0:T(8,128)(2,1)}, u32[]{:S(2)}, u32[]{:S(2)}) collective-permute-start(bf16[1024,1024]{1,0:T(8,128)(2,1)} %dynamic-slice_bitcast_fusion), channel_id=1, source_target_pairs={{0,16},{4,20},{8,24},{12,28},{16,0},{20,4},{24,8},{28,12},{1,17},{... | collective-permute-start | bytes 6291464 | tf_op jit(solution)/shard_map/ppermute | solution.py:274
  690.2 59.8 %collective-permute-start.15 = (bf16[256,5120]{1,0:T(8,128)(2,1)S(1)}, bf16[256,5120]{1,0:T(8,128)(2,1)S(1)}, u32[]{:S(2)}, u32[]{:S(2)}) collective-permute-start(bf16[256,5120]{1,0:T(8,128)(2,1)S(1)} %bitcast.319), channel_id=1, source_target_pairs={{0,8},{4,12},{8,0},{12,4},{16,24},{20,28},{24,16},{28,20},{1,9},{5... | collective-permute-start | bytes 7864328 | tf_op jit(solution)/shard_map/ppermute | solution.py:274
  700.0 52.2 %collective-permute-start.24 = (f32[4096]{0:T(1024)S(1)}, f32[4096]{0:T(1024)S(1)}, u32[]{:S(2)}, u32[]{:S(2)}) collective-permute-start(f32[4096]{0:T(1024)S(1)} %pad_maximum_fusion.5), channel_id=1, source_target_pairs={{0,4},{4,0},{8,12},{12,8},{16,20},{20,16},{24,28},{28,24},{1,5},{5... | collective-permute-start | bytes 49160 | tf_op jit(solution)/shard_map/ppermute | solution.py:274
  733.9 50.3 %collective-permute-start.21 = (bf16[512,1024]{1,0:T(8,128)(2,1)S(1)}, bf16[512,1024]{1,0:T(8,128)(2,1)S(1)}, u32[]{:S(2)}, u32[]{:S(2)}) collective-permute-start(bf16[512,1024]{1,0:T(8,128)(2,1)S(1)} %dynamic-slice_bitcast_fusion.2), channel_id=1, source_target_pairs={{0,8},{4,12},{8,0},{12,4},{16,24},{20,28},{24,16},{28,20},{1,9},{5... | collective-permute-start | bytes 3145736 | tf_op jit(solution)/shard_map/ppermute | solution.py:274
  751.1 33.6 %collective-permute-start.16 = (bf16[128,5120]{1,0:T(8,128)(2,1)S(1)}, bf16[128,5120]{1,0:T(8,128)(2,1)S(1)}, u32[]{:S(2)}, u32[]{:S(2)}) collective-permute-start(bf16[128,5120]{1,0:T(8,128)(2,1)S(1)} %dynamic-slice_bitcast_fusion.1), channel_id=1, source_target_pairs={{0,16},{4,20},{8,24},{12,28},{16,0},{20,4},{24,8},{28,12},{1,17},{... | collective-permute-start | bytes 3932168 | tf_op jit(solution)/shard_map/ppermute | solution.py:274
  785.1 28.0 %collective-permute-start.17 = (bf16[64,5120]{1,0:T(8,128)(2,1)S(1)}, bf16[64,5120]{1,0:T(8,128)(2,1)S(1)}, u32[]{:S(2)}, u32[]{:S(2)}) collective-permute-start(bf16[64,5120]{1,0:T(8,128)(2,1)S(1)} %bitcast.335), channel_id=1, source_target_pairs={{0,1},{1,0},{2,3},{3,2},{4,5},{5,4},{6,7},{7,6},{8,9},{9,8},{10,11... | collective-permute-start | bytes 1966088 | tf_op jit(solution)/shard_map/ppermute | solution.py:274
  802.0 19.2 %collective-permute-start.23 = (bf16[128,1024]{1,0:T(8,128)(2,1)S(1)}, bf16[128,1024]{1,0:T(8,128)(2,1)S(1)}, u32[]{:S(2)}, u32[]{:S(2)}) collective-permute-start(bf16[128,1024]{1,0:T(8,128)(2,1)S(1)} %dynamic-slice_bitcast_fusion.7), channel_id=1, source_target_pairs={{0,2},{1,3},{2,0},{3,1},{4,6},{5,7},{6,4},{7,5},{8,10},{9,11},{10,... | collective-permute-start | bytes 786440 | tf_op jit(solution)/shard_map/ppermute | solution.py:274
  (92 other events, 1081.1 us)
Sparse Core Ops, SparseCore 0:
  11.5 80.5 all-gather.3
  95.5 90.2 all-gather.5
  188.7 75.7 all-gather.7

commit v3 on v1

--- a/solution.py
+++ b/solution.py
@@ -266,6 +266,71 @@
     return hops
 
 
+def bits_of(axis):
+    return [(axis, bit) for bit in range(lax.axis_size(axis).bit_length() - 1)]
+
+
+def exchange(array, axis, bit):
+    return lax.ppermute(array, axis, [(i, i ^ (1 << bit)) for i in range(lax.axis_size(axis))])
+
+
+def together(*values):
+    return lax.optimization_barrier(values)
+
+
+def pick_columns(array, place, ours):
+    axis, bit = place
+    order = bits_of("dp")[::-1] + bits_of("seq")[::-1]
+    mine = (lax.axis_index(axis) >> bit) & 1
+    split = array.reshape(array.shape[0], 1 << order.index(place), 2, -1)
+    picked = lax.dynamic_index_in_dim(split, mine if ours else 1 - mine, 2, keepdims=False)
+    return picked.reshape(array.shape[0], -1)
+
+
+own_columns = functools.partial(pick_columns, ours=True)
+other_columns = functools.partial(pick_columns, ours=False)
+
+
+class RowSum:
+    def __init__(self, order):
+        self.order = list(order)
+        self.left = bits_of("dp")[::-1] + bits_of("seq")[::-1]
+        self.came = self.kept = self.total = None
+
+    def begin(self, sent):
+        axis, bit = self.order.pop(0)
+        self.left.remove((axis, bit))
+        self.came = exchange(sent, axis, bit)
+
+    def end_step(self, *chain):
+        came, *chain = together(self.came, *chain)
+        self.total = self.kept.astype(jnp.float32) + came.astype(jnp.float32)
+        return chain
+
+    def begin_step(self, *chain):
+        axis, bit = self.order.pop(0)
+        at = self.left.index((axis, bit))
+        self.left.pop(at)
+        total = self.total.astype(jnp.bfloat16)
+        columns = total.shape[-1]
+        split = total.reshape(1 << at, 2, -1, columns)
+        mine = (lax.axis_index(axis) >> bit) & 1
+        gone = lax.dynamic_index_in_dim(split, 1 - mine, 1, keepdims=False).reshape(-1, columns)
+        kept = lax.dynamic_index_in_dim(split, mine, 1, keepdims=False).reshape(-1, columns)
+        gone, self.kept, *chain = together(gone, kept, *chain)
+        self.came = exchange(gone, axis, bit)
+        return chain
+
+    def advance(self, *chain):
+        return self.begin_step(*self.end_step(*chain))
+
+
+def reduce_all(vector):
+    for axis, bit in bits_of("dp") + bits_of("seq"):
+        vector = vector + exchange(vector, axis, bit)
+    return vector
+
+
 def local(
     inputs,
     cotangent,
@@ -300,10 +365,19 @@
     upward = [(i, i + 1) for i in range(ranks - 1)]
     downward = [(i + 1, i) for i in range(ranks - 1)]
 
-    halos, moving = [], inputs
-    for hop_rows in hops:
-        moving = lax.ppermute(moving[:, rows - hop_rows :], "seq", upward)
-        halos.append(moving)
+    halos = []
+    if hops:
+        onward = hops[1] if len(hops) > 1 else hops[0]
+        shift = lambda array: lax.ppermute(array, "seq", upward)
+        moving = shift(inputs[:, rows - onward :])
+        nearest = moving
+        if onward < hops[0]:
+            rest, moving = together(inputs[:, rows - hops[0] : rows - onward], moving)
+            nearest = jnp.concatenate([shift(rest), moving], 1)
+        halos.append(nearest)
+        for hop_rows in hops[1:]:
+            moving = shift(moving[:, moving.shape[1] - hop_rows :])
+            halos.append(moving)
 
     inward = jnp.concatenate([query_weight, key_weight, value_weight], 1)
     inward = lax.all_gather(inward, BOTH, axis=0, tiled=True)
@@ -325,11 +399,12 @@
     query = stacked((projected[:, :model] + query_bias).astype(jnp.bfloat16))
     keys = [stacked(projected[:, model : 2 * model].astype(jnp.bfloat16))]
     values = [stacked((projected[:, 2 * model :] + value_bias).astype(jnp.bfloat16))]
-    normed_pieces = [normed]
+    normed_pieces, hats = [normed], [hat_one]
     for halo in halos:
         hat, _ = moments(flat(halo).astype(jnp.float32))
         piece = (hat * first_gain + first_shift).astype(jnp.bfloat16)
         normed_pieces.append(piece)
+        hats.append(hat)
         both = dot_nn(piece, inward[:, model:])
         keys.append(stacked(both[:, :model].astype(jnp.bfloat16)))
         values.append(stacked((both[:, model:] + value_bias).astype(jnp.bfloat16)))
@@ -345,22 +420,90 @@
     phi = 0.5 * (1.0 + lax.erf(upper * 0.7071067811865476))
     hat_middle, scale_middle = moments(upper * phi)
     mixed = (hat_middle * middle_gain + middle_shift).astype(jnp.bfloat16)
-    layer_output = (middle + dot_nn(mixed, down_full) + down_bias).astype(jnp.bfloat16)
-
     grad_low = flat(cotangent)
     grad_out = grad_low.astype(jnp.float32)
-    grad_mixed = dot_nt(grad_low, down_full)
+    core, *planes = bits_of("dp")
+    one_way = [core, *reversed(planes), *bits_of("seq")]
+    other_way = [core, *planes, *bits_of("seq")]
+
+    down_sum, up_sum = RowSum(one_way), RowSum(other_way)
+    sent = dot_tn(other_columns(mixed, core), grad_low).astype(jnp.bfloat16)
+    down_sum.begin(sent)
+    down_sum.kept = dot_tn(own_columns(mixed, core), grad_low)
+    (late_low,) = down_sum.advance(grad_low)
+
+    layer_output = (middle + dot_nn(mixed, down_full) + down_bias).astype(jnp.bfloat16)
+    grad_mixed = dot_nt(late_low, down_full)
     slope = phi + upper * (0.3989422804014327 * jnp.exp(-0.5 * upper * upper))
     grad_upper = (norm_back(hat_middle, scale_middle, middle_gain, grad_mixed) * slope).astype(jnp.bfloat16)
+    (grad_upper,) = down_sum.advance(grad_upper)
+    sent = dot_tn(other_columns(second, core), grad_upper).astype(jnp.bfloat16)
+    sent, grad_upper = together(sent, grad_upper)
+    up_sum.begin(sent)
     grad_second = dot_nt(grad_upper, up_full)
     grad_middle = grad_out + norm_back(hat_two, scale_two, second_gain, grad_second)
     grad_branch = norm_back(hat_post, scale_post, post_gain, grad_middle).astype(jnp.bfloat16)
+    up_sum.kept = dot_tn(own_columns(second, core), grad_upper)
+    (grad_branch,) = up_sum.advance(grad_branch)
     grad_scaled = dot_nt(grad_branch, output_full)
     grad_attended = (grad_scaled * jnp.repeat(head_scale, model // head_count)).astype(jnp.bfloat16)
+    (grad_attended,) = down_sum.advance(grad_attended)
     head_columns = jnp.sum(grad_scaled * scaled_low.astype(jnp.float32), 0)
     head_term = jnp.sum(head_columns.reshape(head_count, -1), -1) / head_scale
 
-    early_vectors = lax.psum(
+    dquery, dkeys, dvalues = attend_back(
+        first, head_scale, query, keys, values, start, lse, scaled, stacked(grad_attended), hops
+    )
+    partials = [
+        dot_nt(flat(dkeys[hop + 1]), inward[:, model : 2 * model])
+        + dot_nt(flat(dvalues[hop + 1]), inward[:, 2 * model :])
+        for hop in range(len(hops))
+    ]
+    lower = lambda array: lax.ppermute(array, "seq", downward)
+    query_low, key_low, value_low = flat(dquery), flat(dkeys[0]), flat(dvalues[0])
+    carried = None
+    if hops:
+        going = stacked(partials[-1]).astype(jnp.bfloat16)
+        going, query_low = together(going, query_low)
+        carried = lower(going)
+    query_low, key_low, value_low = down_sum.advance(query_low, key_low, value_low)
+    query_low, key_low, value_low = up_sum.advance(query_low, key_low, value_low)
+
+    inward_sums = RowSum(one_way), RowSum(other_way)
+    halo_normed = normed_pieces[1:]
+    halo_pairs = [(flat(k), flat(v)) for k, v in zip(dkeys[1:], dvalues[1:])]
+
+    def four(pick):
+        mine = pick(normed, core)
+        key_part, value_part = dot_tn(mine, key_low), dot_tn(mine, value_low)
+        for piece, (dkey, dvalue) in zip(halo_normed, halo_pairs):
+            picked = pick(piece, core)
+            key_part, value_part = key_part + dot_tn(picked, dkey), value_part + dot_tn(picked, dvalue)
+        return dot_tn(mine, query_low), key_part, value_part, dot_tn(pick(scaled_low, core), grad_branch)
+
+    sent = jnp.concatenate([part.astype(jnp.bfloat16) for part in four(other_columns)], 1)
+    came = exchange(sent, *core)
+    own = (
+        dot_nt(query_low, inward[:, :model])
+        + dot_nt(key_low, inward[:, model : 2 * model])
+        + dot_nt(value_low, inward[:, 2 * model :])
+    )
+    for hop in reversed(range(len(hops) - 1)):
+        carried, own = together(carried, own)
+        partial = stacked(partials[hop])
+        going = partial + jnp.pad(
+            carried.astype(jnp.float32), ((0, 0), (partial.shape[1] - carried.shape[1], 0), (0, 0))
+        )
+        going, own = together(going.astype(jnp.bfloat16), own)
+        carried = lower(going)
+    mine = four(own_columns)
+    for index, row_sum in enumerate(inward_sums):
+        row_sum.order.pop(0)
+        row_sum.left.remove(core)
+        row_sum.came = came[:, 2 * index * model : 2 * (index + 1) * model]
+        row_sum.kept = jnp.concatenate(mine[2 * index : 2 * (index + 1)], 1)
+
+    vectors = reduce_all(
         jnp.concatenate(
             [
                 head_term,
@@ -369,88 +512,54 @@
                 jnp.sum(grad_middle, 0),
                 jnp.sum(grad_second * hat_two, 0),
                 jnp.sum(grad_second, 0),
+                jnp.sum(grad_out, 0),
+                jnp.sum(own * hat_one, 0) + sum(jnp.sum(p * h, 0) for p, h in zip(partials, hats[1:])),
+                jnp.sum(own, 0) + sum(jnp.sum(p, 0) for p in partials),
+                jnp.sum(query_low.astype(jnp.float32), 0),
+                sum(jnp.sum(d.astype(jnp.float32), (0, 1)) for d in dvalues),
                 jnp.sum(grad_upper.astype(jnp.float32), 0),
                 jnp.sum(grad_mixed * hat_middle, 0),
                 jnp.sum(grad_mixed, 0),
-                jnp.sum(grad_out, 0),
             ]
-        ),
-        BOTH,
+        )
     )
-    scatter = lambda array: lax.psum_scatter(array, BOTH, scatter_dimension=0, tiled=True)
-    down_part = scatter(dot_tn(mixed, grad_low).astype(jnp.bfloat16))
-    outward_part = scatter(
-        jnp.concatenate([dot_tn(scaled_low, grad_branch), dot_tn(second, grad_upper)], 1).astype(jnp.bfloat16)
-    )
-
-    dquery, dkeys, dvalues = attend_back(
-        first, head_scale, query, keys, values, start, lse, scaled, stacked(grad_attended), hops
-    )
-    carried = None
-    for hop in reversed(range(len(hops))):
-        partial = stacked(
-            dot_nt(flat(dkeys[hop + 1]), inward[:, model : 2 * model])
-            + dot_nt(flat(dvalues[hop + 1]), inward[:, 2 * model :])
-        )
-        if carried is not None:
-            partial = partial + jnp.pad(carried, ((0, 0), (partial.shape[1] - carried.shape[1], 0), (0, 0)))
-        carried = lax.ppermute(partial.astype(jnp.bfloat16), "seq", downward).astype(jnp.float32)
-    query_low, key_low, value_low = flat(dquery), flat(dkeys[0]), flat(dvalues[0])
-    grad_normed = (
-        dot_nt(query_low, inward[:, :model])
-        + dot_nt(key_low, inward[:, model : 2 * model])
-        + dot_nt(value_low, inward[:, 2 * model :])
-    )
-    if carried is not None:
-        grad_normed = grad_normed + flat(jnp.pad(carried, ((0, 0), (rows - carried.shape[1], 0), (0, 0))))
+    for row_sum in (down_sum, up_sum, *inward_sums):
+        while row_sum.order:
+            row_sum.advance()
+        row_sum.end_step()
+
+    grad_normed = own
+    if hops:
+        grad_normed = own + flat(jnp.pad(carried.astype(jnp.float32), ((0, 0), (rows - carried.shape[1], 0), (0, 0))))
     input_grad = (grad_middle + norm_back(hat_one, scale_one, first_gain, grad_normed)).astype(jnp.bfloat16)
 
-    value_bias_term = sum(jnp.sum(d.astype(jnp.float32), (0, 1)) for d in dvalues)
-    late_vectors = lax.psum(
-        jnp.concatenate(
-            [
-                jnp.sum(grad_normed * hat_one, 0),
-                jnp.sum(grad_normed, 0),
-                jnp.sum(query_low.astype(jnp.float32), 0),
-                value_bias_term,
-            ]
-        ),
-        BOTH,
-    )
-    key_matrix = sum(dot_tn(n, flat(d)) for n, d in zip(normed_pieces, dkeys))
-    value_matrix = sum(dot_tn(n, flat(d)) for n, d in zip(normed_pieces, dvalues))
-    inward_part = scatter(
-        jnp.concatenate([dot_tn(normed, query_low), key_matrix, value_matrix], 1).astype(jnp.bfloat16)
-    )
-    inward_part = inward_part.astype(jnp.float32)
-    outward_part = outward_part.astype(jnp.float32)
-    late = late_vectors.reshape(4, model)
-    early = early_vectors[head_count:]
-    five = early[: 5 * model].reshape(5, model)
-    three = early[5 * model : 5 * model + 3 * hidden].reshape(3, hidden)
+    query_key, value_output = (row_sum.total for row_sum in inward_sums)
+    rest = vectors[head_count:]
+    narrow = rest[: 10 * model].reshape(10, model)
+    broad = rest[10 * model :].reshape(3, hidden)
     return (
         stacked(layer_output),
         stacked(input_grad),
-        inward_part[:, :model],
-        inward_part[:, model : 2 * model],
-        inward_part[:, 2 * model :],
-        outward_part[:, :model],
-        outward_part[:, model:],
-        down_part.astype(jnp.float32),
-        late[0],
-        late[1],
-        late[2],
-        late[3],
-        early_vectors[:head_count],
-        five[0],
-        five[1],
-        five[2],
-        five[3],
-        five[4],
-        three[0],
-        three[1],
-        three[2],
-        early[5 * model + 3 * hidden :],
+        query_key[:, :model],
+        query_key[:, model:],
+        value_output[:, :model],
+        value_output[:, model:],
+        up_sum.total,
+        down_sum.total,
+        narrow[6],
+        narrow[7],
+        narrow[8],
+        narrow[9],
+        vectors[:head_count],
+        narrow[0],
+        narrow[1],
+        narrow[2],
+        narrow[3],
+        narrow[4],
+        broad[0],
+        broad[1],
+        broad[2],
+        narrow[5],
     )
 
 

time: 1060 us -> 934 us (0.88)
  waiting for transfers between devices: 578 us -> 149 us
  local copies, waits for them, and re-layouts: 38.7 us -> 203 us
  starting transfers between devices: 19.5 us -> 156 us
  blocking collectives: 40 us -> 0 us
  other arithmetic: 99.6 us -> 139 us
    reduce_scatter x2 -> x0, waiting for transfers between devices: 305 us -> none  [local(): lax.psum_scatter(array, BOTH, scatter_dimension=0, tiled=True)]
    ppermute x4 -> x29, starting transfers between devices: 19.2 us -> 156 us  [the longest x24 139 us: exchange(): lax.ppermute(array, axis, [(i, i ^ 1 << bit) for i in range(lax.axis_size...]
    ppermute x4 -> x29, waiting for transfers between devices: 229 us -> 149 us  [the longest x24 90.9 us: exchange(): lax.ppermute(array, axis, [(i, i ^ 1 << bit) for i in range(lax.axis_size...]
    dynamic_slice x0 -> x14, local copies, waits for them, and re-layouts: none -> 70.5 us  [the longest x8 67.3 us: pick_columns(): lax.dynamic_index_in_dim(split, mine if ours else 1 - mine, 2, keepdims=F...]
    unnamed x145 -> x242, local copies, waits for them, and re-layouts: 16.9 us -> 70.9 us
    convert_element_type x2 -> x22, other arithmetic: 3.7 us -> 56 us  [the longest x1 17.4 us: local(): (norm_back(hat_middle, scale_middle, middle_gain, grad_mixed) * slope).as...]
    all_gather x1, waiting for transfers between devices: 41.3 us -> 0.01 us  [local(): down_full = lax.all_gather(down_weight, BOTH, axis=0, tiled=True)]
    psum x1 -> x0, blocking collectives: 40 us -> none  [local(): lax.psum(jnp.concatenate([jnp.sum(grad_normed * hat_one, 0), jnp.sum(grad...]
  transfers between devices with their start and end apart: 11 -> 32, of which waited for: 8 -> 20; matrix products, arithmetic and copies ran while one was open for 23% -> 52% of each run, Pallas kernels for 7% -> 3%
where the time goes in v3:
time: 934 us; the launch traced here: 927 us
  local copies, waits for them, and re-layouts  203 us (22%)
  matrix products  190 us (20%)
  starting transfers between devices  156 us (17%)
  waiting for transfers between devices  149 us (16%)
  other arithmetic  139 us (15%)
  Pallas kernels  74.6 us (8%)
  between operations  15.5 us (2%)
    ppermute x24, starting transfers between devices, exchange(): lax.ppermute(array, axis, [(i, i ^ 1 << bit) for i in range(lax.axis_size...  139 us
    ppermute x24, waiting for transfers between devices, exchange(): lax.ppermute(array, axis, [(i, i ^ 1 << bit) for i in range(lax.axis_size...  90.9 us
    unnamed x242, local copies, waits for them, and re-layouts  70.9 us
    dot_general x10, matrix products, dot_nt(): lax.dot_general(a, b, (((1,), (1,)), ((), ())), preferred_element_type=jn...  70.1 us
    dynamic_slice x8, local copies, waits for them, and re-layouts, pick_columns(): lax.dynamic_index_in_dim(split, mine if ours else 1 - mine, 2, keepdims=F...  67.3 us
    dot_general x20, matrix products, dot_tn(): lax.dot_general(a, b, (((0,), (0,)), ((), ())), preferred_element_type=jn...  64.8 us
    ppermute x3, waiting for transfers between devices, local(): shift = lambda array: lax.ppermute(array, 'seq', upward)  57.9 us
    dot_general x6, matrix products, dot_nn(): lax.dot_general(a, b, (((1,), (0,)), ((), ())), preferred_element_type=jn...  55.1 us
  transfers between devices with their start and end apart: 32, of which 20 were waited for; matrix products, arithmetic and copies ran while one was open for 52% of the time, Pallas kernels for 3%

profile of v3, /device:TPU:0, one launch (start us, length us, event | category | flops | bytes accessed | tf_op | source)
XLA Modules:
  0.0 926.6 jit_solution(12930926564442737534)
XLA Ops:
  27.1 28.6 %collective-permute-done = bf16[2,288,1024]{2,1,0:T(8,128)(2,1)S(1)} collective-permute-done((bf16[2,288,1024]{2,1,0:T(8,128)(2,1)}, bf16[2,288,1024]{2,1,0:T(8,128)(2,1)S(1)}, u32[]{:S(2)}, u32[]{:S(2)}) %collective-permute-start) | collective-permute-done | bytes 1179680 | tf_op jit(solution)/shard_map/ppermute | solution.py:371
  68.7 29.1 %collective-permute-done.1 = bf16[2,224,1024]{2,1,0:T(8,128)(2,1)} collective-permute-done((bf16[2,224,1024]{2,1,0:T(8,128)(2,1)}, bf16[2,224,1024]{2,1,0:T(8,128)(2,1)}, u32[]{:S(2)}, u32[]{:S(2)}) %collective-permute-start.1) | collective-permute-done | bytes 917536 | tf_op jit(solution)/shard_map/ppermute | solution.py:371
  138.2 9.8 %fusion.84 = f32[1024,3072]{1,0:T(8,128)S(1)} fusion(bf16[1024,1024]{1,0:T(8,128)(2,1)} %get-tuple-element.272, bf16[1024,3072]{1,0:T(8,128)(2,1)} %all-gather.4.cloned.1.call-done), kind=kOutput, calls=%fused_computation.244 | convolution fusion | flops 6442450944 | bytes 20971520 | tf_op jit(solution)/shard_map/dot_general | solution.py:19
  165.3 30.2 %attend.1 = (bf16[2,512,1024]{2,1,0:T(8,128)(2,1)}, f32[2,4,4,512]{3,2,1,0:T(4,128)}) custom-call(s32[2,2]{1,0:T(2,128)} %slice.147.first_ref, f32[16]{0:T(128)} %scale_ref.3, bf16[2,512,1024]{2,1,0:T(8,128)(2,1)} %bitcast.246, bf16[2,512,1024]{2,1,0:T(8,128)(2,1)} %bitcast.250, bf16[2,512,1024]{2,1,0:T(8,128)(2,1)} %bitcast.252, ...), custom_call_target="tpu_custom_call" | custom-call | tf_op jit(solution)/shard_map/attend/pallas_call | solution.py:133
  199.9 12.1 %constant_dynamic-slice_fusion.6 = (bf16[1024,4,1,128]{3,2,1,0:T(2,128)(2,1)}, bf16[1024,4,1,128]{3,2,1,0:T(2,128)(2,1)}, bf16[1024,4,1,128]{3,2,1,0:T(2,128)(2,1)}, bf16[1024,4,1,128]{3,2,1,0:T(2,128)(2,1)}) fusion(bf16[1024,4,2,128]{3,2,1,0:T(2,128)(2,1)} %reshape_reshape.4, s32[]{:T(128)S(6)} %select_n.85, s32[]{:T(128)S(6)} %select_n.84, ...), kind=kLoop, calls=%fused_computation.189 | loop fusion | bytes 8388616 | tf_op jit(solution)/shard_map/jit(dynamic_index_in_dim)/dynamic_slice | solution.py:286
  250.7 17.7 %fusion.76 = (f32[1024]{0:T(1024)S(1)}, f32[1024,4096]{1,0:T(8,128)}, f32[1024,4096]{1,0:T(8,128)}) fusion(f32[4096]{0:T(1024)S(1)} %copy-done.97, bf16[1024,1024]{1,0:T(8,128)(2,1)} %add_convert_fusion.9, bf16[1024,5120]{1,0:T(8,128)(2,1)} %all-gather.6.cloned.1.call-done), kind=kOutput, calls=%fused_computation.237 | convolution fusion | flops 8615099392 | bytes 44060672 | tf_op jit(solution)/shard_map/dot_general | solution.py:19
  275.9 10.2 %add_convert_fusion = bf16[1024,4096]{1,0:T(8,128)(2,1)} fusion(f32[1024,4096]{1,0:T(8,128)} %get-tuple-element.198, f32[4096]{0:T(1024)S(1)} %copy-done.95, f32[4096]{0:T(1024)S(1)} %copy-done.74, f32[1024]{0:T(1024)S(1)} %add_rsqrt_fusion, f32[1024]{0:T(1024)S(1)} %broadcast_multiply_fusion.2), kind=kLoop, calls=%fused_computation.10 | loop fusion | flops 20971520 | bytes 25206784 | tf_op jit(solution)/shard_map/convert_element_type | solution.py:422
  286.1 14.5 %reshape.658 = bf16[1024,4,2,512]{3,2,1,0:T(2,128)(2,1)} reshape(bf16[1024,4096]{1,0:T(8,128)(2,1)} %add_convert_fusion) | data formatting | bytes 16777216 | tf_op jit(solution)/shard_map/reshape | solution.py:285
  300.6 20.5 %constant_dynamic-slice_fusion.21 = (bf16[1024,4,1,512]{3,2,1,0:T(2,128)(2,1)}, bf16[1024,4,1,512]{3,2,1,0:T(2,128)(2,1)}) fusion(bf16[1024,4,2,512]{3,2,1,0:T(2,128)(2,1)} %reshape.658, s32[]{:T(128)S(6)} %select_n.84, s32[]{:T(128)S(6)} %select_n.85), kind=kLoop, calls=%fused_computation.204 | loop fusion | bytes 16777224 | tf_op jit(solution)/shard_map/jit(dynamic_index_in_dim)/dynamic_slice | solution.py:286
  321.2 20.2 %copy.80 = bf16[1024,4,1,512]{0,3,1,2:T(8,128)(2,1)} copy(bf16[1024,4,1,512]{3,2,1,0:T(2,128)(2,1)} %get-tuple-element.203) | data formatting | bytes 8388608
  341.4 9.5 %convolution_convert_fusion.1 = bf16[2048,1024]{1,0:T(8,128)(2,1)} fusion(bf16[1024,2048]{0,1:T(8,128)(2,1)} %bitcast.280, bf16[1024,1024]{1,0:T(8,128)(2,1)} %bitcast.266), kind=kOutput, calls=%fused_computation.89 | convolution fusion | flops 4297064448 | bytes 10485760 | tf_op jit(solution)/shard_map/dot_general | solution.py:27
  350.9 9.9 %constant_dynamic-slice_fusion.12 = (bf16[1024,4,1,128]{3,2,1,0:T(2,128)(2,1)}, bf16[1024,4,1,128]{3,2,1,0:T(2,128)(2,1)}, bf16[1024,4,1,128]{3,2,1,0:T(2,128)(2,1)}, bf16[1024,4,1,128]{3,2,1,0:T(2,128)(2,1)}) fusion(bf16[1024,4,2,128]{3,2,1,0:T(2,128)(2,1)S(1)} %copy-done.14, s32[]{:T(128)S(6)} %select_n.84, s32[]{:T(128)S(6)} %select_n.85, ...), kind=kLoop, calls=%fused_computation.195 | loop fusion | bytes 8388616 | tf_op jit(solution)/shard_map/jit(dynamic_index_in_dim)/dynamic_slice | solution.py:286
  366.6 20.0 %copy.79 = bf16[1024,4,1,512]{0,3,1,2:T(8,128)(2,1)} copy(bf16[1024,4,1,512]{3,2,1,0:T(2,128)(2,1)} %get-tuple-element.204) | data formatting | bytes 8388608
  413.2 15.8 %add_convert_fusion.8 = bf16[1024,1024]{1,0:T(8,128)(2,1)} fusion(f32[1024,1024]{1,0:T(8,128)} %copy-done.4, f32[1024]{0:T(1024)S(1)} %copy-done.111, bf16[1024,4096]{1,0:T(8,128)(2,1)} %add_convert_fusion, bf16[4096,1024]{1,0:T(8,128)(2,1)} %all-gather.8.cloned.1.call-done), kind=kOutput, calls=%fused_computation.81 | convolution fusion | flops 8593080320 | bytes 23072768 | tf_op jit(solution)/shard_map/dot_general | solution.py:19
  436.0 21.6 %multiply_reduce_fusion = (f32[4096]{0:T(1024)}, f32[1024]{0:T(1024)S(1)}, f32[1024]{0:T(1024)S(1)}, f32[4096]{0:T(1024)}, f32[1024,4096]{1,0:T(8,128)}) fusion(f32[1024,4096]{1,0:T(8,128)} %get-tuple-element.198, f32[1024]{0:T(1024)S(1)} %add_rsqrt_fusion, f32[1024]{0:T(1024)S(1)} %broadcast_multiply_fusion.2, f32[4096]{0:T(1024)S(1)} %copy-done.74, ...), kind=kOutput, calls=%fused_computation.7 | convolution fusion | flops 8627673088 | bytes 44105728 | tf_op jit(solution)/shard_map/dot_general | solution.py:23
  457.7 17.4 %fusion.5 = bf16[1024,4096]{1,0:T(8,128)(2,1)S(1)} fusion(f32[1024,4096]{1,0:T(8,128)} %get-tuple-element.281, f32[1024,4096]{1,0:T(8,128)} %get-tuple-element.280, f32[1024,4096]{1,0:T(8,128)} %get-tuple-element.198, f32[1024]{0:T(1024)S(1)} %get-tuple-element.289, f32[1024]{0:T(1024)S(1)} %get-tuple-element.290, f32[4096]{0:T(1024)S(1)} %copy-done.74, ...), kind=kLoop, calls=%fused_computation.6 | loop fusion | flops 75497472 | bytes 58769408 | tf_op jit(solution)/shard_map/convert_element_type | solution.py:438
  493.4 14.4 %multiply_reduce_fusion.5 = (f32[1024]{0:T(1024)}, f32[1024]{0:T(1024)S(1)}, f32[1024]{0:T(1024)S(1)}, f32[1024]{0:T(1024)}, f32[1024,1024]{1,0:T(8,128)}) fusion(f32[1024,1024]{1,0:T(8,128)S(1)} %copy-done.5, f32[1024]{0:T(1024)S(1)} %copy-done.86, f32[1024]{0:T(1024)S(1)} %copy-done.73, f32[1024]{0:T(1024)S(1)} %copy-done.89, ...), kind=kOutput, calls=%fused_computation.66 | convolution fusion | flops 8599367680 | bytes 25194496 | tf_op jit(solution)/shard_map/dot_general | solution.py:23
  546.9 44.4 %attend_back.1 = (bf16[2,512,1024]{2,1,0:T(8,128)(2,1)}, bf16[2,512,1024]{2,1,0:T(8,128)(2,1)}, bf16[2,512,1024]{2,1,0:T(8,128)(2,1)}, bf16[2,288,1024]{2,1,0:T(...) custom-call(s32[2,2]{1,0:T(2,128)} %slice.147.first_ref, ...), custom_call_target="tpu_custom_call" | custom-call | tf_op jit(solution)/shard_map/attend_back/pallas_call | solution.py:229
  610.1 85.6 %collective-permute-start.9 = (bf16[256,1024]{1,0:T(8,128)(2,1)S(1)}, bf16[256,1024]{1,0:T(8,128)(2,1)S(1)}, u32[]{:S(2)}, u32[]{:S(2)}) collective-permute-start(bf16[256,1024]{1,0:T(8,128)(2,1)S(1)} %bitcast.324), channel_id=1, source_target_pairs={{0,1},{1,0},{2,3},{3,2},{4,5},{5,4},{6,7},{7,6},{8,9},{9,8},{10,11... | collective-permute-start | bytes 1572872 | tf_op jit(solution)/shard_map/ppermute | solution.py:274
  767.4 18.4 %collective-permute-done.20 = bf16[128,4096]{1,0:T(8,128)(2,1)S(1)} collective-permute-done((bf16[128,4096]{1,0:T(8,128)(2,1)S(1)}, bf16[128,4096]{1,0:T(8,128)(2,1)S(1)}, u32[]{:S(2)}, u32[]{:S(2)}) %collective-permute-start.20) | collective-permute-done | bytes 1048608 | tf_op jit(solution)/shard_map/ppermute | solution.py:274
  786.2 14.3 %collective-permute-start.21 = (bf16[64,4096]{1,0:T(8,128)(2,1)S(1)}, bf16[64,4096]{1,0:T(8,128)(2,1)S(1)}, u32[]{:S(2)}, u32[]{:S(2)}) collective-permute-start(bf16[64,4096]{1,0:T(8,128)(2,1)S(1)} %bitcast.325), channel_id=1, source_target_pairs={{0,1},{1,0},{2,3},{3,2},{4,5},{5,4},{6,7},{7,6},{8,9},{9,8},{10,11... | collective-permute-start | bytes 1572872 | tf_op jit(solution)/shard_map/ppermute | solution.py:274
  803.2 9.2 collective-permute-done.21
  832.8 14.0 %collective-permute-start.26 = (f32[22544]{0:T(1024)S(1)}, f32[22544]{0:T(1024)S(1)}, u32[]{:S(2)}, u32[]{:S(2)}) collective-permute-start(f32[22544]{0:T(1024)S(1)} %add.511), channel_id=1, source_target_pairs={{0,16},{4,20},{8,24},{12,28},{16,0},{20,4},{24,8},{28,12},{1,17},{... | collective-permute-start | bytes 270536 | tf_op jit(solution)/shard_map/ppermute | solution.py:274
  870.8 14.7 %collective-permute-done.12 = bf16[256,2048]{1,0:T(8,128)(2,1)S(1)} collective-permute-done((bf16[256,2048]{1,0:T(8,128)(2,1)S(1)}, bf16[256,2048]{1,0:T(8,128)(2,1)S(1)}, u32[]{:S(2)}, u32[]{:S(2)}) %collective-permute-start.12) | collective-permute-done | bytes 1048608 | tf_op jit(solution)/shard_map/ppermute | solution.py:274
  (463 shorter events, 409.0 us)
Async XLA Ops:
  7.2 130.9 %all-gather.4.cloned.1.call-start = ((), (), s32[]{:S(2)}) async-start(), calls=%async_computation | async-start | bytes 6488064 | tf_op jit(solution)/shard_map/all_gather | solution.py:383
  9.0 226.4 %all-gather.6.cloned.1.call-start = ((), (), s32[]{:S(2)}) async-start(), calls=%async_computation.1 | async-start | bytes 10813440 | tf_op jit(solution)/shard_map/all_gather | solution.py:384
  10.8 402.4 %all-gather.8.cloned.1.call-start = ((), (), s32[]{:S(2)}) async-start(), calls=%async_computation.2 | async-start | bytes 8650752 | tf_op jit(solution)/shard_map/all_gather | solution.py:385
  13.2 42.5 %collective-permute-start = (bf16[2,288,1024]{2,1,0:T(8,128)(2,1)}, bf16[2,288,1024]{2,1,0:T(8,128)(2,1)S(1)}, u32[]{:S(2)}, u32[]{:S(2)}) collective-permute-start(bf16[2,288,1024]{2,1,0:T(8,128)(2,1)} %slice.151), channel_id=1, source_target_pairs={{0,1},{1,2},{2,3},{4,5},{5,6},{6,7},{8,9},{9,10},{10,11},{12,13},{... | collective-permute-start | bytes 3538952 | tf_op jit(solution)/shard_map/ppermute | solution.py:371
  55.7 42.2 %collective-permute-start.1 = (bf16[2,224,1024]{2,1,0:T(8,128)(2,1)}, bf16[2,224,1024]{2,1,0:T(8,128)(2,1)}, u32[]{:S(2)}, u32[]{:S(2)}) collective-permute-start(bf16[2,224,1024]{2,1,0:T(8,128)(2,1)} %slice.150), channel_id=1, source_target_pairs={{0,1},{1,2},{2,3},{4,5},{5,6},{6,7},{8,9},{9,10},{10,11},{12,13},{... | collective-permute-start | bytes 2752520 | tf_op jit(solution)/shard_map/ppermute | solution.py:371
  65.6 60.6 %collective-permute-start.2 = (bf16[2,288,1024]{2,1,0:T(8,128)(2,1)}, bf16[2,288,1024]{2,1,0:T(8,128)(2,1)S(1)}, u32[]{:S(2)}, u32[]{:S(2)}) collective-permute-start(bf16[2,288,1024]{2,1,0:T(8,128)(2,1)} %copy-done.11), channel_id=1, source_target_pairs={{0,1},{1,2},{2,3},{4,5},{5,6},{6,7},{8,9},{9,10},{10,11},{12,13},{... | collective-permute-start | bytes 3538952 | tf_op jit(solution)/shard_map/ppermute | solution.py:371
  350.9 78.1 %collective-permute-start.3 = (bf16[2048,1024]{1,0:T(8,128)(2,1)}, bf16[2048,1024]{1,0:T(8,128)(2,1)}, u32[]{:S(2)}, u32[]{:S(2)}) collective-permute-start(bf16[2048,1024]{1,0:T(8,128)(2,1)} %convolution_convert_fusion.1), channel_id=1, source_target_pairs={{0,4},{4,0},{8,12},{12,8},{16,20},{20,16},{24,28},{28,24},{1,5},{5... | collective-permute-start | bytes 12582920 | tf_op jit(solution)/shard_map/ppermute | solution.py:274
  434.6 48.3 %collective-permute-start.4 = (bf16[1024,1024]{1,0:T(8,128)(2,1)}, bf16[1024,1024]{1,0:T(8,128)(2,1)}, u32[]{:S(2)}, u32[]{:S(2)}) collective-permute-start(bf16[1024,1024]{1,0:T(8,128)(2,1)} %get-tuple-element.105), channel_id=1, source_target_pairs={{0,16},{4,20},{8,24},{12,28},{16,0},{20,4},{24,8},{28,12},{1,17},{... | collective-permute-start | bytes 6291464 | tf_op jit(solution)/shard_map/ppermute | solution.py:274
  493.2 38.5 %collective-permute-start.6 = (bf16[512,4096]{1,0:T(8,128)(2,1)}, bf16[512,4096]{1,0:T(8,128)(2,1)}, u32[]{:S(2)}, u32[]{:S(2)}) collective-permute-start(bf16[512,4096]{1,0:T(8,128)(2,1)} %convolution_convert_fusion), channel_id=1, source_target_pairs={{0,4},{4,0},{8,12},{12,8},{16,20},{20,16},{24,28},{28,24},{1,5},{5... | collective-permute-start | bytes 12582920 | tf_op jit(solution)/shard_map/ppermute | solution.py:274
  507.8 36.4 %collective-permute-start.5 = (bf16[512,1024]{1,0:T(8,128)(2,1)}, bf16[512,1024]{1,0:T(8,128)(2,1)}, u32[]{:S(2)}, u32[]{:S(2)}) collective-permute-start(bf16[512,1024]{1,0:T(8,128)(2,1)} %get-tuple-element.113), channel_id=1, source_target_pairs={{0,8},{4,12},{8,0},{12,4},{16,24},{20,28},{24,16},{28,20},{1,9},{5... | collective-permute-start | bytes 3145736 | tf_op jit(solution)/shard_map/ppermute | solution.py:274
  609.4 117.3 %collective-permute-start.8 = (bf16[256,4096]{1,0:T(8,128)(2,1)}, bf16[256,4096]{1,0:T(8,128)(2,1)}, u32[]{:S(2)}, u32[]{:S(2)}) collective-permute-start(bf16[256,4096]{1,0:T(8,128)(2,1)} %bitcast.24), channel_id=1, source_target_pairs={{0,8},{4,12},{8,0},{12,4},{16,24},{20,28},{24,16},{28,20},{1,9},{5... | collective-permute-start | bytes 6291464 | tf_op jit(solution)/shard_map/ppermute | solution.py:274
  610.1 100.9 %collective-permute-start.9 = (bf16[256,1024]{1,0:T(8,128)(2,1)S(1)}, bf16[256,1024]{1,0:T(8,128)(2,1)S(1)}, u32[]{:S(2)}, u32[]{:S(2)}) collective-permute-start(bf16[256,1024]{1,0:T(8,128)(2,1)S(1)} %bitcast.324), channel_id=1, source_target_pairs={{0,1},{1,0},{2,3},{3,2},{4,5},{5,4},{6,7},{7,6},{8,9},{9,8},{10,11... | collective-permute-start | bytes 1572872 | tf_op jit(solution)/shard_map/ppermute | solution.py:274
  712.0 12.9 %collective-permute-start.23 = (bf16[128,1024]{1,0:T(8,128)(2,1)}, bf16[128,1024]{1,0:T(8,128)(2,1)}, u32[]{:S(2)}, u32[]{:S(2)}) collective-permute-start(bf16[128,1024]{1,0:T(8,128)(2,1)} %get-tuple-element.175), channel_id=1, source_target_pairs={{0,2},{1,3},{2,0},{3,1},{4,6},{5,7},{6,4},{7,5},{8,10},{9,11},{10,... | collective-permute-start | bytes 786440 | tf_op jit(solution)/shard_map/ppermute | solution.py:274
  712.8 35.7 %collective-permute-start.7 = (bf16[2,288,1024]{2,1,0:T(8,128)(2,1)}, bf16[2,288,1024]{2,1,0:T(8,128)(2,1)}, u32[]{:S(2)}, u32[]{:S(2)}) collective-permute-start(bf16[2,288,1024]{2,1,0:T(8,128)(2,1)} %bitcast.35), channel_id=1, source_target_pairs={{1,0},{2,1},{3,2},{5,4},{6,5},{7,6},{9,8},{10,9},{11,10},{13,12},{... | collective-permute-start | bytes 3538952 | tf_op jit(solution)/shard_map/ppermute | solution.py:462
  751.5 65.2 %collective-permute-start.10 = (bf16[2,512,1024]{2,1,0:T(8,128)(2,1)S(1)}, bf16[2,512,1024]{2,1,0:T(8,128)(2,1)S(1)}, u32[]{:S(2)}, u32[]{:S(2)}) collective-permute-start(bf16[2,512,1024]{2,1,0:T(8,128)(2,1)S(1)} %add_convert_fusion.5), channel_id=1, source_target_pairs={{1,0},{2,1},{3,2},{5,4},{6,5},{7,6},{9,8},{10,9},{11,10},{13,12},{... | collective-permute-start | bytes 6291464 | tf_op jit(solution)/shard_map/ppermute | solution.py:462
  758.0 102.0 %collective-permute-start.11 = (bf16[512,4096]{1,0:T(8,128)(2,1)}, bf16[512,4096]{1,0:T(8,128)(2,1)}, u32[]{:S(2)}, u32[]{:S(2)}) collective-permute-start(bf16[512,4096]{1,0:T(8,128)(2,1)} %pad_maximum_fusion), channel_id=1, source_target_pairs={{0,4},{4,0},{8,12},{12,8},{16,20},{20,16},{24,28},{28,24},{1,5},{5... | collective-permute-start | bytes 12582920 | tf_op jit(solution)/shard_map/ppermute | solution.py:274
  758.0 27.8 %collective-permute-start.20 = (bf16[128,4096]{1,0:T(8,128)(2,1)S(1)}, bf16[128,4096]{1,0:T(8,128)(2,1)S(1)}, u32[]{:S(2)}, u32[]{:S(2)}) collective-permute-start(bf16[128,4096]{1,0:T(8,128)(2,1)S(1)} %get-tuple-element.169), channel_id=1, source_target_pairs={{0,16},{4,20},{8,24},{12,28},{16,0},{20,4},{24,8},{28,12},{1,17},{... | collective-permute-start | bytes 3145736 | tf_op jit(solution)/shard_map/ppermute | solution.py:274
  786.2 26.3 %collective-permute-start.21 = (bf16[64,4096]{1,0:T(8,128)(2,1)S(1)}, bf16[64,4096]{1,0:T(8,128)(2,1)S(1)}, u32[]{:S(2)}, u32[]{:S(2)}) collective-permute-start(bf16[64,4096]{1,0:T(8,128)(2,1)S(1)} %bitcast.325), channel_id=1, source_target_pairs={{0,1},{1,0},{2,3},{3,2},{4,5},{5,4},{6,7},{7,6},{8,9},{9,8},{10,11... | collective-permute-start | bytes 1572872 | tf_op jit(solution)/shard_map/ppermute | solution.py:274
  813.4 14.7 %collective-permute-start.22 = (bf16[32,4096]{1,0:T(8,128)(2,1)}, bf16[32,4096]{1,0:T(8,128)(2,1)}, u32[]{:S(2)}, u32[]{:S(2)}) collective-permute-start(bf16[32,4096]{1,0:T(8,128)(2,1)} %get-tuple-element.173), channel_id=1, source_target_pairs={{0,2},{1,3},{2,0},{3,1},{4,6},{5,7},{6,4},{7,5},{8,10},{9,11},{10,... | collective-permute-start | bytes 786440 | tf_op jit(solution)/shard_map/ppermute | solution.py:274
  832.8 16.5 %collective-permute-start.26 = (f32[22544]{0:T(1024)S(1)}, f32[22544]{0:T(1024)S(1)}, u32[]{:S(2)}, u32[]{:S(2)}) collective-permute-start(f32[22544]{0:T(1024)S(1)} %add.511), channel_id=1, source_target_pairs={{0,16},{4,20},{8,24},{12,28},{16,0},{20,4},{24,8},{28,12},{1,17},{... | collective-permute-start | bytes 270536 | tf_op jit(solution)/shard_map/ppermute | solution.py:274
  863.9 21.7 %collective-permute-start.12 = (bf16[256,2048]{1,0:T(8,128)(2,1)S(1)}, bf16[256,2048]{1,0:T(8,128)(2,1)S(1)}, u32[]{:S(2)}, u32[]{:S(2)}) collective-permute-start(bf16[256,2048]{1,0:T(8,128)(2,1)S(1)} %get-tuple-element.153), channel_id=1, source_target_pairs={{0,16},{4,20},{8,24},{12,28},{16,0},{20,4},{24,8},{28,12},{1,17},{... | collective-permute-start | bytes 3145736 | tf_op jit(solution)/shard_map/ppermute | solution.py:274
  866.9 25.6 %collective-permute-start.16 = (bf16[256,2048]{1,0:T(8,128)(2,1)S(1)}, bf16[256,2048]{1,0:T(8,128)(2,1)S(1)}, u32[]{:S(2)}, u32[]{:S(2)}) collective-permute-start(bf16[256,2048]{1,0:T(8,128)(2,1)S(1)} %bitcast.319), channel_id=1, source_target_pairs={{0,8},{4,12},{8,0},{12,4},{16,24},{20,28},{24,16},{28,20},{1,9},{5... | collective-permute-start | bytes 3145736 | tf_op jit(solution)/shard_map/ppermute | solution.py:274
  886.0 13.7 %collective-permute-start.13 = (bf16[128,2048]{1,0:T(8,128)(2,1)S(1)}, bf16[128,2048]{1,0:T(8,128)(2,1)S(1)}, u32[]{:S(2)}, u32[]{:S(2)}) collective-permute-start(bf16[128,2048]{1,0:T(8,128)(2,1)S(1)} %get-tuple-element.155), channel_id=1, source_target_pairs={{0,8},{4,12},{8,0},{12,4},{16,24},{20,28},{24,16},{28,20},{1,9},{5... | collective-permute-start | bytes 1572872 | tf_op jit(solution)/shard_map/ppermute | solution.py:274
  902.5 10.1 %collective-permute-start.18 = (bf16[64,2048]{1,0:T(8,128)(2,1)S(1)}, bf16[64,2048]{1,0:T(8,128)(2,1)S(1)}, u32[]{:S(2)}, u32[]{:S(2)}) collective-permute-start(bf16[64,2048]{1,0:T(8,128)(2,1)S(1)} %bitcast.327), channel_id=1, source_target_pairs={{0,1},{1,0},{2,3},{3,2},{4,5},{5,4},{6,7},{7,6},{8,9},{9,8},{10,11... | collective-permute-start | bytes 786440 | tf_op jit(solution)/shard_map/ppermute | solution.py:274
  (124 other events, 1490.0 us)
Sparse Core Ops, SparseCore 0:
  11.5 85.4 all-gather.3
  100.3 90.3 all-gather.5
  193.6 75.5 all-gather.7

commit v4 on v3

--- a/solution.py
+++ b/solution.py
@@ -278,17 +278,48 @@
     return lax.optimization_barrier(values)
 
 
-def pick_columns(array, place, ours):
+def pick_kernel(mine_ref, array_ref, other_ref, own_ref):
+    width = own_ref.shape[1]
+    halves = array_ref[:, :width], array_ref[:, width:]
+    for index in range(2):
+        @pl.when(mine_ref[0] == index)
+        def _():
+            own_ref[...] = halves[index]
+            other_ref[...] = halves[1 - index]
+
+
+def pick_columns(array, place):
     axis, bit = place
     order = bits_of("dp")[::-1] + bits_of("seq")[::-1]
     mine = (lax.axis_index(axis) >> bit) & 1
-    split = array.reshape(array.shape[0], 1 << order.index(place), 2, -1)
-    picked = lax.dynamic_index_in_dim(split, mine if ours else 1 - mine, 2, keepdims=False)
-    return picked.reshape(array.shape[0], -1)
-
-
-own_columns = functools.partial(pick_columns, ours=True)
-other_columns = functools.partial(pick_columns, ours=False)
+    tokens, columns = array.shape
+    above = 1 << order.index(place)
+    width = columns // above // 2
+    if width % 128:
+        split = array.reshape(tokens, above, 2, width)
+        take = lambda index: lax.dynamic_index_in_dim(split, index, 2, keepdims=False).reshape(tokens, -1)
+        return take(1 - mine), take(mine)
+    half = jax.ShapeDtypeStruct((tokens, columns // 2), array.dtype)
+    return pl.pallas_call(
+        pick_kernel,
+        grid_spec=pltpu.PrefetchScalarGridSpec(
+            num_scalar_prefetch=1,
+            grid=(above,),
+            in_specs=[pl.BlockSpec((tokens, 2 * width), lambda block, _: (0, block))],
+            out_specs=[pl.BlockSpec((tokens, width), lambda block, _: (0, block))] * 2,
+        ),
+        out_shape=[half, half],
+        name="pick",
+    )(mine.reshape(1), array)
+
+
+class Sequence:
+    def __init__(self, token):
+        self.token = token
+
+    def __call__(self, *values):
+        *values, self.token = together(*values, self.token)
+        return values[0] if len(values) == 1 else values
 
 
 class RowSum:
@@ -297,38 +328,27 @@
         self.left = bits_of("dp")[::-1] + bits_of("seq")[::-1]
         self.came = self.kept = self.total = None
 
-    def begin(self, sent):
-        axis, bit = self.order.pop(0)
-        self.left.remove((axis, bit))
-        self.came = exchange(sent, axis, bit)
-
-    def end_step(self, *chain):
-        came, *chain = together(self.came, *chain)
-        self.total = self.kept.astype(jnp.float32) + came.astype(jnp.float32)
-        return chain
-
-    def begin_step(self, *chain):
+    def begin(self, came):
+        self.left.remove(self.order.pop(0))
+        self.came = came
+
+    def step(self, sequence):
+        came, self.kept = sequence(self.came, self.kept)
+        total = self.kept.astype(jnp.float32) + came.astype(jnp.float32)
+        if not self.order:
+            self.total = sequence(total)
+            return
         axis, bit = self.order.pop(0)
         at = self.left.index((axis, bit))
         self.left.pop(at)
-        total = self.total.astype(jnp.bfloat16)
+        total = total.astype(jnp.bfloat16)
         columns = total.shape[-1]
         split = total.reshape(1 << at, 2, -1, columns)
         mine = (lax.axis_index(axis) >> bit) & 1
         gone = lax.dynamic_index_in_dim(split, 1 - mine, 1, keepdims=False).reshape(-1, columns)
         kept = lax.dynamic_index_in_dim(split, mine, 1, keepdims=False).reshape(-1, columns)
-        gone, self.kept, *chain = together(gone, kept, *chain)
+        gone, self.kept = sequence(gone, kept)
         self.came = exchange(gone, axis, bit)
-        return chain
-
-    def advance(self, *chain):
-        return self.begin_step(*self.end_step(*chain))
-
-
-def reduce_all(vector):
-    for axis, bit in bits_of("dp") + bits_of("seq"):
-        vector = vector + exchange(vector, axis, bit)
-    return vector
 
 
 def local(
@@ -427,113 +447,144 @@
     other_way = [core, *planes, *bits_of("seq")]
 
     down_sum, up_sum = RowSum(one_way), RowSum(other_way)
-    sent = dot_tn(other_columns(mixed, core), grad_low).astype(jnp.bfloat16)
-    down_sum.begin(sent)
-    down_sum.kept = dot_tn(own_columns(mixed, core), grad_low)
-    (late_low,) = down_sum.advance(grad_low)
-
-    layer_output = (middle + dot_nn(mixed, down_full) + down_bias).astype(jnp.bfloat16)
-    grad_mixed = dot_nt(late_low, down_full)
+    sums = query_key_sum, value_output_sum = RowSum(one_way), RowSum(other_way)
+    sequence = Sequence(jnp.zeros((8, 128), jnp.float32))
+    other_mixed, own_mixed = pick_columns(mixed, core)
+    sent, own_mixed, low = sequence(dot_tn(other_mixed, grad_low).astype(jnp.bfloat16), own_mixed, grad_low)
+    down_sum.begin(exchange(sent, *core))
+    down_sum.kept = dot_tn(own_mixed, low)
+    down_sum.step(sequence)
+
+    low = sequence(low)
+    grad_mixed = dot_nt(low, down_full)
     slope = phi + upper * (0.3989422804014327 * jnp.exp(-0.5 * upper * upper))
     grad_upper = (norm_back(hat_middle, scale_middle, middle_gain, grad_mixed) * slope).astype(jnp.bfloat16)
-    (grad_upper,) = down_sum.advance(grad_upper)
-    sent = dot_tn(other_columns(second, core), grad_upper).astype(jnp.bfloat16)
-    sent, grad_upper = together(sent, grad_upper)
-    up_sum.begin(sent)
+    other_second, own_second = pick_columns(second, core)
+    grad_upper = sequence(grad_upper)
+    down_sum.step(sequence)
+    sent = dot_tn(other_second, sequence(grad_upper)).astype(jnp.bfloat16)
+    sent, grad_upper = sequence(sent, grad_upper)
+    up_sum.begin(exchange(sent, *core))
+    up_sum.kept = dot_tn(own_second, grad_upper)
+    up_sum.step(sequence)
+    grad_upper = sequence(grad_upper)
     grad_second = dot_nt(grad_upper, up_full)
     grad_middle = grad_out + norm_back(hat_two, scale_two, second_gain, grad_second)
     grad_branch = norm_back(hat_post, scale_post, post_gain, grad_middle).astype(jnp.bfloat16)
-    up_sum.kept = dot_tn(own_columns(second, core), grad_upper)
-    (grad_branch,) = up_sum.advance(grad_branch)
+    grad_branch = sequence(grad_branch)
+    down_sum.step(sequence)
+    grad_branch = sequence(grad_branch)
     grad_scaled = dot_nt(grad_branch, output_full)
     grad_attended = (grad_scaled * jnp.repeat(head_scale, model // head_count)).astype(jnp.bfloat16)
-    (grad_attended,) = down_sum.advance(grad_attended)
     head_columns = jnp.sum(grad_scaled * scaled_low.astype(jnp.float32), 0)
     head_term = jnp.sum(head_columns.reshape(head_count, -1), -1) / head_scale
+    grad_attended = sequence(grad_attended)
 
     dquery, dkeys, dvalues = attend_back(
         first, head_scale, query, keys, values, start, lse, scaled, stacked(grad_attended), hops
     )
-    partials = [
-        dot_nt(flat(dkeys[hop + 1]), inward[:, model : 2 * model])
-        + dot_nt(flat(dvalues[hop + 1]), inward[:, 2 * model :])
-        for hop in range(len(hops))
-    ]
+    dkeys, dvalues = [flat(d) for d in dkeys], [flat(d) for d in dvalues]
+    query_low = sequence(flat(dquery))
+    back = lambda dkey, dvalue: dot_nt(dkey, inward[:, model : 2 * model]) + dot_nt(dvalue, inward[:, 2 * model :])
     lower = lambda array: lax.ppermute(array, "seq", downward)
-    query_low, key_low, value_low = flat(dquery), flat(dkeys[0]), flat(dvalues[0])
+    partials = [None] * len(hops)
     carried = None
     if hops:
-        going = stacked(partials[-1]).astype(jnp.bfloat16)
-        going, query_low = together(going, query_low)
-        carried = lower(going)
-    query_low, key_low, value_low = down_sum.advance(query_low, key_low, value_low)
-    query_low, key_low, value_low = up_sum.advance(query_low, key_low, value_low)
-
-    inward_sums = RowSum(one_way), RowSum(other_way)
-    halo_normed = normed_pieces[1:]
-    halo_pairs = [(flat(k), flat(v)) for k, v in zip(dkeys[1:], dvalues[1:])]
-
-    def four(pick):
-        mine = pick(normed, core)
-        key_part, value_part = dot_tn(mine, key_low), dot_tn(mine, value_low)
-        for piece, (dkey, dvalue) in zip(halo_normed, halo_pairs):
-            picked = pick(piece, core)
-            key_part, value_part = key_part + dot_tn(picked, dkey), value_part + dot_tn(picked, dvalue)
-        return dot_tn(mine, query_low), key_part, value_part, dot_tn(pick(scaled_low, core), grad_branch)
-
-    sent = jnp.concatenate([part.astype(jnp.bfloat16) for part in four(other_columns)], 1)
+        partials[-1] = back(dkeys[-1], dvalues[-1])
+        carried = lower(sequence(stacked(partials[-1]).astype(jnp.bfloat16)))
+    down_sum.step(sequence)
+    up_sum.step(sequence)
+
+    picked = [pick_columns(piece, core) for piece in normed_pieces]
+    picked_scaled = pick_columns(scaled_low, core)
+    query_low, grad_branch, dkeys[0], dvalues[0] = sequence(query_low, grad_branch, dkeys[0], dvalues[0])
+
+    def four(side):
+        return (
+            dot_tn(picked[0][side], query_low),
+            sum(dot_tn(p[side], d) for p, d in zip(picked, dkeys)),
+            sum(dot_tn(p[side], d) for p, d in zip(picked, dvalues)),
+            dot_tn(picked_scaled[side], grad_branch),
+        )
+
+    sent = sequence(jnp.concatenate([part.astype(jnp.bfloat16) for part in four(0)], 1))
     came = exchange(sent, *core)
+    query_low, grad_branch, dkeys[0], dvalues[0] = sequence(query_low, grad_branch, dkeys[0], dvalues[0])
+    mine = four(1)
+    for hop in range(len(hops) - 1):
+        partials[hop] = back(*sequence(dkeys[hop + 1], dvalues[hop + 1]))
+    for index, row_sum in enumerate(sums):
+        columns = slice(2 * index * model, 2 * (index + 1) * model)
+        row_sum.begin(came[:, columns])
+        row_sum.kept = jnp.concatenate(mine[2 * index : 2 * (index + 1)], 1)
+        row_sum.step(sequence)
+    for hop in reversed(range(len(hops) - 1)):
+        carried, partial = sequence(carried, partials[hop])
+        partial = stacked(partial)
+        missing = partial.shape[1] - carried.shape[1]
+        going = partial + jnp.pad(carried.astype(jnp.float32), ((0, 0), (missing, 0), (0, 0)))
+        carried = lower(sequence(going.astype(jnp.bfloat16)))
+    down_sum.step(sequence)
+
+    query_low, dkeys[0], dvalues[0] = sequence(query_low, dkeys[0], dvalues[0])
     own = (
         dot_nt(query_low, inward[:, :model])
-        + dot_nt(key_low, inward[:, model : 2 * model])
-        + dot_nt(value_low, inward[:, 2 * model :])
+        + dot_nt(dkeys[0], inward[:, model : 2 * model])
+        + dot_nt(dvalues[0], inward[:, 2 * model :])
     )
-    for hop in reversed(range(len(hops) - 1)):
-        carried, own = together(carried, own)
-        partial = stacked(partials[hop])
-        going = partial + jnp.pad(
-            carried.astype(jnp.float32), ((0, 0), (partial.shape[1] - carried.shape[1], 0), (0, 0))
-        )
-        going, own = together(going.astype(jnp.bfloat16), own)
-        carried = lower(going)
-    mine = four(own_columns)
-    for index, row_sum in enumerate(inward_sums):
-        row_sum.order.pop(0)
-        row_sum.left.remove(core)
-        row_sum.came = came[:, 2 * index * model : 2 * (index + 1) * model]
-        row_sum.kept = jnp.concatenate(mine[2 * index : 2 * (index + 1)], 1)
-
-    vectors = reduce_all(
-        jnp.concatenate(
-            [
-                head_term,
-                jnp.sum(grad_branch.astype(jnp.float32), 0),
-                jnp.sum(grad_middle * hat_post, 0),
-                jnp.sum(grad_middle, 0),
-                jnp.sum(grad_second * hat_two, 0),
-                jnp.sum(grad_second, 0),
-                jnp.sum(grad_out, 0),
-                jnp.sum(own * hat_one, 0) + sum(jnp.sum(p * h, 0) for p, h in zip(partials, hats[1:])),
-                jnp.sum(own, 0) + sum(jnp.sum(p, 0) for p in partials),
-                jnp.sum(query_low.astype(jnp.float32), 0),
-                sum(jnp.sum(d.astype(jnp.float32), (0, 1)) for d in dvalues),
-                jnp.sum(grad_upper.astype(jnp.float32), 0),
-                jnp.sum(grad_mixed * hat_middle, 0),
-                jnp.sum(grad_mixed, 0),
-            ]
-        )
+    own = sequence(own)
+    for row_sum in sums:
+        row_sum.step(sequence)
+    own = sequence(own)
+    vector = jnp.concatenate(
+        [
+            head_term,
+            jnp.sum(grad_branch.astype(jnp.float32), 0),
+            jnp.sum(grad_middle * hat_post, 0),
+            jnp.sum(grad_middle, 0),
+            jnp.sum(grad_second * hat_two, 0),
+            jnp.sum(grad_second, 0),
+            jnp.sum(grad_out, 0),
+            jnp.sum(own * hat_one, 0) + sum(jnp.sum(p * h, 0) for p, h in zip(partials, hats[1:])),
+            jnp.sum(own, 0) + sum(jnp.sum(p, 0) for p in partials),
+            jnp.sum(query_low.astype(jnp.float32), 0),
+            sum(jnp.sum(d.astype(jnp.float32), 0) for d in dvalues),
+            jnp.sum(grad_upper.astype(jnp.float32), 0),
+            jnp.sum(grad_mixed * hat_middle, 0),
+            jnp.sum(grad_mixed, 0),
+        ]
     )
-    for row_sum in (down_sum, up_sum, *inward_sums):
-        while row_sum.order:
-            row_sum.advance()
-        row_sum.end_step()
-
+    places = bits_of("dp") + bits_of("seq")
+
+    def sum_vector(vector, count):
+        for _ in range(min(count, len(places))):
+            vector = sequence(vector + exchange(vector, *places.pop(0)))
+        return vector
+
+    vector = sum_vector(sequence(vector), 1)
+    up_sum.step(sequence)
+    mixed, middle = sequence(mixed, middle)
+    layer_output = sequence((middle + dot_nn(mixed, down_full) + down_bias).astype(jnp.bfloat16))
+    for row_sum in sums:
+        row_sum.step(sequence)
+    vector = sum_vector(vector, 2)
+    up_sum.step(sequence)
+    vector = sum_vector(vector, 1)
     grad_normed = own
     if hops:
+        carried, own = sequence(carried, own)
         grad_normed = own + flat(jnp.pad(carried.astype(jnp.float32), ((0, 0), (rows - carried.shape[1], 0), (0, 0))))
     input_grad = (grad_middle + norm_back(hat_one, scale_one, first_gain, grad_normed)).astype(jnp.bfloat16)
-
-    query_key, value_output = (row_sum.total for row_sum in inward_sums)
+    for row_sum in sums:
+        row_sum.step(sequence)
+    input_grad = sequence(input_grad)
+    vector = sum_vector(vector, len(places))
+    for row_sum in (up_sum, *sums, down_sum):
+        while row_sum.total is None:
+            row_sum.step(sequence)
+    vectors = vector + sequence.token[0, 0]
+
+    query_key, value_output = query_key_sum.total, value_output_sum.total
     rest = vectors[head_count:]
     narrow = rest[: 10 * model].reshape(10, model)
     broad = rest[10 * model :].reshape(3, hidden)

time: 934 us -> 780 us (0.84)
  local copies, waits for them, and re-layouts: 203 us -> 38.5 us
  waiting for transfers between devices: 149 us -> 187 us
  starting transfers between devices: 156 us -> 124 us
  Pallas kernels: 74.6 us -> 103 us
  other arithmetic: 139 us -> 117 us
    dynamic_slice x14 -> x6, local copies, waits for them, and re-layouts: 70.5 us -> 6.58 us  [step(): lax.dynamic_index_in_dim(split, mine, 1, keepdims=False)]
    unnamed x242 -> x222, local copies, waits for them, and re-layouts: 70.9 us -> 7.78 us
    ppermute x24, starting transfers between devices: 139 us -> 108 us  [exchange(): lax.ppermute(array, axis, [(i, i ^ 1 << bit) for i in range(lax.axis_size...]
    ppermute x3, waiting for transfers between devices: 57.9 us -> 87.2 us  [local(): shift = lambda array: lax.ppermute(array, 'seq', upward)]
    pallas_call x0 -> x6, Pallas kernels: none -> 28 us  [pick_columns(): pl.pallas_call(pick_kernel, grid_spec=pltpu.PrefetchScalarGridSpec(num_sc...]
    reshape x12 -> x10, local copies, waits for them, and re-layouts: 23.2 us -> 7.99 us  [step(): lax.dynamic_index_in_dim(split, mine, 1, keepdims=False)]
    convert_element_type x3 -> x0, local copies, waits for them, and re-layouts: 15.2 us -> none  [the longest x2 10 us: local(): hat, _ = moments(flat(halo).astype(jnp.float32))]
    convert_element_type x4 -> x2, other arithmetic: 18.6 us -> 5.81 us  [local(): piece = (hat * first_gain + first_shift).astype(jnp.bfloat16)]
  transfers between devices with their start and end apart: 32 -> 32, of which waited for: 20 -> 14; matrix products, arithmetic and copies ran while one was open for 52% -> 39% of each run, Pallas kernels for 3% -> 8%
where the time goes in v4:
time: 780 us; the launch traced here: 769 us
  waiting for transfers between devices  187 us (24%)
  matrix products  184 us (24%)
  starting transfers between devices  124 us (16%)
  other arithmetic  117 us (15%)
  Pallas kernels  103 us (13%)
  local copies, waits for them, and re-layouts  38.5 us (5%)
  between operations  15.9 us (2%)
    ppermute x24, starting transfers between devices, exchange(): lax.ppermute(array, axis, [(i, i ^ 1 << bit) for i in range(lax.axis_size...  108 us
    ppermute x24, waiting for transfers between devices, exchange(): lax.ppermute(array, axis, [(i, i ^ 1 << bit) for i in range(lax.axis_size...  98.2 us
    ppermute x3, waiting for transfers between devices, local(): shift = lambda array: lax.ppermute(array, 'seq', upward)  87.2 us
    dot_general x10, matrix products, dot_nt(): lax.dot_general(a, b, (((1,), (1,)), ((), ())), preferred_element_type=jn...  67.6 us
    dot_general x20, matrix products, dot_tn(): lax.dot_general(a, b, (((0,), (0,)), ((), ())), preferred_element_type=jn...  62.4 us
    dot_general x6, matrix products, dot_nn(): lax.dot_general(a, b, (((1,), (0,)), ((), ())), preferred_element_type=jn...  54 us
    pallas_call x1, Pallas kernels, attend_back(): pl.pallas_call(kernel, grid_spec=pltpu.PrefetchScalarGridSpec(num_scalar_...  44.4 us
    pallas_call x1, Pallas kernels, attend(): pl.pallas_call(kernel, grid_spec=pltpu.PrefetchScalarGridSpec(num_scalar_...  30.2 us
  transfers between devices with their start and end apart: 32, of which 14 were waited for; matrix products, arithmetic and copies ran while one was open for 39% of the time, Pallas kernels for 8%

profile of v4, /device:TPU:0, one launch (start us, length us, event | category | flops | bytes accessed | tf_op | source)
XLA Modules:
  0.0 769.1 jit_solution(14912967175067426283)
XLA Ops:
  21.6 34.1 %collective-permute-done = bf16[2,288,1024]{2,1,0:T(8,128)(2,1)S(1)} collective-permute-done((bf16[2,288,1024]{2,1,0:T(8,128)(2,1)}, bf16[2,288,1024]{2,1,0:T(8,128)(2,1)S(1)}, u32[]{:S(2)}, u32[]{:S(2)}) %collective-permute-start) | collective-permute-done | bytes 1179680 | tf_op jit(solution)/shard_map/ppermute | solution.py:391
  65.5 32.4 %collective-permute-done.1 = bf16[2,224,1024]{2,1,0:T(8,128)(2,1)} collective-permute-done((bf16[2,224,1024]{2,1,0:T(8,128)(2,1)}, bf16[2,224,1024]{2,1,0:T(8,128)(2,1)}, u32[]{:S(2)}, u32[]{:S(2)}) %collective-permute-start.1) | collective-permute-done | bytes 917536 | tf_op jit(solution)/shard_map/ppermute | solution.py:391
  105.4 20.7 %collective-permute-done.2 = bf16[2,288,1024]{2,1,0:T(8,128)(2,1)S(1)} collective-permute-done((bf16[2,288,1024]{2,1,0:T(8,128)(2,1)S(1)}, bf16[2,288,1024]{2,1,0:T(8,128)(2,1)S(1)}, u32[]{:S(2)}, u32[]{:S(2)}) %collective-permute-start.2) | collective-permute-done | bytes 1179680 | tf_op jit(solution)/shard_map/ppermute | solution.py:391
  131.1 9.8 %fusion.70 = f32[1024,3072]{1,0:T(8,128)S(1)} fusion(bf16[1024,1024]{1,0:T(8,128)(2,1)} %get-tuple-element.532.array_ref, bf16[1024,3072]{1,0:T(8,128)(2,1)} %all-gather.4.cloned.1.call-done), kind=kOutput, calls=%fused_computation.218 | convolution fusion | flops 6442450944 | bytes 20971520 | tf_op jit(solution)/shard_map/dot_general | solution.py:19
  159.3 30.2 %attend.1 = (bf16[2,512,1024]{2,1,0:T(8,128)(2,1)}, f32[2,4,4,512]{3,2,1,0:T(4,128)}) custom-call(s32[2,2]{1,0:T(2,128)} %slice.150.first_ref, f32[16]{0:T(128)} %scale_ref.3, bf16[2,512,1024]{2,1,0:T(8,128)(2,1)} %bitcast.239, bf16[2,512,1024]{2,1,0:T(8,128)(2,1)} %bitcast.243, bf16[2,512,1024]{2,1,0:T(8,128)(2,1)} %bitcast.245, ...), custom_call_target="tpu_custom_call" | custom-call | tf_op jit(solution)/shard_map/attend/pallas_call | solution.py:133
  202.8 15.7 %fusion.62 = (f32[1024]{0:T(1024)S(1)}, f32[1024,4096]{1,0:T(8,128)}, f32[1024,4096]{1,0:T(8,128)}) fusion(f32[4096]{0:T(1024)S(1)} %copy-done.86, bf16[1024,1024]{1,0:T(8,128)(2,1)S(1)} %add_convert_fusion.9.array_ref, bf16[1024,5120]{1,0:T(8,128)(2,1)S(1)} %bitcast.310), kind=kOutput, calls=%fused_computation.211 | convolution fusion | flops 8615099392 | bytes 44060672 | tf_op jit(solution)/shard_map/dot_general | solution.py:19
  218.5 7.6 multiply_reduce_fusion.2
  226.1 10.2 %add_convert_fusion.array_ref = bf16[1024,4096]{1,0:T(8,128)(2,1)} fusion(f32[1024,4096]{1,0:T(8,128)} %get-tuple-element.472, f32[4096]{0:T(1024)S(1)} %copy-done.84, f32[4096]{0:T(1024)S(1)} %copy-done.62, f32[1024]{0:T(1024)S(1)} %add_rsqrt_fusion, f32[1024]{0:T(1024)S(1)} %broadcast_multiply_fusion.2), kind=kLoop, calls=%fused_computation.10 | loop fusion | flops 20971520 | bytes 25206784 | tf_op jit(solution)/shard_map/convert_element_type | solution.py:442
  236.2 7.8 %pick.7 = (bf16[1024,2048]{1,0:T(8,128)(2,1)}, bf16[1024,2048]{1,0:T(8,128)(2,1)}) custom-call(s32[1]{0:T(128)} %bitcast.11.mine_ref, bf16[1024,4096]{1,0:T(8,128)(2,1)} %add_convert_fusion.array_ref), custom_call_target="tpu_custom_call" | custom-call | tf_op jit(solution)/shard_map/pick/pallas_call | solution.py:303
  244.0 8.4 %convolution_convert_fusion.1 = bf16[2048,1024]{1,0:T(8,128)(2,1)} fusion(bf16[1024,2048]{1,0:T(8,128)(2,1)} %get-tuple-element.240, bf16[1024,1024]{1,0:T(8,128)(2,1)S(1)} %bitcast.260), kind=kOutput, calls=%fused_computation.87 | convolution fusion | flops 4297064448 | bytes 10485760 | tf_op jit(solution)/shard_map/dot_general | solution.py:27
  256.7 9.2 %fusion.71 = f32[2048,1024]{1,0:T(8,128)} fusion(bf16[1024,2048]{1,0:T(8,128)(2,1)} %get-tuple-element.244, bf16[1024,1024]{1,0:T(8,128)(2,1)S(1)} %bitcast.261), kind=kOutput, calls=%fused_computation.219 | convolution fusion | flops 4294967296 | bytes 14680064 | tf_op jit(solution)/shard_map/dot_general | solution.py:27
  275.8 21.8 %multiply_reduce_fusion = (f32[4096]{0:T(1024)}, f32[1024]{0:T(1024)S(1)}, f32[1024]{0:T(1024)S(1)}, f32[4096]{0:T(1024)}, f32[1024,4096]{1,0:T(8,128)}) fusion(f32[1024,4096]{1,0:T(8,128)} %get-tuple-element.472, f32[1024]{0:T(1024)S(1)} %add_rsqrt_fusion, f32[1024]{0:T(1024)S(1)} %broadcast_multiply_fusion.2, f32[4096]{0:T(1024)S(1)} %copy-done.62, ...), kind=kOutput, calls=%fused_computation.7 | convolution fusion | flops 8627673088 | bytes 44105728 | tf_op jit(solution)/shard_map/dot_general | solution.py:23
  297.6 17.2 %fusion.5 = bf16[1024,4096]{1,0:T(8,128)(2,1)S(1)} fusion(f32[1024,4096]{1,0:T(8,128)} %get-tuple-element.541, f32[1024,4096]{1,0:T(8,128)} %get-tuple-element.540, f32[1024,4096]{1,0:T(8,128)} %get-tuple-element.472, f32[1024]{0:T(1024)S(1)} %get-tuple-element.545, f32[1024]{0:T(1024)S(1)} %get-tuple-element.546, f32[4096]{0:T(1024)S(1)} %copy-done.62, ...), kind=kLoop, calls=%fused_computation.6 | loop fusion | flops 75497472 | bytes 58769408 | tf_op jit(solution)/shard_map/convert_element_type | solution.py:461
  314.8 7.2 collective-permute-done.4
  351.4 11.7 %fusion.72 = f32[512,4096]{1,0:T(8,128)} fusion(bf16[1024,512]{1,0:T(8,128)(2,1)} %get-tuple-element.263, bf16[1024,4096]{1,0:T(8,128)(2,1)} %copy-done.2), kind=kOutput, calls=%fused_computation.220 | convolution fusion | flops 4294967296 | bytes 17825792 | tf_op jit(solution)/shard_map/dot_general | solution.py:27
  363.1 8.2 %add_convert_fusion.1 = bf16[512,4096]{1,0:T(8,128)(2,1)} fusion(f32[512,4096]{1,0:T(8,128)} %fusion.72, bf16[512,4096]{1,0:T(8,128)(2,1)} %collective-permute-done.5), kind=kLoop, calls=%fused_computation.16 | loop fusion | flops 6291456 | bytes 16777216 | tf_op jit(solution)/shard_map/convert_element_type | solution.py:344
  376.4 14.5 %multiply_reduce_fusion.5 = (f32[1024]{0:T(1024)}, f32[1024]{0:T(1024)S(1)}, f32[1024]{0:T(1024)S(1)}, f32[1024]{0:T(1024)}, f32[1024,1024]{1,0:T(8,128)}) fusion(f32[1024,1024]{1,0:T(8,128)S(1)} %copy-done.4, f32[1024]{0:T(1024)S(1)} %add_rsqrt_fusion.1, f32[1024]{0:T(1024)S(1)} %broadcast_multiply_fusion.9, f32[1024]{0:T(1024)S(1)} %copy-done.71, ...), kind=kOutput, calls=%fused_computation.69 | convolution fusion | flops 8599367680 | bytes 25194496 | tf_op jit(solution)/shard_map/dot_general | solution.py:23
  407.7 44.4 %attend_back.1 = (bf16[2,512,1024]{2,1,0:T(8,128)(2,1)}, bf16[2,512,1024]{2,1,0:T(8,128)(2,1)}, bf16[2,512,1024]{2,1,0:T(8,128)(2,1)}, bf16[2,288,1024]{2,1,0:T(...) custom-call(s32[2,2]{1,0:T(2,128)} %slice.150.first_ref, ...), custom_call_target="tpu_custom_call" | custom-call | tf_op jit(solution)/shard_map/attend_back/pallas_call | solution.py:229
  462.8 85.8 %collective-permute-start.8 = (bf16[256,1024]{1,0:T(8,128)(2,1)}, bf16[256,1024]{1,0:T(8,128)(2,1)}, u32[]{:S(2)}, u32[]{:S(2)}) collective-permute-start(bf16[256,1024]{1,0:T(8,128)(2,1)} %bitcast.23), channel_id=1, source_target_pairs={{0,1},{1,0},{2,3},{3,2},{4,5},{5,4},{6,7},{7,6},{8,9},{9,8},{10,11... | collective-permute-start | bytes 1572872 | tf_op jit(solution)/shard_map/ppermute | solution.py:274
  570.1 14.1 %collective-permute-done.6 = bf16[256,4096]{1,0:T(8,128)(2,1)} collective-permute-done((bf16[256,4096]{1,0:T(8,128)(2,1)}, bf16[256,4096]{1,0:T(8,128)(2,1)}, u32[]{:S(2)}, u32[]{:S(2)}) %collective-permute-start.6) | collective-permute-done | bytes 2097184 | tf_op jit(solution)/shard_map/ppermute | solution.py:274
  638.2 13.7 %collective-permute-done.14 = bf16[256,2048]{1,0:T(8,128)(2,1)S(1)} collective-permute-done((bf16[256,2048]{1,0:T(8,128)(2,1)S(1)}, bf16[256,2048]{1,0:T(8,128)(2,1)S(1)}, u32[]{:S(2)}, u32[]{:S(2)}) %collective-permute-start.14) | collective-permute-done | bytes 1048608 | tf_op jit(solution)/shard_map/ppermute | solution.py:274
  663.7 14.9 %add_convert_fusion.3 = bf16[1024,1024]{1,0:T(8,128)(2,1)} fusion(f32[1024,1024]{1,0:T(8,128)S(1)} %copy-done.5, f32[1024]{0:T(1024)S(1)} %copy-done.99, bf16[1024,4096]{1,0:T(8,128)(2,1)} %add_convert_fusion.array_ref, bf16[4096,1024]{1,0:T(8,128)(2,1)} %all-gather.8.cloned.1.call-done), kind=kOutput, calls=%fused_computation.59 | convolution fusion | flops 8593080320 | bytes 23072768 | tf_op jit(solution)/shard_map/dot_general | solution.py:19
  686.4 32.4 %collective-permute-done.22 = bf16[64,4096]{1,0:T(8,128)(2,1)S(1)} collective-permute-done((bf16[64,4096]{1,0:T(8,128)(2,1)S(1)}, bf16[64,4096]{1,0:T(8,128)(2,1)S(1)}, u32[]{:S(2)}, u32[]{:S(2)}) %collective-permute-start.22) | collective-permute-done | bytes 524320 | tf_op jit(solution)/shard_map/ppermute | solution.py:274
  732.7 7.0 collective-permute-done.23
  (438 shorter events, 274.4 us)
Async XLA Ops:
  7.2 123.9 %all-gather.4.cloned.1.call-start = ((), (), s32[]{:S(2)}) async-start(), calls=%async_computation | async-start | bytes 6488064 | tf_op jit(solution)/shard_map/all_gather | solution.py:403
  9.0 181.6 %all-gather.6.cloned.1.call-start = ((), (), s32[]{:S(2)}) async-start(), calls=%async_computation.1 | async-start | bytes 10813440 | tf_op jit(solution)/shard_map/all_gather | solution.py:404
  10.8 265.0 %all-gather.8.cloned.1.call-start = ((), (), s32[]{:S(2)}) async-start(), calls=%async_computation.2 | async-start | bytes 8650752 | tf_op jit(solution)/shard_map/all_gather | solution.py:405
  13.2 42.5 %collective-permute-start = (bf16[2,288,1024]{2,1,0:T(8,128)(2,1)}, bf16[2,288,1024]{2,1,0:T(8,128)(2,1)S(1)}, u32[]{:S(2)}, u32[]{:S(2)}) collective-permute-start(bf16[2,288,1024]{2,1,0:T(8,128)(2,1)} %slice.154), channel_id=1, source_target_pairs={{0,1},{1,2},{2,3},{4,5},{5,6},{6,7},{8,9},{9,10},{10,11},{12,13},{... | collective-permute-start | bytes 3538952 | tf_op jit(solution)/shard_map/ppermute | solution.py:391
  55.7 42.2 %collective-permute-start.1 = (bf16[2,224,1024]{2,1,0:T(8,128)(2,1)}, bf16[2,224,1024]{2,1,0:T(8,128)(2,1)}, u32[]{:S(2)}, u32[]{:S(2)}) collective-permute-start(bf16[2,224,1024]{2,1,0:T(8,128)(2,1)} %slice.153), channel_id=1, source_target_pairs={{0,1},{1,2},{2,3},{4,5},{5,6},{6,7},{8,9},{9,10},{10,11},{12,13},{... | collective-permute-start | bytes 2752520 | tf_op jit(solution)/shard_map/ppermute | solution.py:391
  62.0 64.1 %collective-permute-start.2 = (bf16[2,288,1024]{2,1,0:T(8,128)(2,1)S(1)}, bf16[2,288,1024]{2,1,0:T(8,128)(2,1)S(1)}, u32[]{:S(2)}, u32[]{:S(2)}) collective-permute-start(bf16[2,288,1024]{2,1,0:T(8,128)(2,1)S(1)} %collective-permute-done), channel_id=1, source_target_pairs={{0,1},{1,2},{2,3},{4,5},{5,6},{6,7},{8,9},{9,10},{10,11},{12,13},{... | collective-permute-start | bytes 3538952 | tf_op jit(solution)/shard_map/ppermute | solution.py:391
  274.2 47.8 %collective-permute-start.4 = (bf16[1024,1024]{1,0:T(8,128)(2,1)}, bf16[1024,1024]{1,0:T(8,128)(2,1)}, u32[]{:S(2)}, u32[]{:S(2)}) collective-permute-start(bf16[1024,1024]{1,0:T(8,128)(2,1)} %get-tuple-element.253), channel_id=1, source_target_pairs={{0,16},{4,20},{8,24},{12,28},{16,0},{20,4},{24,8},{28,12},{1,17},{... | collective-permute-start | bytes 6291464 | tf_op jit(solution)/shard_map/ppermute | solution.py:274
  332.4 30.7 %collective-permute-start.5 = (bf16[512,4096]{1,0:T(8,128)(2,1)}, bf16[512,4096]{1,0:T(8,128)(2,1)}, u32[]{:S(2)}, u32[]{:S(2)}) collective-permute-start(bf16[512,4096]{1,0:T(8,128)(2,1)} %convolution_convert_fusion), channel_id=1, source_target_pairs={{0,4},{4,0},{8,12},{12,8},{16,20},{20,16},{24,28},{28,24},{1,5},{5... | collective-permute-start | bytes 12582920 | tf_op jit(solution)/shard_map/ppermute | solution.py:274
  349.7 49.8 %collective-permute-start.7 = (bf16[512,1024]{1,0:T(8,128)(2,1)}, bf16[512,1024]{1,0:T(8,128)(2,1)}, u32[]{:S(2)}, u32[]{:S(2)}) collective-permute-start(bf16[512,1024]{1,0:T(8,128)(2,1)} %get-tuple-element.271), channel_id=1, source_target_pairs={{0,8},{4,12},{8,0},{12,4},{16,24},{20,28},{24,16},{28,20},{1,9},{5... | collective-permute-start | bytes 3145736 | tf_op jit(solution)/shard_map/ppermute | solution.py:274
  462.8 103.1 %collective-permute-start.8 = (bf16[256,1024]{1,0:T(8,128)(2,1)}, bf16[256,1024]{1,0:T(8,128)(2,1)}, u32[]{:S(2)}, u32[]{:S(2)}) collective-permute-start(bf16[256,1024]{1,0:T(8,128)(2,1)} %bitcast.23), channel_id=1, source_target_pairs={{0,1},{1,0},{2,3},{3,2},{4,5},{5,4},{6,7},{7,6},{8,9},{9,8},{10,11... | collective-permute-start | bytes 1572872 | tf_op jit(solution)/shard_map/ppermute | solution.py:274
  548.6 35.6 %collective-permute-start.6 = (bf16[256,4096]{1,0:T(8,128)(2,1)}, bf16[256,4096]{1,0:T(8,128)(2,1)}, u32[]{:S(2)}, u32[]{:S(2)}) collective-permute-start(bf16[256,4096]{1,0:T(8,128)(2,1)} %bitcast.20), channel_id=1, source_target_pairs={{0,8},{4,12},{8,0},{12,4},{16,24},{20,28},{24,16},{28,20},{1,9},{5... | collective-permute-start | bytes 6291464 | tf_op jit(solution)/shard_map/ppermute | solution.py:274
  549.1 72.3 %collective-permute-start.11 = (bf16[2,288,1024]{2,1,0:T(8,128)(2,1)}, bf16[2,288,1024]{2,1,0:T(8,128)(2,1)}, u32[]{:S(2)}, u32[]{:S(2)}) collective-permute-start(bf16[2,288,1024]{2,1,0:T(8,128)(2,1)} %bitcast.28), channel_id=1, source_target_pairs={{1,0},{2,1},{3,2},{5,4},{6,5},{7,6},{9,8},{10,9},{11,10},{13,12},{... | collective-permute-start | bytes 3538952 | tf_op jit(solution)/shard_map/ppermute | solution.py:489
  567.9 56.8 %collective-permute-start.10 = (bf16[128,1024]{1,0:T(8,128)(2,1)}, bf16[128,1024]{1,0:T(8,128)(2,1)}, u32[]{:S(2)}, u32[]{:S(2)}) collective-permute-start(bf16[128,1024]{1,0:T(8,128)(2,1)} %get-tuple-element.323), channel_id=1, source_target_pairs={{0,2},{1,3},{2,0},{3,1},{4,6},{5,7},{6,4},{7,5},{8,10},{9,11},{10,... | collective-permute-start | bytes 786440 | tf_op jit(solution)/shard_map/ppermute | solution.py:274
  597.0 19.6 %collective-permute-start.12 = (bf16[512,4096]{1,0:T(8,128)(2,1)S(1)}, bf16[512,4096]{1,0:T(8,128)(2,1)}, u32[]{:S(2)}, u32[]{:S(2)}) collective-permute-start(bf16[512,4096]{1,0:T(8,128)(2,1)S(1)} %pad_maximum_fusion), channel_id=1, source_target_pairs={{0,4},{4,0},{8,12},{12,8},{16,20},{20,16},{24,28},{28,24},{1,5},{5... | collective-permute-start | bytes 12582920 | tf_op jit(solution)/shard_map/ppermute | solution.py:274
  597.1 63.5 %collective-permute-start.9 = (bf16[128,4096]{1,0:T(8,128)(2,1)}, bf16[128,4096]{1,0:T(8,128)(2,1)}, u32[]{:S(2)}, u32[]{:S(2)}) collective-permute-start(bf16[128,4096]{1,0:T(8,128)(2,1)} %get-tuple-element.301), channel_id=1, source_target_pairs={{0,16},{4,20},{8,24},{12,28},{16,0},{20,4},{24,8},{28,12},{1,17},{... | collective-permute-start | bytes 3145736 | tf_op jit(solution)/shard_map/ppermute | solution.py:274
  626.9 25.1 %collective-permute-start.14 = (bf16[256,2048]{1,0:T(8,128)(2,1)S(1)}, bf16[256,2048]{1,0:T(8,128)(2,1)S(1)}, u32[]{:S(2)}, u32[]{:S(2)}) collective-permute-start(bf16[256,2048]{1,0:T(8,128)(2,1)S(1)} %get-tuple-element.358), channel_id=1, source_target_pairs={{0,16},{4,20},{8,24},{12,28},{16,0},{20,4},{24,8},{28,12},{1,17},{... | collective-permute-start | bytes 3145736 | tf_op jit(solution)/shard_map/ppermute | solution.py:274
  628.5 25.0 %collective-permute-start.13 = (bf16[256,2048]{1,0:T(8,128)(2,1)S(1)}, bf16[256,2048]{1,0:T(8,128)(2,1)S(1)}, u32[]{:S(2)}, u32[]{:S(2)}) collective-permute-start(bf16[256,2048]{1,0:T(8,128)(2,1)S(1)} %bitcast.289), channel_id=1, source_target_pairs={{0,8},{4,12},{8,0},{12,4},{16,24},{20,28},{24,16},{28,20},{1,9},{5... | collective-permute-start | bytes 3145736 | tf_op jit(solution)/shard_map/ppermute | solution.py:274
  656.6 75.9 %collective-permute-start.16 = (bf16[2,512,1024]{2,1,0:T(8,128)(2,1)}, bf16[2,512,1024]{2,1,0:T(8,128)(2,1)S(1)}, u32[]{:S(2)}, u32[]{:S(2)}) collective-permute-start(bf16[2,512,1024]{2,1,0:T(8,128)(2,1)} %add_convert_fusion.4), channel_id=1, source_target_pairs={{1,0},{2,1},{3,2},{5,4},{6,5},{7,6},{9,8},{10,9},{11,10},{13,12},{... | collective-permute-start | bytes 6291464 | tf_op jit(solution)/shard_map/ppermute | solution.py:489
  658.2 23.1 %collective-permute-start.19 = (bf16[128,2048]{1,0:T(8,128)(2,1)}, bf16[128,2048]{1,0:T(8,128)(2,1)S(1)}, u32[]{:S(2)}, u32[]{:S(2)}) collective-permute-start(bf16[128,2048]{1,0:T(8,128)(2,1)} %get-tuple-element.386), channel_id=1, source_target_pairs={{0,8},{4,12},{8,0},{12,4},{16,24},{20,28},{24,16},{28,20},{1,9},{5... | collective-permute-start | bytes 1572872 | tf_op jit(solution)/shard_map/ppermute | solution.py:274
  660.0 21.5 %collective-permute-start.18 = (bf16[128,2048]{1,0:T(8,128)(2,1)}, bf16[128,2048]{1,0:T(8,128)(2,1)S(1)}, u32[]{:S(2)}, u32[]{:S(2)}) collective-permute-start(bf16[128,2048]{1,0:T(8,128)(2,1)} %get-tuple-element.384), channel_id=1, source_target_pairs={{0,16},{4,20},{8,24},{12,28},{16,0},{20,4},{24,8},{28,12},{1,17},{... | collective-permute-start | bytes 1572872 | tf_op jit(solution)/shard_map/ppermute | solution.py:274
  662.2 19.1 %collective-permute-start.17 = (f32[22544]{0:T(1024)S(1)}, f32[22544]{0:T(1024)S(1)}, u32[]{:S(2)}, u32[]{:S(2)}) collective-permute-start(f32[22544]{0:T(1024)S(1)} %add.459), channel_id=1, source_target_pairs={{0,8},{4,12},{8,0},{12,4},{16,24},{20,28},{24,16},{28,20},{1,9},{5... | collective-permute-start | bytes 270536 | tf_op jit(solution)/shard_map/ppermute | solution.py:274
  678.6 40.1 %collective-permute-start.22 = (bf16[64,4096]{1,0:T(8,128)(2,1)S(1)}, bf16[64,4096]{1,0:T(8,128)(2,1)S(1)}, u32[]{:S(2)}, u32[]{:S(2)}) collective-permute-start(bf16[64,4096]{1,0:T(8,128)(2,1)S(1)} %bitcast.294), channel_id=1, source_target_pairs={{0,1},{1,0},{2,3},{3,2},{4,5},{5,4},{6,7},{7,6},{8,9},{9,8},{10,11... | collective-permute-start | bytes 1572872 | tf_op jit(solution)/shard_map/ppermute | solution.py:274
  682.1 50.4 %collective-permute-start.24 = (bf16[64,2048]{1,0:T(8,128)(2,1)S(1)}, bf16[64,2048]{1,0:T(8,128)(2,1)S(1)}, u32[]{:S(2)}, u32[]{:S(2)}) collective-permute-start(bf16[64,2048]{1,0:T(8,128)(2,1)S(1)} %bitcast.295), channel_id=1, source_target_pairs={{0,1},{1,0},{2,3},{3,2},{4,5},{5,4},{6,7},{7,6},{8,9},{9,8},{10,11... | collective-permute-start | bytes 786440 | tf_op jit(solution)/shard_map/ppermute | solution.py:274
  725.8 18.9 %collective-permute-start.26 = (bf16[32,4096]{1,0:T(8,128)(2,1)S(1)}, bf16[32,4096]{1,0:T(8,128)(2,1)S(1)}, u32[]{:S(2)}, u32[]{:S(2)}) collective-permute-start(bf16[32,4096]{1,0:T(8,128)(2,1)S(1)} %get-tuple-element.426), channel_id=1, source_target_pairs={{0,2},{1,3},{2,0},{3,1},{4,6},{5,7},{6,4},{7,5},{8,10},{9,11},{10,... | collective-permute-start | bytes 786440 | tf_op jit(solution)/shard_map/ppermute | solution.py:274
  (117 other events, 1503.2 us)
Sparse Core Ops, SparseCore 0:
  11.5 85.4 all-gather.3
  100.3 90.2 all-gather.5
  193.6 75.5 all-gather.7

commit v5 on v4

--- a/solution.py
+++ b/solution.py
@@ -118,6 +118,15 @@
             lanes = slice(head * width, (head + 1) * width)
             acc_ref[lanes] = acc_ref[lanes] * (scale_ref[group * heads + head] / total[head : head + 1])
         out_ref[0, first_query : first_query + BLOCK, :] = acc_ref[...].T.astype(jnp.bfloat16)
+
+
+def attention_cost(sequences, rows, counts, head_count, model, products):
+    pairs = sequences * head_count * rows * sum(counts)
+    return pl.CostEstimate(
+        flops=2 * products * pairs * LANES,
+        bytes_accessed=4 * products * sequences * sum(counts) * model,
+        transcendentals=pairs,
+    )
 
 
 def attend(first, head_scale, query, keys, values, start, hops):
@@ -150,6 +159,7 @@
             jax.ShapeDtypeStruct((sequences, groups, heads, rows), jnp.float32),
         ],
         name="attend",
+        cost_estimate=attention_cost(sequences, rows, counts, head_count, model, 3),
     )(first, head_scale, query, *keys, *values, start)
 
 
@@ -252,6 +262,7 @@
         ),
         out_shape=[shape(rows)] + [shape(c) for c in counts] * 2,
         name="attend_back",
+        cost_estimate=attention_cost(sequences, rows, counts, head_count, model, 5),
     )(first, head_scale, query, *keys, *values, start, lse, scaled, grad)
     return results[0], results[1 : 1 + pieces], results[1 + pieces :]
 
@@ -310,6 +321,7 @@
         ),
         out_shape=[half, half],
         name="pick",
+        cost_estimate=pl.CostEstimate(flops=0, bytes_accessed=4 * array.size * array.dtype.itemsize, transcendentals=0),
     )(mine.reshape(1), array)
 
 
@@ -333,8 +345,11 @@
         self.came = came
 
     def step(self, sequence):
-        came, self.kept = sequence(self.came, self.kept)
-        total = self.kept.astype(jnp.float32) + came.astype(jnp.float32)
+        if callable(self.kept):
+            came, kept = sequence(self.came), self.kept()
+        else:
+            came, kept = sequence(self.came, self.kept)
+        total = kept.astype(jnp.float32) + came.astype(jnp.float32)
         if not self.order:
             self.total = sequence(total)
             return
@@ -419,8 +434,10 @@
     query = stacked((projected[:, :model] + query_bias).astype(jnp.bfloat16))
     keys = [stacked(projected[:, model : 2 * model].astype(jnp.bfloat16))]
     values = [stacked((projected[:, 2 * model :] + value_bias).astype(jnp.bfloat16))]
-    normed_pieces, hats = [normed], [hat_one]
+    core, *planes = bits_of("dp")
+    normed_pieces, hats, picked = [normed], [hat_one], [pick_columns(normed, core)]
     for halo in halos:
+        halo, query, keys[-1], values[-1], picked[-1] = together(halo, query, keys[-1], values[-1], picked[-1])
         hat, _ = moments(flat(halo).astype(jnp.float32))
         piece = (hat * first_gain + first_shift).astype(jnp.bfloat16)
         normed_pieces.append(piece)
@@ -428,6 +445,7 @@
         both = dot_nn(piece, inward[:, model:])
         keys.append(stacked(both[:, :model].astype(jnp.bfloat16)))
         values.append(stacked((both[:, model:] + value_bias).astype(jnp.bfloat16)))
+        picked.append(pick_columns(piece, core))
     scaled, lse = attend(first, head_scale, query, keys, values, start, hops)
 
     scaled_low = flat(scaled)
@@ -442,7 +460,6 @@
     mixed = (hat_middle * middle_gain + middle_shift).astype(jnp.bfloat16)
     grad_low = flat(cotangent)
     grad_out = grad_low.astype(jnp.float32)
-    core, *planes = bits_of("dp")
     one_way = [core, *reversed(planes), *bits_of("seq")]
     other_way = [core, *planes, *bits_of("seq")]
 
@@ -452,7 +469,7 @@
     other_mixed, own_mixed = pick_columns(mixed, core)
     sent, own_mixed, low = sequence(dot_tn(other_mixed, grad_low).astype(jnp.bfloat16), own_mixed, grad_low)
     down_sum.begin(exchange(sent, *core))
-    down_sum.kept = dot_tn(own_mixed, low)
+    down_sum.kept = lambda: dot_tn(own_mixed, sequence(low))
     down_sum.step(sequence)
 
     low = sequence(low)
@@ -461,14 +478,15 @@
     grad_upper = (norm_back(hat_middle, scale_middle, middle_gain, grad_mixed) * slope).astype(jnp.bfloat16)
     other_second, own_second = pick_columns(second, core)
     grad_upper = sequence(grad_upper)
-    down_sum.step(sequence)
-    sent = dot_tn(other_second, sequence(grad_upper)).astype(jnp.bfloat16)
+    sent = dot_tn(other_second, grad_upper).astype(jnp.bfloat16)
     sent, grad_upper = sequence(sent, grad_upper)
     up_sum.begin(exchange(sent, *core))
-    up_sum.kept = dot_tn(own_second, grad_upper)
+    down_sum.step(sequence)
+    up_sum.kept = lambda: dot_tn(own_second, sequence(grad_upper))
+    grad_upper = sequence(grad_upper)
+    grad_second = sequence(dot_nt(grad_upper, up_full))
     up_sum.step(sequence)
-    grad_upper = sequence(grad_upper)
-    grad_second = dot_nt(grad_upper, up_full)
+    grad_second = sequence(grad_second)
     grad_middle = grad_out + norm_back(hat_two, scale_two, second_gain, grad_second)
     grad_branch = norm_back(hat_post, scale_post, post_gain, grad_middle).astype(jnp.bfloat16)
     grad_branch = sequence(grad_branch)
@@ -483,8 +501,11 @@
     dquery, dkeys, dvalues = attend_back(
         first, head_scale, query, keys, values, start, lse, scaled, stacked(grad_attended), hops
     )
-    dkeys, dvalues = [flat(d) for d in dkeys], [flat(d) for d in dvalues]
-    query_low = sequence(flat(dquery))
+    query_low, *pairs = sequence(flat(dquery), *[flat(d) for d in dkeys], *[flat(d) for d in dvalues])
+    down_sum.step(sequence)
+    up_sum.step(sequence)
+    query_low, *pairs = sequence(query_low, *pairs)
+    dkeys, dvalues = pairs[: len(keys)], pairs[len(keys) :]
     back = lambda dkey, dvalue: dot_nt(dkey, inward[:, model : 2 * model]) + dot_nt(dvalue, inward[:, 2 * model :])
     lower = lambda array: lax.ppermute(array, "seq", downward)
     partials = [None] * len(hops)
@@ -492,12 +513,18 @@
     if hops:
         partials[-1] = back(dkeys[-1], dvalues[-1])
         carried = lower(sequence(stacked(partials[-1]).astype(jnp.bfloat16)))
-    down_sum.step(sequence)
-    up_sum.step(sequence)
-
-    picked = [pick_columns(piece, core) for piece in normed_pieces]
+    for hop in range(len(hops) - 1):
+        partials[hop] = back(*sequence(dkeys[hop + 1], dvalues[hop + 1]))
+    for hop in reversed(range(len(hops) - 1)):
+        carried, partial = sequence(carried, partials[hop])
+        partial = stacked(partial)
+        missing = partial.shape[1] - carried.shape[1]
+        going = partial + jnp.pad(carried.astype(jnp.float32), ((0, 0), (missing, 0), (0, 0)))
+        carried = lower(sequence(going.astype(jnp.bfloat16)))
+
     picked_scaled = pick_columns(scaled_low, core)
-    query_low, grad_branch, dkeys[0], dvalues[0] = sequence(query_low, grad_branch, dkeys[0], dvalues[0])
+    query_low, grad_branch, *pairs = sequence(query_low, grad_branch, *dkeys, *dvalues)
+    dkeys, dvalues = pairs[: len(dkeys)], pairs[len(dkeys) :]
 
     def four(side):
         return (
@@ -509,21 +536,13 @@
 
     sent = sequence(jnp.concatenate([part.astype(jnp.bfloat16) for part in four(0)], 1))
     came = exchange(sent, *core)
-    query_low, grad_branch, dkeys[0], dvalues[0] = sequence(query_low, grad_branch, dkeys[0], dvalues[0])
-    mine = four(1)
-    for hop in range(len(hops) - 1):
-        partials[hop] = back(*sequence(dkeys[hop + 1], dvalues[hop + 1]))
+    query_low, grad_branch, *pairs = sequence(query_low, grad_branch, *dkeys, *dvalues)
+    dkeys, dvalues = pairs[: len(dkeys)], pairs[len(dkeys) :]
     for index, row_sum in enumerate(sums):
         columns = slice(2 * index * model, 2 * (index + 1) * model)
         row_sum.begin(came[:, columns])
-        row_sum.kept = jnp.concatenate(mine[2 * index : 2 * (index + 1)], 1)
+        row_sum.kept = lambda index=index: jnp.concatenate(four(1)[2 * index : 2 * (index + 1)], 1)
         row_sum.step(sequence)
-    for hop in reversed(range(len(hops) - 1)):
-        carried, partial = sequence(carried, partials[hop])
-        partial = stacked(partial)
-        missing = partial.shape[1] - carried.shape[1]
-        going = partial + jnp.pad(carried.astype(jnp.float32), ((0, 0), (missing, 0), (0, 0)))
-        carried = lower(sequence(going.astype(jnp.bfloat16)))
     down_sum.step(sequence)
 
     query_low, dkeys[0], dvalues[0] = sequence(query_low, dkeys[0], dvalues[0])
@@ -533,7 +552,13 @@
         + dot_nt(dvalues[0], inward[:, 2 * model :])
     )
     own = sequence(own)
+    grad_normed = own
     for row_sum in sums:
+        row_sum.step(sequence)
+    if hops:
+        carried, own = sequence(carried, own)
+        grad_normed = own + flat(jnp.pad(carried.astype(jnp.float32), ((0, 0), (rows - carried.shape[1], 0), (0, 0))))
+    for row_sum in (*sums, up_sum):
         row_sum.step(sequence)
     own = sequence(own)
     vector = jnp.concatenate(
@@ -561,23 +586,16 @@
             vector = sequence(vector + exchange(vector, *places.pop(0)))
         return vector
 
-    vector = sum_vector(sequence(vector), 1)
-    up_sum.step(sequence)
-    mixed, middle = sequence(mixed, middle)
-    layer_output = sequence((middle + dot_nn(mixed, down_full) + down_bias).astype(jnp.bfloat16))
-    for row_sum in sums:
+    vector = sequence(vector)
+    grad_normed, mixed, middle = sequence(grad_normed, mixed, middle)
+    input_grad = (grad_middle + norm_back(hat_one, scale_one, first_gain, grad_normed)).astype(jnp.bfloat16)
+    layer_output = (middle + dot_nn(mixed, down_full) + down_bias).astype(jnp.bfloat16)
+    input_grad, layer_output = sequence(input_grad, layer_output)
+    vector = sum_vector(vector, 1)
+    for row_sum in (*sums, up_sum):
         row_sum.step(sequence)
     vector = sum_vector(vector, 2)
     up_sum.step(sequence)
-    vector = sum_vector(vector, 1)
-    grad_normed = own
-    if hops:
-        carried, own = sequence(carried, own)
-        grad_normed = own + flat(jnp.pad(carried.astype(jnp.float32), ((0, 0), (rows - carried.shape[1], 0), (0, 0))))
-    input_grad = (grad_middle + norm_back(hat_one, scale_one, first_gain, grad_normed)).astype(jnp.bfloat16)
-    for row_sum in sums:
-        row_sum.step(sequence)
-    input_grad = sequence(input_grad)
     vector = sum_vector(vector, len(places))
     for row_sum in (up_sum, *sums, down_sum):
         while row_sum.total is None:

time: 780 us -> 740 us (0.949)
  starting transfers between devices: 124 us -> 80 us
  waiting for transfers between devices: 187 us -> 212 us
  matrix products: 184 us -> 164 us
    ppermute x2, waiting for transfers between devices: 0.01 us -> 50.2 us  [local(): lower = lambda array: lax.ppermute(array, 'seq', downward)]
    ppermute x24, starting transfers between devices: 108 us -> 60.6 us  [exchange(): lax.ppermute(array, axis, [(i, i ^ 1 << bit) for i in range(lax.axis_size...]
    ppermute x3, waiting for transfers between devices: 87.2 us -> 57.1 us  [local(): shift = lambda array: lax.ppermute(array, 'seq', upward)]
    all_gather x1, waiting for transfers between devices: 1.18 us -> 17.7 us  [local(): lax.all_gather(jnp.concatenate([output_weight, up_weight], 1), BOTH, axis...]
    dot_general x20, matrix products: 62.4 us -> 47.7 us  [dot_tn(): lax.dot_general(a, b, (((0,), (0,)), ((), ())), preferred_element_type=jn...]
    ppermute x24, waiting for transfers between devices: 98.2 us -> 87.1 us  [exchange(): lax.ppermute(array, axis, [(i, i ^ 1 << bit) for i in range(lax.axis_size...]
  transfers between devices with their start and end apart: 32 -> 32, of which waited for: 14 -> 19; matrix products, arithmetic and copies ran while one was open for 39% -> 32% of each run, Pallas kernels for 8% -> 14%
where the time goes in v5:
time: 740 us; the launch traced here: 730 us
  waiting for transfers between devices  212 us (29%)
  matrix products  164 us (22%)
  other arithmetic  118 us (16%)
  Pallas kernels  103 us (14%)
  starting transfers between devices  80 us (11%)
  local copies, waits for them, and re-layouts  36.4 us (5%)
  between operations  15.8 us (2%)
    ppermute x24, waiting for transfers between devices, exchange(): lax.ppermute(array, axis, [(i, i ^ 1 << bit) for i in range(lax.axis_size...  87.1 us
    ppermute x24, starting transfers between devices, exchange(): lax.ppermute(array, axis, [(i, i ^ 1 << bit) for i in range(lax.axis_size...  60.6 us
    dot_general x10, matrix products, dot_nt(): lax.dot_general(a, b, (((1,), (1,)), ((), ())), preferred_element_type=jn...  60.6 us
    ppermute x3, waiting for transfers between devices, local(): shift = lambda array: lax.ppermute(array, 'seq', upward)  57.1 us
    dot_general x6, matrix products, dot_nn(): lax.dot_general(a, b, (((1,), (0,)), ((), ())), preferred_element_type=jn...  56.2 us
    ppermute x2, waiting for transfers between devices, local(): lower = lambda array: lax.ppermute(array, 'seq', downward)  50.2 us
    dot_general x20, matrix products, dot_tn(): lax.dot_general(a, b, (((0,), (0,)), ((), ())), preferred_element_type=jn...  47.7 us
    pallas_call x1, Pallas kernels, attend_back(): pl.pallas_call(kernel, grid_spec=pltpu.PrefetchScalarGridSpec(num_scalar_...  44.5 us
  transfers between devices with their start and end apart: 32, of which 19 were waited for; matrix products, arithmetic and copies ran while one was open for 32% of the time, Pallas kernels for 14%

profile of v5, /device:TPU:0, one launch (start us, length us, event | category | flops | bytes accessed | tf_op | source)
XLA Modules:
  0.0 729.5 jit_solution(10922163724483365561)
XLA Ops:
  20.7 32.5 %collective-permute-done = bf16[2,288,1024]{2,1,0:T(8,128)(2,1)} collective-permute-done((bf16[2,288,1024]{2,1,0:T(8,128)(2,1)S(1)}, bf16[2,288,1024]{2,1,0:T(8,128)(2,1)}, u32[]{:S(2)}, u32[]{:S(2)}) %collective-permute-start) | collective-permute-done | bytes 1179680 | tf_op jit(solution)/shard_map/ppermute | solution.py:406
  71.7 24.7 %collective-permute-done.2 = bf16[2,224,1024]{2,1,0:T(8,128)(2,1)} collective-permute-done((bf16[2,224,1024]{2,1,0:T(8,128)(2,1)}, bf16[2,224,1024]{2,1,0:T(8,128)(2,1)}, u32[]{:S(2)}, u32[]{:S(2)}) %collective-permute-start.2) | collective-permute-done | bytes 917536 | tf_op jit(solution)/shard_map/ppermute | solution.py:406
  99.4 9.4 %fusion.70 = f32[1024,3072]{1,0:T(8,128)S(1)} fusion(bf16[1024,1024]{1,0:T(8,128)(2,1)} %fusion.24.array_ref, bf16[1024,3072]{1,0:T(8,128)(2,1)} %all-gather.4.cloned.1.call-done), kind=kOutput, calls=%fused_computation.217 | convolution fusion | flops 6442450944 | bytes 20971520 | tf_op jit(solution)/shard_map/dot_general | solution.py:19
  121.9 6.9 fusion.34
  141.3 30.2 %attend.1 = (bf16[2,512,1024]{2,1,0:T(8,128)(2,1)}, f32[2,4,4,512]{3,2,1,0:T(4,128)}) custom-call(s32[2,2]{1,0:T(2,128)} %slice.150.first_ref, f32[16]{0:T(128)} %scale_ref.3, bf16[2,512,1024]{2,1,0:T(8,128)(2,1)} %bitcast.263, bf16[2,512,1024]{2,1,0:T(8,128)(2,1)} %bitcast.251, bf16[2,512,1024]{2,1,0:T(8,128)(2,1)} %bitcast.253, ...), custom_call_target="tpu_custom_call" | custom-call | flops 33017561088 | bytes 32243712 | tf_op jit(solution)/shard_map/attend/pallas_call | solution.py:142
  171.5 17.7 %all-gather.6.cloned.1.call-done = bf16[1024,5120]{1,0:T(8,128)(2,1)} async-done(((bf16[32,5120]{1,0:T(8,128)(2,1)}), bf16[1024,5120]{1,0:T(8,128)(2,1)}) %all-gather.6.cloned.1.call-update) | async-done | bytes 10485776 | tf_op jit(solution)/shard_map/all_gather | solution.py:419
  201.3 15.7 %fusion.62 = (f32[1024]{0:T(1024)S(1)}, f32[1024,4096]{1,0:T(8,128)}, f32[1024,4096]{1,0:T(8,128)}) fusion(f32[4096]{0:T(1024)S(1)} %copy-done.81, bf16[1024,1024]{1,0:T(8,128)(2,1)S(1)} %add_convert_fusion.7.array_ref, bf16[1024,5120]{1,0:T(8,128)(2,1)S(1)} %bitcast.296), kind=kOutput, calls=%fused_computation.210 | convolution fusion | flops 8615099392 | bytes 44060672 | tf_op jit(solution)/shard_map/dot_general | solution.py:19
  217.0 7.6 %multiply_reduce_fusion.2 = f32[1024]{0:T(1024)S(1)} fusion(f32[1024,4096]{1,0:T(8,128)} %get-tuple-element.544, f32[1024]{0:T(1024)S(1)} %broadcast_multiply_fusion.2), kind=kLoop, calls=%fused_computation.11 | loop fusion | flops 12581888 | bytes 16785408 | tf_op jit(solution)/shard_map/reduce_sum | solution.py:33
  224.6 10.2 %add_convert_fusion.array_ref = bf16[1024,4096]{1,0:T(8,128)(2,1)} fusion(f32[1024,4096]{1,0:T(8,128)} %get-tuple-element.544, f32[4096]{0:T(1024)S(1)} %copy-done.80, f32[4096]{0:T(1024)S(1)} %copy-done.57, f32[1024]{0:T(1024)S(1)} %add_rsqrt_fusion, f32[1024]{0:T(1024)S(1)} %broadcast_multiply_fusion.2), kind=kLoop, calls=%fused_computation.10 | loop fusion | flops 20971520 | bytes 25206784 | tf_op jit(solution)/shard_map/convert_element_type | solution.py:460
  234.8 7.7 %pick.9 = (bf16[1024,2048]{1,0:T(8,128)(2,1)}, bf16[1024,2048]{1,0:T(8,128)(2,1)}) custom-call(s32[1]{0:T(128)} %bitcast.5.mine_ref, bf16[1024,4096]{1,0:T(8,128)(2,1)} %add_convert_fusion.array_ref), custom_call_target="tpu_custom_call" | custom-call | bytes 33554432 | tf_op jit(solution)/shard_map/pick/pallas_call | solution.py:314
  242.6 8.4 %convolution_convert_fusion.1 = bf16[2048,1024]{1,0:T(8,128)(2,1)} fusion(bf16[1024,2048]{1,0:T(8,128)(2,1)} %get-tuple-element.288, bf16[1024,1024]{1,0:T(8,128)(2,1)S(1)} %bitcast.232), kind=kOutput, calls=%fused_computation.86 | convolution fusion | flops 4297064448 | bytes 10485760 | tf_op jit(solution)/shard_map/dot_general | solution.py:27
  259.1 9.0 %fusion.71 = f32[2048,1024]{1,0:T(8,128)} fusion(bf16[1024,2048]{1,0:T(8,128)(2,1)} %get-tuple-element.291, bf16[1024,1024]{1,0:T(8,128)(2,1)S(1)} %bitcast.233), kind=kOutput, calls=%fused_computation.218 | convolution fusion | flops 4294967296 | bytes 14680064 | tf_op jit(solution)/shard_map/dot_general | solution.py:27
  276.1 21.7 %multiply_reduce_fusion = (f32[4096]{0:T(1024)}, f32[1024]{0:T(1024)S(1)}, f32[1024]{0:T(1024)S(1)}, f32[4096]{0:T(1024)}, f32[1024,4096]{1,0:T(8,128)}) fusion(f32[1024,4096]{1,0:T(8,128)} %get-tuple-element.544, f32[1024]{0:T(1024)S(1)} %add_rsqrt_fusion, f32[1024]{0:T(1024)S(1)} %broadcast_multiply_fusion.2, f32[4096]{0:T(1024)S(1)} %copy-done.57, ...), kind=kOutput, calls=%fused_computation.7 | convolution fusion | flops 8627673088 | bytes 44105728 | tf_op jit(solution)/shard_map/dot_general | solution.py:23
  297.9 17.3 %fusion.5 = bf16[1024,4096]{1,0:T(8,128)(2,1)S(1)} fusion(f32[1024,4096]{1,0:T(8,128)} %get-tuple-element.610, f32[1024,4096]{1,0:T(8,128)} %get-tuple-element.609, f32[1024,4096]{1,0:T(8,128)} %get-tuple-element.544, f32[1024]{0:T(1024)S(1)} %get-tuple-element.613, f32[1024]{0:T(1024)S(1)} %get-tuple-element.614, f32[4096]{0:T(1024)S(1)} %copy-done.57, ...), kind=kLoop, calls=%fused_computation.6 | loop fusion | flops 75497472 | bytes 58769408 | tf_op jit(solution)/shard_map/convert_element_type | solution.py:478
  333.8 29.8 %collective-permute-done.4 = bf16[1024,1024]{1,0:T(8,128)(2,1)} collective-permute-done((bf16[1024,1024]{1,0:T(8,128)(2,1)}, bf16[1024,1024]{1,0:T(8,128)(2,1)}, u32[]{:S(2)}, u32[]{:S(2)}) %collective-permute-start.4) | collective-permute-done | bytes 2097184 | tf_op jit(solution)/shard_map/ppermute | solution.py:285
  367.4 11.6 %fusion.6 = f32[1024,1024]{1,0:T(8,128)S(1)} fusion(bf16[1024,4096]{1,0:T(8,128)(2,1)S(1)} %copy-done.6, bf16[1024,5120]{1,0:T(8,128)(2,1)} %all-gather.6.cloned.1.call-done), kind=kOutput, calls=%fused_computation.19 | convolution fusion | flops 8589934592 | bytes 20971520 | tf_op jit(solution)/shard_map/dot_general | solution.py:23
  414.2 19.9 %collective-permute-start.8 = (bf16[256,1024]{1,0:T(8,128)(2,1)}, bf16[256,1024]{1,0:T(8,128)(2,1)S(1)}, u32[]{:S(2)}, u32[]{:S(2)}) collective-permute-start(bf16[256,1024]{1,0:T(8,128)(2,1)} %bitcast.23), channel_id=1, source_target_pairs={{0,1},{1,0},{2,3},{3,2},{4,5},{5,4},{6,7},{7,6},{8,9},{9,8},{10,11... | collective-permute-start | bytes 1572872 | tf_op jit(solution)/shard_map/ppermute | solution.py:285
  434.2 44.5 %attend_back.1 = (bf16[2,512,1024]{2,1,0:T(8,128)(2,1)}, bf16[2,512,1024]{2,1,0:T(8,128)(2,1)}, bf16[2,512,1024]{2,1,0:T(8,128)(2,1)}, bf16[2,288,1024]{2,1,0:T(...) custom-call(s32[2,2]{1,0:T(2,128)} %slice.150.first_ref, ...), custom_call_target="tpu_custom_call" | custom-call | flops 55029268480 | bytes 53739520 | tf_op jit(solution)/shard_map/attend_back/pallas_call | solution.py:239
  496.9 47.3 %collective-permute-done.9 = bf16[2,288,1024]{2,1,0:T(8,128)(2,1)S(1)} collective-permute-done((bf16[2,288,1024]{2,1,0:T(8,128)(2,1)S(1)}, bf16[2,288,1024]{2,1,0:T(8,128)(2,1)S(1)}, u32[]{:S(2)}, u32[]{:S(2)}) %collective-permute-start.9) | collective-permute-done | bytes 1179680 | tf_op jit(solution)/shard_map/ppermute | solution.py:510
  559.1 10.3 %collective-permute-start.12 = (bf16[512,4096]{1,0:T(8,128)(2,1)}, bf16[512,4096]{1,0:T(8,128)(2,1)}, u32[]{:S(2)}, u32[]{:S(2)}) collective-permute-start(bf16[512,4096]{1,0:T(8,128)(2,1)} %pad_maximum_fusion), channel_id=1, source_target_pairs={{0,4},{4,0},{8,12},{12,8},{16,20},{20,16},{24,28},{28,24},{1,5},{5... | collective-permute-start | bytes 12582920 | tf_op jit(solution)/shard_map/ppermute | solution.py:285
  609.9 9.8 %collective-permute-done.14 = bf16[256,2048]{1,0:T(8,128)(2,1)S(1)} collective-permute-done((bf16[256,2048]{1,0:T(8,128)(2,1)S(1)}, bf16[256,2048]{1,0:T(8,128)(2,1)S(1)}, u32[]{:S(2)}, u32[]{:S(2)}) %collective-permute-start.14) | collective-permute-done | bytes 1048608 | tf_op jit(solution)/shard_map/ppermute | solution.py:285
  652.0 14.7 %add_convert_fusion.3 = bf16[1024,1024]{1,0:T(8,128)(2,1)} fusion(f32[1024,1024]{1,0:T(8,128)S(1)} %copy-done.4, f32[1024]{0:T(1024)S(1)} %copy-done.90, bf16[1024,4096]{1,0:T(8,128)(2,1)} %add_convert_fusion.array_ref, bf16[4096,1024]{1,0:T(8,128)(2,1)} %all-gather.8.cloned.1.call-done), kind=kOutput, calls=%fused_computation.60 | convolution fusion | flops 8593080320 | bytes 23072768 | tf_op jit(solution)/shard_map/dot_general | solution.py:19
  678.5 10.2 %collective-permute-done.22 = bf16[64,4096]{1,0:T(8,128)(2,1)S(1)} collective-permute-done((bf16[64,4096]{1,0:T(8,128)(2,1)S(1)}, bf16[64,4096]{1,0:T(8,128)(2,1)S(1)}, u32[]{:S(2)}, u32[]{:S(2)}) %collective-permute-start.22) | collective-permute-done | bytes 524320 | tf_op jit(solution)/shard_map/ppermute | solution.py:285
  699.0 6.9 collective-permute-done.26
  (433 shorter events, 289.6 us)
Async XLA Ops:
  7.2 92.2 %all-gather.4.cloned.1.call-start = ((), (), s32[]{:S(2)}) async-start(), calls=%async_computation | async-start | bytes 6488064 | tf_op jit(solution)/shard_map/all_gather | solution.py:418
  9.0 180.1 %all-gather.6.cloned.1.call-start = ((), (), s32[]{:S(2)}) async-start(), calls=%async_computation.1 | async-start | bytes 10813440 | tf_op jit(solution)/shard_map/all_gather | solution.py:419
  10.8 265.3 %all-gather.8.cloned.1.call-start = ((), (), s32[]{:S(2)}) async-start(), calls=%async_computation.2 | async-start | bytes 8650752 | tf_op jit(solution)/shard_map/all_gather | solution.py:420
  12.2 40.9 %collective-permute-start = (bf16[2,288,1024]{2,1,0:T(8,128)(2,1)S(1)}, bf16[2,288,1024]{2,1,0:T(8,128)(2,1)}, u32[]{:S(2)}, u32[]{:S(2)}) collective-permute-start(bf16[2,288,1024]{2,1,0:T(8,128)(2,1)S(1)} %slice.152), channel_id=1, source_target_pairs={{0,1},{1,2},{2,3},{4,5},{5,6},{6,7},{8,9},{9,10},{10,11},{12,13},{... | collective-permute-start | bytes 3538952 | tf_op jit(solution)/shard_map/ppermute | solution.py:406
  53.2 43.2 %collective-permute-start.2 = (bf16[2,224,1024]{2,1,0:T(8,128)(2,1)}, bf16[2,224,1024]{2,1,0:T(8,128)(2,1)}, u32[]{:S(2)}, u32[]{:S(2)}) collective-permute-start(bf16[2,224,1024]{2,1,0:T(8,128)(2,1)} %slice.151), channel_id=1, source_target_pairs={{0,1},{1,2},{2,3},{4,5},{5,6},{6,7},{8,9},{9,10},{10,11},{12,13},{... | collective-permute-start | bytes 2752520 | tf_op jit(solution)/shard_map/ppermute | solution.py:406
  67.9 64.6 %collective-permute-start.1 = (bf16[2,288,1024]{2,1,0:T(8,128)(2,1)}, bf16[2,288,1024]{2,1,0:T(8,128)(2,1)S(1)}, u32[]{:S(2)}, u32[]{:S(2)}) collective-permute-start(bf16[2,288,1024]{2,1,0:T(8,128)(2,1)} %collective-permute-done), channel_id=1, source_target_pairs={{0,1},{1,2},{2,3},{4,5},{5,6},{6,7},{8,9},{9,10},{10,11},{12,13},{... | collective-permute-start | bytes 3538952 | tf_op jit(solution)/shard_map/ppermute | solution.py:406
  315.2 48.5 %collective-permute-start.4 = (bf16[1024,1024]{1,0:T(8,128)(2,1)}, bf16[1024,1024]{1,0:T(8,128)(2,1)}, u32[]{:S(2)}, u32[]{:S(2)}) collective-permute-start(bf16[1024,1024]{1,0:T(8,128)(2,1)} %get-tuple-element.304), channel_id=1, source_target_pairs={{0,16},{4,20},{8,24},{12,28},{16,0},{20,4},{24,8},{28,12},{1,17},{... | collective-permute-start | bytes 6291464 | tf_op jit(solution)/shard_map/ppermute | solution.py:285
  323.3 57.3 %collective-permute-start.5 = (bf16[512,4096]{1,0:T(8,128)(2,1)}, bf16[512,4096]{1,0:T(8,128)(2,1)}, u32[]{:S(2)}, u32[]{:S(2)}) collective-permute-start(bf16[512,4096]{1,0:T(8,128)(2,1)} %convolution_convert_fusion), channel_id=1, source_target_pairs={{0,4},{4,0},{8,12},{12,8},{16,20},{20,16},{24,28},{28,24},{1,5},{5... | collective-permute-start | bytes 12582920 | tf_op jit(solution)/shard_map/ppermute | solution.py:285
  379.0 27.2 %collective-permute-start.6 = (bf16[512,1024]{1,0:T(8,128)(2,1)}, bf16[512,1024]{1,0:T(8,128)(2,1)}, u32[]{:S(2)}, u32[]{:S(2)}) collective-permute-start(bf16[512,1024]{1,0:T(8,128)(2,1)} %get-tuple-element.326), channel_id=1, source_target_pairs={{0,8},{4,12},{8,0},{12,4},{16,24},{20,28},{24,16},{28,20},{1,9},{5... | collective-permute-start | bytes 3145736 | tf_op jit(solution)/shard_map/ppermute | solution.py:285
  414.2 64.5 %collective-permute-start.8 = (bf16[256,1024]{1,0:T(8,128)(2,1)}, bf16[256,1024]{1,0:T(8,128)(2,1)S(1)}, u32[]{:S(2)}, u32[]{:S(2)}) collective-permute-start(bf16[256,1024]{1,0:T(8,128)(2,1)} %bitcast.23), channel_id=1, source_target_pairs={{0,1},{1,0},{2,3},{3,2},{4,5},{5,4},{6,7},{7,6},{8,9},{9,8},{10,11... | collective-permute-start | bytes 1572872 | tf_op jit(solution)/shard_map/ppermute | solution.py:285
  434.1 46.6 %collective-permute-start.7 = (bf16[256,4096]{1,0:T(8,128)(2,1)}, bf16[256,4096]{1,0:T(8,128)(2,1)}, u32[]{:S(2)}, u32[]{:S(2)}) collective-permute-start(bf16[256,4096]{1,0:T(8,128)(2,1)} %bitcast.20), channel_id=1, source_target_pairs={{0,8},{4,12},{8,0},{12,4},{16,24},{20,28},{24,16},{28,20},{1,9},{5... | collective-permute-start | bytes 6291464 | tf_op jit(solution)/shard_map/ppermute | solution.py:285
  490.1 54.1 %collective-permute-start.9 = (bf16[2,288,1024]{2,1,0:T(8,128)(2,1)S(1)}, bf16[2,288,1024]{2,1,0:T(8,128)(2,1)S(1)}, u32[]{:S(2)}, u32[]{:S(2)}) collective-permute-start(bf16[2,288,1024]{2,1,0:T(8,128)(2,1)S(1)} %bitcast.301), channel_id=1, source_target_pairs={{1,0},{2,1},{3,2},{5,4},{6,5},{7,6},{9,8},{10,9},{11,10},{13,12},{... | collective-permute-start | bytes 3538952 | tf_op jit(solution)/shard_map/ppermute | solution.py:510
  559.1 29.3 %collective-permute-start.12 = (bf16[512,4096]{1,0:T(8,128)(2,1)}, bf16[512,4096]{1,0:T(8,128)(2,1)}, u32[]{:S(2)}, u32[]{:S(2)}) collective-permute-start(bf16[512,4096]{1,0:T(8,128)(2,1)} %pad_maximum_fusion), channel_id=1, source_target_pairs={{0,4},{4,0},{8,12},{12,8},{16,20},{20,16},{24,28},{28,24},{1,5},{5... | collective-permute-start | bytes 12582920 | tf_op jit(solution)/shard_map/ppermute | solution.py:285
  570.9 22.1 %collective-permute-start.11 = (bf16[128,1024]{1,0:T(8,128)(2,1)}, bf16[128,1024]{1,0:T(8,128)(2,1)S(1)}, u32[]{:S(2)}, u32[]{:S(2)}) collective-permute-start(bf16[128,1024]{1,0:T(8,128)(2,1)} %get-tuple-element.399), channel_id=1, source_target_pairs={{0,2},{1,3},{2,0},{3,1},{4,6},{5,7},{6,4},{7,5},{8,10},{9,11},{10,... | collective-permute-start | bytes 786440 | tf_op jit(solution)/shard_map/ppermute | solution.py:285
  572.3 67.1 %collective-permute-start.15 = (bf16[128,4096]{1,0:T(8,128)(2,1)}, bf16[128,4096]{1,0:T(8,128)(2,1)S(1)}, u32[]{:S(2)}, u32[]{:S(2)}) collective-permute-start(bf16[128,4096]{1,0:T(8,128)(2,1)} %get-tuple-element.442), channel_id=1, source_target_pairs={{0,16},{4,20},{8,24},{12,28},{16,0},{20,4},{24,8},{28,12},{1,17},{... | collective-permute-start | bytes 3145736 | tf_op jit(solution)/shard_map/ppermute | solution.py:285
  572.3 53.4 %collective-permute-start.10 = (bf16[2,512,1024]{2,1,0:T(8,128)(2,1)}, bf16[2,512,1024]{2,1,0:T(8,128)(2,1)S(1)}, u32[]{:S(2)}, u32[]{:S(2)}) collective-permute-start(bf16[2,512,1024]{2,1,0:T(8,128)(2,1)} %add_convert_fusion.4), channel_id=1, source_target_pairs={{1,0},{2,1},{3,2},{5,4},{6,5},{7,6},{9,8},{10,9},{11,10},{13,12},{... | collective-permute-start | bytes 6291464 | tf_op jit(solution)/shard_map/ppermute | solution.py:510
  593.9 25.9 %collective-permute-start.14 = (bf16[256,2048]{1,0:T(8,128)(2,1)S(1)}, bf16[256,2048]{1,0:T(8,128)(2,1)S(1)}, u32[]{:S(2)}, u32[]{:S(2)}) collective-permute-start(bf16[256,2048]{1,0:T(8,128)(2,1)S(1)} %get-tuple-element.429), channel_id=1, source_target_pairs={{0,16},{4,20},{8,24},{12,28},{16,0},{20,4},{24,8},{28,12},{1,17},{... | collective-permute-start | bytes 3145736 | tf_op jit(solution)/shard_map/ppermute | solution.py:285
  595.9 24.4 %collective-permute-start.13 = (bf16[256,2048]{1,0:T(8,128)(2,1)S(1)}, bf16[256,2048]{1,0:T(8,128)(2,1)S(1)}, u32[]{:S(2)}, u32[]{:S(2)}) collective-permute-start(bf16[256,2048]{1,0:T(8,128)(2,1)S(1)} %bitcast.276), channel_id=1, source_target_pairs={{0,8},{4,12},{8,0},{12,4},{16,24},{20,28},{24,16},{28,20},{1,9},{5... | collective-permute-start | bytes 3145736 | tf_op jit(solution)/shard_map/ppermute | solution.py:285
  642.3 29.0 %collective-permute-start.19 = (f32[22544]{0:T(1024)S(1)}, f32[22544]{0:T(1024)S(1)}, u32[]{:S(2)}, u32[]{:S(2)}) collective-permute-start(f32[22544]{0:T(1024)S(1)} %concatenate.27), channel_id=1, source_target_pairs={{0,4},{4,0},{8,12},{12,8},{16,20},{20,16},{24,28},{28,24},{1,5},{5... | collective-permute-start | bytes 270536 | tf_op jit(solution)/shard_map/ppermute | solution.py:285
  645.8 28.2 %collective-permute-start.18 = (bf16[64,2048]{1,0:T(8,128)(2,1)}, bf16[64,2048]{1,0:T(8,128)(2,1)S(1)}, u32[]{:S(2)}, u32[]{:S(2)}) collective-permute-start(bf16[64,2048]{1,0:T(8,128)(2,1)} %bitcast.55), channel_id=1, source_target_pairs={{0,1},{1,0},{2,3},{3,2},{4,5},{5,4},{6,7},{7,6},{8,9},{9,8},{10,11... | collective-permute-start | bytes 786440 | tf_op jit(solution)/shard_map/ppermute | solution.py:285
  669.4 19.3 %collective-permute-start.22 = (bf16[64,4096]{1,0:T(8,128)(2,1)S(1)}, bf16[64,4096]{1,0:T(8,128)(2,1)S(1)}, u32[]{:S(2)}, u32[]{:S(2)}) collective-permute-start(bf16[64,4096]{1,0:T(8,128)(2,1)S(1)} %bitcast.281), channel_id=1, source_target_pairs={{0,1},{1,0},{2,3},{3,2},{4,5},{5,4},{6,7},{7,6},{8,9},{9,8},{10,11... | collective-permute-start | bytes 1572872 | tf_op jit(solution)/shard_map/ppermute | solution.py:285
  671.3 17.7 %collective-permute-start.21 = (f32[22544]{0:T(1024)S(1)}, f32[22544]{0:T(1024)S(1)}, u32[]{:S(2)}, u32[]{:S(2)}) collective-permute-start(f32[22544]{0:T(1024)S(1)} %add.467), channel_id=1, source_target_pairs={{0,8},{4,12},{8,0},{12,4},{16,24},{20,28},{24,16},{28,20},{1,9},{5... | collective-permute-start | bytes 270536 | tf_op jit(solution)/shard_map/ppermute | solution.py:285
  688.9 17.1 %collective-permute-start.26 = (bf16[32,4096]{1,0:T(8,128)(2,1)S(1)}, bf16[32,4096]{1,0:T(8,128)(2,1)S(1)}, u32[]{:S(2)}, u32[]{:S(2)}) collective-permute-start(bf16[32,4096]{1,0:T(8,128)(2,1)S(1)} %get-tuple-element.497), channel_id=1, source_target_pairs={{0,2},{1,3},{2,0},{3,1},{4,6},{5,7},{6,4},{7,5},{8,10},{9,11},{10,... | collective-permute-start | bytes 786440 | tf_op jit(solution)/shard_map/ppermute | solution.py:285
  694.8 20.6 %collective-permute-start.20 = (bf16[32,2048]{1,0:T(8,128)(2,1)S(1)}, bf16[32,2048]{1,0:T(8,128)(2,1)S(1)}, u32[]{:S(2)}, u32[]{:S(2)}) collective-permute-start(bf16[32,2048]{1,0:T(8,128)(2,1)S(1)} %get-tuple-element.478), channel_id=1, source_target_pairs={{0,2},{1,3},{2,0},{3,1},{4,6},{5,7},{6,4},{7,5},{8,10},{9,11},{10,... | collective-permute-start | bytes 393224 | tf_op jit(solution)/shard_map/ppermute | solution.py:285
  (113 other events, 800.8 us)
Sparse Core Ops, SparseCore 0:
  11.5 85.0 all-gather.3
  100.0 89.1 all-gather.5
  192.1 75.6 all-gather.7

commit v6 on v5

--- a/solution.py
+++ b/solution.py
@@ -334,6 +334,11 @@
         return values[0] if len(values) == 1 else values
 
 
+def lay_rows(total, width, shares):
+    total = total.astype(jnp.bfloat16)
+    return [total[:, left : left + width].reshape(shares, -1, width) for left in range(0, total.shape[1], width)]
+
+
 class RowSum:
     def __init__(self, order):
         self.order = list(order)
@@ -351,8 +356,11 @@
             came, kept = sequence(self.came, self.kept)
         total = kept.astype(jnp.float32) + came.astype(jnp.float32)
         if not self.order:
-            self.total = sequence(total)
+            self.total = total
             return
+        self.send(total, sequence)
+
+    def send(self, total, sequence):
         axis, bit = self.order.pop(0)
         at = self.left.index((axis, bit))
         self.left.pop(at)
@@ -460,8 +468,7 @@
     mixed = (hat_middle * middle_gain + middle_shift).astype(jnp.bfloat16)
     grad_low = flat(cotangent)
     grad_out = grad_low.astype(jnp.float32)
-    one_way = [core, *reversed(planes), *bits_of("seq")]
-    other_way = [core, *planes, *bits_of("seq")]
+    one_way, other_way = [core, *reversed(planes)], [core, *planes]
 
     down_sum, up_sum = RowSum(one_way), RowSum(other_way)
     sums = query_key_sum, value_output_sum = RowSum(one_way), RowSum(other_way)
@@ -481,7 +488,6 @@
     sent = dot_tn(other_second, grad_upper).astype(jnp.bfloat16)
     sent, grad_upper = sequence(sent, grad_upper)
     up_sum.begin(exchange(sent, *core))
-    down_sum.step(sequence)
     up_sum.kept = lambda: dot_tn(own_second, sequence(grad_upper))
     grad_upper = sequence(grad_upper)
     grad_second = sequence(dot_nt(grad_upper, up_full))
@@ -489,8 +495,6 @@
     grad_second = sequence(grad_second)
     grad_middle = grad_out + norm_back(hat_two, scale_two, second_gain, grad_second)
     grad_branch = norm_back(hat_post, scale_post, post_gain, grad_middle).astype(jnp.bfloat16)
-    grad_branch = sequence(grad_branch)
-    down_sum.step(sequence)
     grad_branch = sequence(grad_branch)
     grad_scaled = dot_nt(grad_branch, output_full)
     grad_attended = (grad_scaled * jnp.repeat(head_scale, model // head_count)).astype(jnp.bfloat16)
@@ -536,6 +540,18 @@
 
     sent = sequence(jnp.concatenate([part.astype(jnp.bfloat16) for part in four(0)], 1))
     came = exchange(sent, *core)
+
+    def join(row_sums, width):
+        for row_sum in row_sums:
+            while row_sum.total is None:
+                row_sum.step(sequence)
+        joint = RowSum(bits_of("seq"))
+        joint.left = bits_of("seq")[::-1]
+        pieces = [piece for row_sum in row_sums for piece in lay_rows(row_sum.total, width, ranks)]
+        joint.send(jnp.concatenate(pieces, 1).reshape(-1, width), sequence)
+        return joint
+
+    outer = join([down_sum, up_sum], model)
     query_low, grad_branch, *pairs = sequence(query_low, grad_branch, *dkeys, *dvalues)
     dkeys, dvalues = pairs[: len(dkeys)], pairs[len(dkeys) :]
     for index, row_sum in enumerate(sums):
@@ -543,7 +559,6 @@
         row_sum.begin(came[:, columns])
         row_sum.kept = lambda index=index: jnp.concatenate(four(1)[2 * index : 2 * (index + 1)], 1)
         row_sum.step(sequence)
-    down_sum.step(sequence)
 
     query_low, dkeys[0], dvalues[0] = sequence(query_low, dkeys[0], dvalues[0])
     own = (
@@ -552,14 +567,9 @@
         + dot_nt(dvalues[0], inward[:, 2 * model :])
     )
     own = sequence(own)
-    grad_normed = own
     for row_sum in sums:
         row_sum.step(sequence)
-    if hops:
-        carried, own = sequence(carried, own)
-        grad_normed = own + flat(jnp.pad(carried.astype(jnp.float32), ((0, 0), (rows - carried.shape[1], 0), (0, 0))))
-    for row_sum in (*sums, up_sum):
-        row_sum.step(sequence)
+    outer.step(sequence)
     own = sequence(own)
     vector = jnp.concatenate(
         [
@@ -580,29 +590,41 @@
         ]
     )
     places = bits_of("dp") + bits_of("seq")
-
-    def sum_vector(vector, count):
-        for _ in range(min(count, len(places))):
-            vector = sequence(vector + exchange(vector, *places.pop(0)))
-        return vector
-
     vector = sequence(vector)
+    vector_came = exchange(vector, *places.pop(0))
+
+    def add_vector(vector, vector_came):
+        if vector_came is not None:
+            vector = sequence(vector + vector_came)
+            vector_came = exchange(vector, *places.pop(0)) if places else None
+        return vector, vector_came
+
+    grad_normed = own
+    if hops:
+        carried, own = sequence(carried, own)
+        grad_normed = own + flat(jnp.pad(carried.astype(jnp.float32), ((0, 0), (rows - carried.shape[1], 0), (0, 0))))
+    vector, vector_came = add_vector(vector, vector_came)
+    inner = join(sums, 2 * model)
+    vector, vector_came = add_vector(vector, vector_came)
     grad_normed, mixed, middle = sequence(grad_normed, mixed, middle)
     input_grad = (grad_middle + norm_back(hat_one, scale_one, first_gain, grad_normed)).astype(jnp.bfloat16)
+    input_grad = sequence(input_grad)
+    vector, vector_came = add_vector(vector, vector_came)
+    mixed, middle = sequence(mixed, middle)
     layer_output = (middle + dot_nn(mixed, down_full) + down_bias).astype(jnp.bfloat16)
-    input_grad, layer_output = sequence(input_grad, layer_output)
-    vector = sum_vector(vector, 1)
-    for row_sum in (*sums, up_sum):
-        row_sum.step(sequence)
-    vector = sum_vector(vector, 2)
-    up_sum.step(sequence)
-    vector = sum_vector(vector, len(places))
-    for row_sum in (up_sum, *sums, down_sum):
-        while row_sum.total is None:
-            row_sum.step(sequence)
+    layer_output = sequence(layer_output)
+    inner.step(sequence)
+    while vector_came is not None:
+        vector, vector_came = add_vector(vector, vector_came)
+    for joint in (outer, inner):
+        while joint.total is None:
+            joint.step(sequence)
     vectors = vector + sequence.token[0, 0]
 
-    query_key, value_output = query_key_sum.total, value_output_sum.total
+    share = down_weight.shape[0]
+    down_total, outer_total = outer.total[:share], outer.total[share:]
+    up_total = jnp.concatenate(jnp.split(outer_total, hidden // model), 1)
+    query_key, value_output = jnp.split(inner.total, 2)
     rest = vectors[head_count:]
     narrow = rest[: 10 * model].reshape(10, model)
     broad = rest[10 * model :].reshape(3, hidden)
@@ -613,8 +635,8 @@
         query_key[:, model:],
         value_output[:, :model],
         value_output[:, model:],
-        up_sum.total,
-        down_sum.total,
+        up_total,
+        down_total,
         narrow[6],
         narrow[7],
         narrow[8],

time: 740 us -> 691 us (0.934)
  starting transfers between devices: 80 us -> 51.3 us
  waiting for transfers between devices: 212 us -> 196 us
    ppermute x24 -> x20, waiting for transfers between devices: 87.1 us -> 39.1 us  [exchange(): lax.ppermute(array, axis, [(i, i ^ 1 << bit) for i in range(lax.axis_size...]
    ppermute x2, waiting for transfers between devices: 50.2 us -> 81.7 us  [local(): lower = lambda array: lax.ppermute(array, 'seq', downward)]
    ppermute x24 -> x20, starting transfers between devices: 60.6 us -> 31.5 us  [exchange(): lax.ppermute(array, axis, [(i, i ^ 1 << bit) for i in range(lax.axis_size...]
    convert_element_type x16 -> x14, other arithmetic: 22.4 us -> 24.4 us  [the longest x10 22.2 us: send(): total = total.astype(jnp.bfloat16)]
  transfers between devices with their start and end apart: 32 -> 28, of which waited for: 19 -> 11; matrix products, arithmetic and copies ran while one was open for 32% -> 37% of each run, Pallas kernels for 14% -> 15%
where the time goes in v6:
time: 691 us; the launch traced here: 680 us
  waiting for transfers between devices  196 us (28%)
  matrix products  164 us (24%)
  other arithmetic  116 us (17%)
  Pallas kernels  102 us (15%)
  starting transfers between devices  51.3 us (7%)
  local copies, waits for them, and re-layouts  35.1 us (5%)
  between operations  15.9 us (2%)
    ppermute x2, waiting for transfers between devices, local(): lower = lambda array: lax.ppermute(array, 'seq', downward)  81.7 us
    dot_general x10, matrix products, dot_nt(): lax.dot_general(a, b, (((1,), (1,)), ((), ())), preferred_element_type=jn...  62.8 us
    ppermute x3, waiting for transfers between devices, local(): shift = lambda array: lax.ppermute(array, 'seq', upward)  57.2 us
    dot_general x6, matrix products, dot_nn(): lax.dot_general(a, b, (((1,), (0,)), ((), ())), preferred_element_type=jn...  51.5 us
    dot_general x20, matrix products, dot_tn(): lax.dot_general(a, b, (((0,), (0,)), ((), ())), preferred_element_type=jn...  50 us
    pallas_call x1, Pallas kernels, attend_back(): pl.pallas_call(kernel, grid_spec=pltpu.PrefetchScalarGridSpec(num_scalar_...  44.3 us
    ppermute x20, waiting for transfers between devices, exchange(): lax.ppermute(array, axis, [(i, i ^ 1 << bit) for i in range(lax.axis_size...  39.1 us
    ppermute x20, starting transfers between devices, exchange(): lax.ppermute(array, axis, [(i, i ^ 1 << bit) for i in range(lax.axis_size...  31.5 us
  transfers between devices with their start and end apart: 28, of which 11 were waited for; matrix products, arithmetic and copies ran while one was open for 37% of the time, Pallas kernels for 15%

profile of v6, /device:TPU:0, one launch (start us, length us, event | category | flops | bytes accessed | tf_op | source)
XLA Modules:
  0.0 680.3 jit_solution(5486073659123867603)
XLA Ops:
  20.7 32.5 %collective-permute-done = bf16[2,288,1024]{2,1,0:T(8,128)(2,1)} collective-permute-done((bf16[2,288,1024]{2,1,0:T(8,128)(2,1)S(1)}, bf16[2,288,1024]{2,1,0:T(8,128)(2,1)}, u32[]{:S(2)}, u32[]{:S(2)}) %collective-permute-start) | collective-permute-done | bytes 1179680 | tf_op jit(solution)/shard_map/ppermute | solution.py:414
  71.6 24.7 %collective-permute-done.2 = bf16[2,224,1024]{2,1,0:T(8,128)(2,1)} collective-permute-done((bf16[2,224,1024]{2,1,0:T(8,128)(2,1)}, bf16[2,224,1024]{2,1,0:T(8,128)(2,1)}, u32[]{:S(2)}, u32[]{:S(2)}) %collective-permute-start.2) | collective-permute-done | bytes 917536 | tf_op jit(solution)/shard_map/ppermute | solution.py:414
  99.4 9.4 %fusion.73 = f32[1024,3072]{1,0:T(8,128)S(1)} fusion(bf16[1024,1024]{1,0:T(8,128)(2,1)} %fusion.24.array_ref, bf16[1024,3072]{1,0:T(8,128)(2,1)} %all-gather.4.cloned.1.call-done), kind=kOutput, calls=%fused_computation.216 | convolution fusion | flops 6442450944 | bytes 20971520 | tf_op jit(solution)/shard_map/dot_general | solution.py:19
  121.9 6.9 %fusion.34 = f32[1024,2048]{1,0:T(8,128)S(1)} fusion(bf16[1024,1024]{1,0:T(8,128)(2,1)} %add_convert_fusion.8.array_ref, bf16[1024,3072]{1,0:T(8,128)(2,1)} %all-gather.4.cloned.1.call-done), kind=kOutput, calls=%fused_computation.90 | convolution fusion | flops 4294967296 | bytes 14680064 | tf_op jit(solution)/shard_map/dot_general | solution.py:19
  141.3 30.2 %attend.1 = (bf16[2,512,1024]{2,1,0:T(8,128)(2,1)}, f32[2,4,4,512]{3,2,1,0:T(4,128)}) custom-call(s32[2,2]{1,0:T(2,128)} %slice.174.first_ref, f32[16]{0:T(128)} %scale_ref.3, bf16[2,512,1024]{2,1,0:T(8,128)(2,1)} %bitcast.251, bf16[2,512,1024]{2,1,0:T(8,128)(2,1)} %bitcast.238, bf16[2,512,1024]{2,1,0:T(8,128)(2,1)} %bitcast.240, ...), custom_call_target="tpu_custom_call" | custom-call | flops 33017561088 | bytes 32243712 | tf_op jit(solution)/shard_map/attend/pallas_call | solution.py:142
  171.5 17.6 %all-gather.6.cloned.1.call-done = bf16[1024,5120]{1,0:T(8,128)(2,1)} async-done(((bf16[32,5120]{1,0:T(8,128)(2,1)}), bf16[1024,5120]{1,0:T(8,128)(2,1)}) %all-gather.6.cloned.1.call-update) | async-done | bytes 10485776 | tf_op jit(solution)/shard_map/all_gather | solution.py:427
  201.2 15.6 %fusion.64 = (f32[1024]{0:T(1024)S(1)}, f32[1024,4096]{1,0:T(8,128)}, f32[1024,4096]{1,0:T(8,128)}) fusion(f32[4096]{0:T(1024)S(1)} %copy-done.74, bf16[1024,1024]{1,0:T(8,128)(2,1)S(1)} %add_convert_fusion.7.array_ref, bf16[1024,5120]{1,0:T(8,128)(2,1)S(1)} %bitcast.283), kind=kOutput, calls=%fused_computation.208 | convolution fusion | flops 8615099392 | bytes 44060672 | tf_op jit(solution)/shard_map/dot_general | solution.py:19
  216.9 7.6 %multiply_reduce_fusion.2 = f32[1024]{0:T(1024)S(1)} fusion(f32[1024,4096]{1,0:T(8,128)} %get-tuple-element.484, f32[1024]{0:T(1024)S(1)} %broadcast_multiply_fusion.2), kind=kLoop, calls=%fused_computation.11 | loop fusion | flops 12581888 | bytes 16785408 | tf_op jit(solution)/shard_map/reduce_sum | solution.py:33
  224.5 10.2 %add_convert_fusion.array_ref = bf16[1024,4096]{1,0:T(8,128)(2,1)} fusion(f32[1024,4096]{1,0:T(8,128)} %get-tuple-element.484, f32[4096]{0:T(1024)S(1)} %copy-done.73, f32[4096]{0:T(1024)S(1)} %copy-done.50, f32[1024]{0:T(1024)S(1)} %add_rsqrt_fusion, f32[1024]{0:T(1024)S(1)} %broadcast_multiply_fusion.2), kind=kLoop, calls=%fused_computation.10 | loop fusion | flops 20971520 | bytes 25206784 | tf_op jit(solution)/shard_map/convert_element_type | solution.py:468
  234.7 7.9 %pick.9 = (bf16[1024,2048]{1,0:T(8,128)(2,1)}, bf16[1024,2048]{1,0:T(8,128)(2,1)}) custom-call(s32[1]{0:T(128)} %bitcast.4.mine_ref, bf16[1024,4096]{1,0:T(8,128)(2,1)} %add_convert_fusion.array_ref), custom_call_target="tpu_custom_call" | custom-call | bytes 33554432 | tf_op jit(solution)/shard_map/pick/pallas_call | solution.py:314
  242.6 8.4 %convolution_convert_fusion.1 = bf16[2048,1024]{1,0:T(8,128)(2,1)} fusion(bf16[1024,2048]{1,0:T(8,128)(2,1)} %get-tuple-element.259, bf16[1024,1024]{1,0:T(8,128)(2,1)S(1)} %bitcast.220), kind=kOutput, calls=%fused_computation.86 | convolution fusion | flops 4297064448 | bytes 10485760 | tf_op jit(solution)/shard_map/dot_general | solution.py:27
  259.1 9.0 %fusion.74 = f32[2048,1024]{1,0:T(8,128)} fusion(bf16[1024,2048]{1,0:T(8,128)(2,1)} %get-tuple-element.262, bf16[1024,1024]{1,0:T(8,128)(2,1)S(1)} %bitcast.221), kind=kOutput, calls=%fused_computation.217 | convolution fusion | flops 4294967296 | bytes 14680064 | tf_op jit(solution)/shard_map/dot_general | solution.py:27
  276.8 20.8 %multiply_reduce_fusion = (f32[4096]{0:T(1024)}, f32[1024]{0:T(1024)S(1)}, f32[1024]{0:T(1024)S(1)}, f32[4096]{0:T(1024)}, f32[1024,4096]{1,0:T(8,128)}) fusion(f32[1024,4096]{1,0:T(8,128)} %get-tuple-element.484, f32[1024]{0:T(1024)S(1)} %add_rsqrt_fusion, f32[1024]{0:T(1024)S(1)} %broadcast_multiply_fusion.2, f32[4096]{0:T(1024)S(1)} %copy-done.50, ...), kind=kOutput, calls=%fused_computation.7 | convolution fusion | flops 8627673088 | bytes 44105728 | tf_op jit(solution)/shard_map/dot_general | solution.py:23
  297.7 17.3 %fusion.5 = bf16[1024,4096]{1,0:T(8,128)(2,1)S(1)} fusion(f32[1024,4096]{1,0:T(8,128)} %get-tuple-element.550, f32[1024,4096]{1,0:T(8,128)} %get-tuple-element.549, f32[1024,4096]{1,0:T(8,128)} %get-tuple-element.484, f32[1024]{0:T(1024)S(1)} %get-tuple-element.553, f32[1024]{0:T(1024)S(1)} %get-tuple-element.554, f32[4096]{0:T(1024)S(1)} %copy-done.50, ...), kind=kLoop, calls=%fused_computation.6 | loop fusion | flops 75497472 | bytes 58769408 | tf_op jit(solution)/shard_map/convert_element_type | solution.py:485
  330.5 13.1 %fusion.6 = f32[1024,1024]{1,0:T(8,128)S(1)} fusion(bf16[1024,4096]{1,0:T(8,128)(2,1)} %copy-done.5, bf16[1024,5120]{1,0:T(8,128)(2,1)} %all-gather.6.cloned.1.call-done), kind=kOutput, calls=%fused_computation.19 | convolution fusion | flops 8589934592 | bytes 20971520 | tf_op jit(solution)/shard_map/dot_general | solution.py:23
  350.4 7.0 %fusion.75 = f32[512,4096]{1,0:T(8,128)S(1)} fusion(bf16[1024,512]{1,0:T(8,128)(2,1)S(1)} %copy-done.30, bf16[1024,4096]{1,0:T(8,128)(2,1)} %copy-done.5), kind=kOutput, calls=%fused_computation.218 | convolution fusion | flops 4294967296 | bytes 17825792 | tf_op jit(solution)/shard_map/dot_general | solution.py:27
  385.7 44.3 %attend_back.1 = (bf16[2,512,1024]{2,1,0:T(8,128)(2,1)}, bf16[2,512,1024]{2,1,0:T(8,128)(2,1)}, bf16[2,512,1024]{2,1,0:T(8,128)(2,1)}, bf16[2,288,1024]{2,1,0:T(...) custom-call(s32[2,2]{1,0:T(2,128)} %slice.174.first_ref, ...), custom_call_target="tpu_custom_call" | custom-call | flops 55029268480 | bytes 53739520 | tf_op jit(solution)/shard_map/attend_back/pallas_call | solution.py:239
  451.9 63.4 %collective-permute-done.7 = bf16[2,288,1024]{2,1,0:T(8,128)(2,1)S(1)} collective-permute-done((bf16[2,288,1024]{2,1,0:T(8,128)(2,1)S(1)}, bf16[2,288,1024]{2,1,0:T(8,128)(2,1)S(1)}, u32[]{:S(2)}, u32[]{:S(2)}) %collective-permute-start.7) | collective-permute-done | bytes 1179680 | tf_op jit(solution)/shard_map/ppermute | solution.py:514
  530.6 11.3 %collective-permute-start.11 = (bf16[512,4096]{1,0:T(8,128)(2,1)S(1)}, bf16[512,4096]{1,0:T(8,128)(2,1)S(1)}, u32[]{:S(2)}, u32[]{:S(2)}) collective-permute-start(bf16[512,4096]{1,0:T(8,128)(2,1)S(1)} %pad_maximum_fusion), channel_id=1, source_target_pairs={{0,4},{4,0},{8,12},{12,8},{16,20},{20,16},{24,28},{28,24},{1,5},{5... | collective-permute-start | bytes 12582920 | tf_op jit(solution)/shard_map/ppermute | solution.py:285
  576.8 8.5 %collective-permute-done.14 = bf16[256,2048]{1,0:T(8,128)(2,1)S(1)} collective-permute-done((bf16[256,2048]{1,0:T(8,128)(2,1)S(1)}, bf16[256,2048]{1,0:T(8,128)(2,1)S(1)}, u32[]{:S(2)}, u32[]{:S(2)}) %collective-permute-start.14) | collective-permute-done | bytes 1048608 | tf_op jit(solution)/shard_map/ppermute | solution.py:285
  595.3 18.4 %collective-permute-done.8 = bf16[2,512,1024]{2,1,0:T(8,128)(2,1)} collective-permute-done((bf16[2,512,1024]{2,1,0:T(8,128)(2,1)}, bf16[2,512,1024]{2,1,0:T(8,128)(2,1)}, u32[]{:S(2)}, u32[]{:S(2)}) %collective-permute-start.8) | collective-permute-done | bytes 2097184 | tf_op jit(solution)/shard_map/ppermute | solution.py:514
  629.0 10.0 %add_convert_fusion.3 = bf16[1024,1024]{1,0:T(8,128)(2,1)} fusion(f32[1024,1024]{1,0:T(8,128)S(1)} %copy-done.4, f32[1024]{0:T(1024)S(1)} %copy-done.83, bf16[1024,4096]{1,0:T(8,128)(2,1)S(1)} %bitcast.206, bf16[4096,1024]{1,0:T(8,128)(2,1)S(1)} %bitcast.285), kind=kOutput, calls=%fused_computation.60 | convolution fusion | flops 8593080320 | bytes 23072768 | tf_op jit(solution)/shard_map/dot_general | solution.py:19
  639.0 12.6 %collective-permute-done.23 = f32[22544]{0:T(1024)S(1)} collective-permute-done((f32[22544]{0:T(1024)S(1)}, f32[22544]{0:T(1024)S(1)}, u32[]{:S(2)}, u32[]{:S(2)}) %collective-permute-start.23) | collective-permute-done | bytes 90208 | tf_op jit(solution)/shard_map/ppermute | solution.py:285
  654.7 9.3 %collective-permute-done.24 = f32[22544]{0:T(1024)S(1)} collective-permute-done((f32[22544]{0:T(1024)S(1)}, f32[22544]{0:T(1024)S(1)}, u32[]{:S(2)}, u32[]{:S(2)}) %collective-permute-start.24) | collective-permute-done | bytes 90208 | tf_op jit(solution)/shard_map/ppermute | solution.py:285
  (414 shorter events, 248.5 us)
Async XLA Ops:
  7.2 92.2 %all-gather.4.cloned.1.call-start = ((), (), s32[]{:S(2)}) async-start(), calls=%async_computation | async-start | bytes 6488064 | tf_op jit(solution)/shard_map/all_gather | solution.py:426
  9.0 180.0 %all-gather.6.cloned.1.call-start = ((), (), s32[]{:S(2)}) async-start(), calls=%async_computation.1 | async-start | bytes 10813440 | tf_op jit(solution)/shard_map/all_gather | solution.py:427
  10.8 266.0 %all-gather.8.cloned.1.call-start = ((), (), s32[]{:S(2)}) async-start(), calls=%async_computation.2 | async-start | bytes 8650752 | tf_op jit(solution)/shard_map/all_gather | solution.py:428
  12.2 40.9 %collective-permute-start = (bf16[2,288,1024]{2,1,0:T(8,128)(2,1)S(1)}, bf16[2,288,1024]{2,1,0:T(8,128)(2,1)}, u32[]{:S(2)}, u32[]{:S(2)}) collective-permute-start(bf16[2,288,1024]{2,1,0:T(8,128)(2,1)S(1)} %slice.176), channel_id=1, source_target_pairs={{0,1},{1,2},{2,3},{4,5},{5,6},{6,7},{8,9},{9,10},{10,11},{12,13},{... | collective-permute-start | bytes 3538952 | tf_op jit(solution)/shard_map/ppermute | solution.py:414
  53.2 43.2 %collective-permute-start.2 = (bf16[2,224,1024]{2,1,0:T(8,128)(2,1)}, bf16[2,224,1024]{2,1,0:T(8,128)(2,1)}, u32[]{:S(2)}, u32[]{:S(2)}) collective-permute-start(bf16[2,224,1024]{2,1,0:T(8,128)(2,1)} %slice.175), channel_id=1, source_target_pairs={{0,1},{1,2},{2,3},{4,5},{5,6},{6,7},{8,9},{9,10},{10,11},{12,13},{... | collective-permute-start | bytes 2752520 | tf_op jit(solution)/shard_map/ppermute | solution.py:414
  67.8 64.7 %collective-permute-start.1 = (bf16[2,288,1024]{2,1,0:T(8,128)(2,1)}, bf16[2,288,1024]{2,1,0:T(8,128)(2,1)S(1)}, u32[]{:S(2)}, u32[]{:S(2)}) collective-permute-start(bf16[2,288,1024]{2,1,0:T(8,128)(2,1)} %collective-permute-done), channel_id=1, source_target_pairs={{0,1},{1,2},{2,3},{4,5},{5,6},{6,7},{8,9},{9,10},{10,11},{12,13},{... | collective-permute-start | bytes 3538952 | tf_op jit(solution)/shard_map/ppermute | solution.py:414
  321.3 29.1 %collective-permute-start.4 = (bf16[512,4096]{1,0:T(8,128)(2,1)}, bf16[512,4096]{1,0:T(8,128)(2,1)}, u32[]{:S(2)}, u32[]{:S(2)}) collective-permute-start(bf16[512,4096]{1,0:T(8,128)(2,1)} %convolution_convert_fusion), channel_id=1, source_target_pairs={{0,4},{4,0},{8,12},{12,8},{16,20},{20,16},{24,28},{28,24},{1,5},{5... | collective-permute-start | bytes 12582920 | tf_op jit(solution)/shard_map/ppermute | solution.py:285
  343.6 86.4 %collective-permute-start.6 = (bf16[1024,1024]{1,0:T(8,128)(2,1)}, bf16[1024,1024]{1,0:T(8,128)(2,1)}, u32[]{:S(2)}, u32[]{:S(2)}) collective-permute-start(bf16[1024,1024]{1,0:T(8,128)(2,1)} %get-tuple-element.309), channel_id=1, source_target_pairs={{0,16},{4,20},{8,24},{12,28},{16,0},{20,4},{24,8},{28,12},{1,17},{... | collective-permute-start | bytes 6291464 | tf_op jit(solution)/shard_map/ppermute | solution.py:285
  384.7 50.9 %collective-permute-start.5 = (bf16[256,4096]{1,0:T(8,128)(2,1)}, bf16[256,4096]{1,0:T(8,128)(2,1)}, u32[]{:S(2)}, u32[]{:S(2)}) collective-permute-start(bf16[256,4096]{1,0:T(8,128)(2,1)} %bitcast.17), channel_id=1, source_target_pairs={{0,8},{4,12},{8,0},{12,4},{16,24},{20,28},{24,16},{28,20},{1,9},{5... | collective-permute-start | bytes 6291464 | tf_op jit(solution)/shard_map/ppermute | solution.py:285
  434.4 94.1 %collective-permute-start.9 = (bf16[512,1024]{1,0:T(8,128)(2,1)}, bf16[512,1024]{1,0:T(8,128)(2,1)}, u32[]{:S(2)}, u32[]{:S(2)}) collective-permute-start(bf16[512,1024]{1,0:T(8,128)(2,1)} %get-tuple-element.346), channel_id=1, source_target_pairs={{0,8},{4,12},{8,0},{12,4},{16,24},{20,28},{24,16},{28,20},{1,9},{5... | collective-permute-start | bytes 3145736 | tf_op jit(solution)/shard_map/ppermute | solution.py:285
  444.1 71.2 %collective-permute-start.7 = (bf16[2,288,1024]{2,1,0:T(8,128)(2,1)S(1)}, bf16[2,288,1024]{2,1,0:T(8,128)(2,1)S(1)}, u32[]{:S(2)}, u32[]{:S(2)}) collective-permute-start(bf16[2,288,1024]{2,1,0:T(8,128)(2,1)S(1)} %bitcast.290), channel_id=1, source_target_pairs={{1,0},{2,1},{3,2},{5,4},{6,5},{7,6},{9,8},{10,9},{11,10},{13,12},{... | collective-permute-start | bytes 3538952 | tf_op jit(solution)/shard_map/ppermute | solution.py:514
  446.0 82.4 %collective-permute-start.10 = (bf16[128,4096]{1,0:T(8,128)(2,1)S(1)}, bf16[128,4096]{1,0:T(8,128)(2,1)S(1)}, u32[]{:S(2)}, u32[]{:S(2)}) collective-permute-start(bf16[128,4096]{1,0:T(8,128)(2,1)S(1)} %get-tuple-element.356), channel_id=1, source_target_pairs={{0,16},{4,20},{8,24},{12,28},{16,0},{20,4},{24,8},{28,12},{1,17},{... | collective-permute-start | bytes 3145736 | tf_op jit(solution)/shard_map/ppermute | solution.py:285
  530.6 26.9 %collective-permute-start.11 = (bf16[512,4096]{1,0:T(8,128)(2,1)S(1)}, bf16[512,4096]{1,0:T(8,128)(2,1)S(1)}, u32[]{:S(2)}, u32[]{:S(2)}) collective-permute-start(bf16[512,4096]{1,0:T(8,128)(2,1)S(1)} %pad_maximum_fusion), channel_id=1, source_target_pairs={{0,4},{4,0},{8,12},{12,8},{16,20},{20,16},{24,28},{28,24},{1,5},{5... | collective-permute-start | bytes 12582920 | tf_op jit(solution)/shard_map/ppermute | solution.py:285
  543.1 44.9 %collective-permute-start.12 = (bf16[512,1024]{1,0:T(8,128)(2,1)}, bf16[512,1024]{1,0:T(8,128)(2,1)}, u32[]{:S(2)}, u32[]{:S(2)}) collective-permute-start(bf16[512,1024]{1,0:T(8,128)(2,1)} %bitcast.40), channel_id=1, source_target_pairs={{0,1},{1,0},{2,3},{3,2},{4,5},{5,4},{6,7},{7,6},{8,9},{9,8},{10,11... | collective-permute-start | bytes 3145736 | tf_op jit(solution)/shard_map/ppermute | solution.py:285
  545.1 68.6 %collective-permute-start.8 = (bf16[2,512,1024]{2,1,0:T(8,128)(2,1)}, bf16[2,512,1024]{2,1,0:T(8,128)(2,1)}, u32[]{:S(2)}, u32[]{:S(2)}) collective-permute-start(bf16[2,512,1024]{2,1,0:T(8,128)(2,1)} %add_convert_fusion.4), channel_id=1, source_target_pairs={{1,0},{2,1},{3,2},{5,4},{6,5},{7,6},{9,8},{10,9},{11,10},{13,12},{... | collective-permute-start | bytes 6291464 | tf_op jit(solution)/shard_map/ppermute | solution.py:514
  560.4 24.9 %collective-permute-start.14 = (bf16[256,2048]{1,0:T(8,128)(2,1)S(1)}, bf16[256,2048]{1,0:T(8,128)(2,1)S(1)}, u32[]{:S(2)}, u32[]{:S(2)}) collective-permute-start(bf16[256,2048]{1,0:T(8,128)(2,1)S(1)} %get-tuple-element.392), channel_id=1, source_target_pairs={{0,16},{4,20},{8,24},{12,28},{16,0},{20,4},{24,8},{28,12},{1,17},{... | collective-permute-start | bytes 3145736 | tf_op jit(solution)/shard_map/ppermute | solution.py:285
  561.3 25.4 %collective-permute-start.13 = (bf16[256,2048]{1,0:T(8,128)(2,1)S(1)}, bf16[256,2048]{1,0:T(8,128)(2,1)S(1)}, u32[]{:S(2)}, u32[]{:S(2)}) collective-permute-start(bf16[256,2048]{1,0:T(8,128)(2,1)S(1)} %bitcast.264), channel_id=1, source_target_pairs={{0,8},{4,12},{8,0},{12,4},{16,24},{20,28},{24,16},{28,20},{1,9},{5... | collective-permute-start | bytes 3145736 | tf_op jit(solution)/shard_map/ppermute | solution.py:285
  592.2 22.5 %collective-permute-start.15 = (f32[22544]{0:T(1024)S(1)}, f32[22544]{0:T(1024)S(1)}, u32[]{:S(2)}, u32[]{:S(2)}) collective-permute-start(f32[22544]{0:T(1024)S(1)} %concatenate.58), channel_id=1, source_target_pairs={{0,4},{4,0},{8,12},{12,8},{16,20},{20,16},{24,28},{28,24},{1,5},{5... | collective-permute-start | bytes 270536 | tf_op jit(solution)/shard_map/ppermute | solution.py:285
  592.3 28.3 %collective-permute-start.17 = (bf16[128,2048]{1,0:T(8,128)(2,1)}, bf16[128,2048]{1,0:T(8,128)(2,1)S(1)}, u32[]{:S(2)}, u32[]{:S(2)}) collective-permute-start(bf16[128,2048]{1,0:T(8,128)(2,1)} %get-tuple-element.415), channel_id=1, source_target_pairs={{0,8},{4,12},{8,0},{12,4},{16,24},{20,28},{24,16},{28,20},{1,9},{5... | collective-permute-start | bytes 1572872 | tf_op jit(solution)/shard_map/ppermute | solution.py:285
  594.4 26.2 %collective-permute-start.18 = (bf16[128,2048]{1,0:T(8,128)(2,1)}, bf16[128,2048]{1,0:T(8,128)(2,1)S(1)}, u32[]{:S(2)}, u32[]{:S(2)}) collective-permute-start(bf16[128,2048]{1,0:T(8,128)(2,1)} %get-tuple-element.420), channel_id=1, source_target_pairs={{0,16},{4,20},{8,24},{12,28},{16,0},{20,4},{24,8},{28,12},{1,17},{... | collective-permute-start | bytes 1572872 | tf_op jit(solution)/shard_map/ppermute | solution.py:285
  613.7 50.4 %collective-permute-start.22 = (bf16[256,1024]{1,0:T(8,128)(2,1)}, bf16[256,1024]{1,0:T(8,128)(2,1)S(1)}, u32[]{:S(2)}, u32[]{:S(2)}) collective-permute-start(bf16[256,1024]{1,0:T(8,128)(2,1)} %get-tuple-element.448), channel_id=1, source_target_pairs={{0,2},{1,3},{2,0},{3,1},{4,6},{5,7},{6,4},{7,5},{8,10},{9,11},{10,... | collective-permute-start | bytes 1572872 | tf_op jit(solution)/shard_map/ppermute | solution.py:285
  626.8 24.7 %collective-permute-start.20 = (bf16[128,2048]{1,0:T(8,128)(2,1)S(1)}, bf16[128,2048]{1,0:T(8,128)(2,1)S(1)}, u32[]{:S(2)}, u32[]{:S(2)}) collective-permute-start(bf16[128,2048]{1,0:T(8,128)(2,1)S(1)} %bitcast.269), channel_id=1, source_target_pairs={{0,1},{1,0},{2,3},{3,2},{4,5},{5,4},{6,7},{7,6},{8,9},{9,8},{10,11... | collective-permute-start | bytes 1572872 | tf_op jit(solution)/shard_map/ppermute | solution.py:285
  628.2 23.4 %collective-permute-start.23 = (f32[22544]{0:T(1024)S(1)}, f32[22544]{0:T(1024)S(1)}, u32[]{:S(2)}, u32[]{:S(2)}) collective-permute-start(f32[22544]{0:T(1024)S(1)} %add.442), channel_id=1, source_target_pairs={{0,1},{1,0},{2,3},{3,2},{4,5},{5,4},{6,7},{7,6},{8,9},{9,8},{10,11... | collective-permute-start | bytes 270536 | tf_op jit(solution)/shard_map/ppermute | solution.py:285
  651.8 17.7 %collective-permute-start.21 = (bf16[64,2048]{1,0:T(8,128)(2,1)S(1)}, bf16[64,2048]{1,0:T(8,128)(2,1)S(1)}, u32[]{:S(2)}, u32[]{:S(2)}) collective-permute-start(bf16[64,2048]{1,0:T(8,128)(2,1)S(1)} %get-tuple-element.446), channel_id=1, source_target_pairs={{0,2},{1,3},{2,0},{3,1},{4,6},{5,7},{6,4},{7,5},{8,10},{9,11},{10,... | collective-permute-start | bytes 786440 | tf_op jit(solution)/shard_map/ppermute | solution.py:285
  (103 other events, 695.6 us)
Sparse Core Ops, SparseCore 0:
  11.5 85.0 all-gather.3
  100.0 89.0 all-gather.5
  192.0 75.7 all-gather.7

commit v7 on v6

--- a/solution.py
+++ b/solution.py
@@ -350,11 +350,9 @@
         self.came = came
 
     def step(self, sequence):
-        if callable(self.kept):
-            came, kept = sequence(self.came), self.kept()
-        else:
-            came, kept = sequence(self.came, self.kept)
-        total = kept.astype(jnp.float32) + came.astype(jnp.float32)
+        came, kept = sequence(self.came), self.kept()
+        total = kept.astype(jnp.float32) + came.reshape(kept.shape).astype(jnp.float32)
+        total = total.reshape(-1, total.shape[-1])
         if not self.order:
             self.total = total
             return
@@ -368,9 +366,9 @@
         columns = total.shape[-1]
         split = total.reshape(1 << at, 2, -1, columns)
         mine = (lax.axis_index(axis) >> bit) & 1
-        gone = lax.dynamic_index_in_dim(split, 1 - mine, 1, keepdims=False).reshape(-1, columns)
-        kept = lax.dynamic_index_in_dim(split, mine, 1, keepdims=False).reshape(-1, columns)
-        gone, self.kept = sequence(gone, kept)
+        take = lambda rows, index: lax.dynamic_index_in_dim(rows, index, 1, keepdims=False)
+        gone, split = sequence(take(split, 1 - mine).reshape(-1, columns), split)
+        self.kept = lambda: take(split, mine)
         self.came = exchange(gone, axis, bit)
 
 
@@ -443,9 +441,9 @@
     keys = [stacked(projected[:, model : 2 * model].astype(jnp.bfloat16))]
     values = [stacked((projected[:, 2 * model :] + value_bias).astype(jnp.bfloat16))]
     core, *planes = bits_of("dp")
-    normed_pieces, hats, picked = [normed], [hat_one], [pick_columns(normed, core)]
+    normed_pieces, hats = [normed], [hat_one]
     for halo in halos:
-        halo, query, keys[-1], values[-1], picked[-1] = together(halo, query, keys[-1], values[-1], picked[-1])
+        halo, query, keys[-1], values[-1] = together(halo, query, keys[-1], values[-1])
         hat, _ = moments(flat(halo).astype(jnp.float32))
         piece = (hat * first_gain + first_shift).astype(jnp.bfloat16)
         normed_pieces.append(piece)
@@ -453,10 +451,10 @@
         both = dot_nn(piece, inward[:, model:])
         keys.append(stacked(both[:, :model].astype(jnp.bfloat16)))
         values.append(stacked((both[:, model:] + value_bias).astype(jnp.bfloat16)))
-        picked.append(pick_columns(piece, core))
     scaled, lse = attend(first, head_scale, query, keys, values, start, hops)
 
-    scaled_low = flat(scaled)
+    scaled_low, *normed_pieces = together(flat(scaled), *normed_pieces)
+    picked = [pick_columns(piece, core) for piece in normed_pieces]
     branch = dot_nn(scaled_low, output_full) + output_bias
     hat_post, scale_post = moments(branch)
     middle = tokens + hat_post * post_gain + post_shift
@@ -464,7 +462,11 @@
     second = (hat_two * second_gain + second_shift).astype(jnp.bfloat16)
     upper = dot_nn(second, up_full) + up_bias
     phi = 0.5 * (1.0 + lax.erf(upper * 0.7071067811865476))
-    hat_middle, scale_middle = moments(upper * phi)
+    bent = upper * phi
+    bent_mean = jnp.mean(bent, -1, keepdims=True)
+    bent_spread = jnp.maximum(jnp.mean(bent * bent, -1, keepdims=True) - bent_mean * bent_mean, 0.0)
+    scale_middle = lax.rsqrt(bent_spread + EPSILON)
+    hat_middle = (bent - bent_mean) * scale_middle
     mixed = (hat_middle * middle_gain + middle_shift).astype(jnp.bfloat16)
     grad_low = flat(cotangent)
     grad_out = grad_low.astype(jnp.float32)
@@ -473,22 +475,15 @@
     down_sum, up_sum = RowSum(one_way), RowSum(other_way)
     sums = query_key_sum, value_output_sum = RowSum(one_way), RowSum(other_way)
     sequence = Sequence(jnp.zeros((8, 128), jnp.float32))
-    other_mixed, own_mixed = pick_columns(mixed, core)
-    sent, own_mixed, low = sequence(dot_tn(other_mixed, grad_low).astype(jnp.bfloat16), own_mixed, grad_low)
-    down_sum.begin(exchange(sent, *core))
-    down_sum.kept = lambda: dot_tn(own_mixed, sequence(low))
-    down_sum.step(sequence)
-
-    low = sequence(low)
+    down_sum.send(dot_tn(mixed, grad_low), sequence)
+
+    low = sequence(grad_low)
     grad_mixed = dot_nt(low, down_full)
     slope = phi + upper * (0.3989422804014327 * jnp.exp(-0.5 * upper * upper))
     grad_upper = (norm_back(hat_middle, scale_middle, middle_gain, grad_mixed) * slope).astype(jnp.bfloat16)
-    other_second, own_second = pick_columns(second, core)
     grad_upper = sequence(grad_upper)
-    sent = dot_tn(other_second, grad_upper).astype(jnp.bfloat16)
-    sent, grad_upper = sequence(sent, grad_upper)
-    up_sum.begin(exchange(sent, *core))
-    up_sum.kept = lambda: dot_tn(own_second, sequence(grad_upper))
+    down_sum.step(sequence)
+    up_sum.send(dot_tn(second, sequence(grad_upper)), sequence)
     grad_upper = sequence(grad_upper)
     grad_second = sequence(dot_nt(grad_upper, up_full))
     up_sum.step(sequence)
@@ -589,7 +584,7 @@
             jnp.sum(grad_mixed, 0),
         ]
     )
-    places = bits_of("dp") + bits_of("seq")
+    places = bits_of("seq") + bits_of("dp")
     vector = sequence(vector)
     vector_came = exchange(vector, *places.pop(0))
 

time: 691 us -> 702 us (1.016)
  waiting for transfers between devices: 196 us -> 236 us
  local copies, waits for them, and re-layouts: 35.1 us -> 52.8 us
  other arithmetic: 116 us -> 101 us
  starting transfers between devices: 51.3 us -> 38 us
  Pallas kernels: 102 us -> 90.6 us
    all_gather x1, waiting for transfers between devices: 0.01 us -> 24.9 us  [local(): down_full = lax.all_gather(down_weight, BOTH, axis=0, tiled=True)]
    ppermute x20, starting transfers between devices: 31.5 us -> 18.3 us  [exchange(): lax.ppermute(array, axis, [(i, i ^ 1 << bit) for i in range(lax.axis_size...]
    pallas_call x6 -> x4, Pallas kernels: 27.9 us -> 15.9 us  [pick_columns(): pl.pallas_call(pick_kernel, grid_spec=pltpu.PrefetchScalarGridSpec(num_sc...]
    dynamic_slice x3 -> x11, local copies, waits for them, and re-layouts: 6.28 us -> 17.8 us  [send(): lax.dynamic_index_in_dim(rows, index, 1, keepdims=False)]
    dot_general x20 -> x18, matrix products: 50 us -> 41.3 us  [dot_tn(): lax.dot_general(a, b, (((0,), (0,)), ((), ())), preferred_element_type=jn...]
    all_gather x1, waiting for transfers between devices: 17.6 us -> 25.7 us  [local(): lax.all_gather(jnp.concatenate([output_weight, up_weight], 1), BOTH, axis...]
    reduce_sum x6 -> x5, other arithmetic: 10.7 us -> 3.08 us  [moments(): spread = jnp.mean(centred * centred, -1, keepdims=True)]
    unnamed x206 -> x202, local copies, waits for them, and re-layouts: 8.48 us -> 14.5 us
  transfers between devices with their start and end apart: 28 -> 28, of which waited for: 11 -> 12; matrix products, arithmetic and copies ran while one was open for 37% -> 39% of each run, Pallas kernels for 15% -> 13%
where the time goes in v7:
time: 702 us; the launch traced here: 698 us
  waiting for transfers between devices  236 us (34%)
  matrix products  164 us (23%)
  other arithmetic  101 us (14%)
  Pallas kernels  90.6 us (13%)
  local copies, waits for them, and re-layouts  52.8 us (8%)
  starting transfers between devices  38 us (5%)
  between operations  15.8 us (2%)
    ppermute x2, waiting for transfers between devices, local(): lower = lambda array: lax.ppermute(array, 'seq', downward)  81.8 us
    dot_general x10, matrix products, dot_nt(): lax.dot_general(a, b, (((1,), (1,)), ((), ())), preferred_element_type=jn...  68 us
    ppermute x3, waiting for transfers between devices, local(): shift = lambda array: lax.ppermute(array, 'seq', upward)  60.7 us
    dot_general x6, matrix products, dot_nn(): lax.dot_general(a, b, (((1,), (0,)), ((), ())), preferred_element_type=jn...  54.2 us
    pallas_call x1, Pallas kernels, attend_back(): pl.pallas_call(kernel, grid_spec=pltpu.PrefetchScalarGridSpec(num_scalar_...  44.8 us
    ppermute x20, waiting for transfers between devices, exchange(): lax.ppermute(array, axis, [(i, i ^ 1 << bit) for i in range(lax.axis_size...  42.5 us
    dot_general x18, matrix products, dot_tn(): lax.dot_general(a, b, (((0,), (0,)), ((), ())), preferred_element_type=jn...  41.3 us
    pallas_call x1, Pallas kernels, attend(): pl.pallas_call(kernel, grid_spec=pltpu.PrefetchScalarGridSpec(num_scalar_...  29.9 us
  transfers between devices with their start and end apart: 28, of which 12 were waited for; matrix products, arithmetic and copies ran while one was open for 39% of the time, Pallas kernels for 13%

profile of v7, /device:TPU:0, one launch (start us, length us, event | category | flops | bytes accessed | tf_op | source)
XLA Modules:
  0.0 697.7 jit_solution(809082541642651223)
XLA Ops:
  12.2 6.0 collective-permute-start
  20.7 32.6 %collective-permute-done = bf16[2,288,1024]{2,1,0:T(8,128)(2,1)} collective-permute-done((bf16[2,288,1024]{2,1,0:T(8,128)(2,1)S(1)}, bf16[2,288,1024]{2,1,0:T(8,128)(2,1)}, u32[]{:S(2)}, u32[]{:S(2)}) %collective-permute-start) | collective-permute-done | bytes 1179680 | tf_op jit(solution)/shard_map/ppermute | solution.py:412
  53.2 6.3 collective-permute-start.2
  68.3 28.1 %collective-permute-done.2 = bf16[2,224,1024]{2,1,0:T(8,128)(2,1)} collective-permute-done((bf16[2,224,1024]{2,1,0:T(8,128)(2,1)}, bf16[2,224,1024]{2,1,0:T(8,128)(2,1)}, u32[]{:S(2)}, u32[]{:S(2)}) %collective-permute-start.2) | collective-permute-done | bytes 917536 | tf_op jit(solution)/shard_map/ppermute | solution.py:412
  99.5 9.4 %fusion.85 = f32[1024,3072]{1,0:T(8,128)S(1)} fusion(bf16[1024,1024]{1,0:T(8,128)(2,1)} %fusion.28.array_ref, bf16[1024,3072]{1,0:T(8,128)(2,1)} %all-gather.4.cloned.1.call-done), kind=kOutput, calls=%fused_computation.231 | convolution fusion | flops 6442450944 | bytes 20971520 | tf_op jit(solution)/shard_map/dot_general | solution.py:19
  133.7 29.9 %attend.1 = (bf16[2,512,1024]{2,1,0:T(8,128)(2,1)}, f32[2,4,4,512]{3,2,1,0:T(4,128)}) custom-call(s32[2,2]{1,0:T(2,128)} %slice.180.first_ref, f32[16]{0:T(128)} %scale_ref.3, bf16[2,512,1024]{2,1,0:T(8,128)(2,1)} %bitcast.312, bf16[2,512,1024]{2,1,0:T(8,128)(2,1)} %bitcast.306, bf16[2,512,1024]{2,1,0:T(8,128)(2,1)} %bitcast.308, ...), custom_call_target="tpu_custom_call" | custom-call | flops 33017561088 | bytes 32243712 | tf_op jit(solution)/shard_map/attend/pallas_call | solution.py:142
  163.6 25.7 %all-gather.6.cloned.1.call-done = bf16[1024,5120]{1,0:T(8,128)(2,1)} async-done(((bf16[32,5120]{1,0:T(8,128)(2,1)}), bf16[1024,5120]{1,0:T(8,128)(2,1)}) %all-gather.6.cloned.1.call-update) | async-done | bytes 10485776 | tf_op jit(solution)/shard_map/all_gather | solution.py:425
  199.2 20.7 %multiply_reduce_fusion.2 = (f32[1024]{0:T(1024)S(1)}, f32[1024]{0:T(1024)S(1)}, f32[1024,4096]{1,0:T(8,128)}, f32[1024,4096]{1,0:T(8,128)}) fusion(f32[4096]{0:T(1024)S(1)} %copy-done.80, bf16[1024,5120]{1,0:T(8,128)(2,1)} %all-gather.6.cloned.1.call-done, f32[1024,1024]{1,0:T(8,128)} %copy-done.2, f32[1024]{0:T(1024)S(1)} %copy-done.85, ...), kind=kOutput, calls=%fused_computation.12 | convolution fusion | flops 8628729856 | bytes 46178304 | tf_op jit(solution)/shard_map/dot_general | solution.py:19
  219.9 7.9 %add_convert_fusion = bf16[1024,4096]{1,0:T(8,128)(2,1)S(1)} fusion(f32[1024,4096]{1,0:T(8,128)} %get-tuple-element.447, f32[4096]{0:T(1024)S(1)} %copy-done.79, f32[1024]{0:T(1024)S(1)} %get-tuple-element.485, f32[4096]{0:T(1024)S(1)} %copy-done.57, f32[1024]{0:T(1024)S(1)} %get-tuple-element.484), kind=kLoop, calls=%fused_computation.10 | loop fusion | flops 20971520 | bytes 25206784 | tf_op jit(solution)/shard_map/convert_element_type | solution.py:470
  227.8 9.6 %convolution_convert_fusion.1 = bf16[4096,1024]{1,0:T(8,128)(2,1)S(1)} fusion(bf16[1024,4096]{1,0:T(8,128)(2,1)S(1)} %add_convert_fusion, bf16[1024,1024]{1,0:T(8,128)(2,1)S(1)} %bitcast.270), kind=kOutput, calls=%fused_computation.22 | convolution fusion | flops 8594128896 | bytes 18874368 | tf_op jit(solution)/shard_map/dot_general | solution.py:27
  243.0 24.9 %all-gather.8.cloned.1.call-done = bf16[4096,1024]{1,0:T(8,128)(2,1)} async-done(((bf16[128,1024]{1,0:T(8,128)(2,1)}), bf16[4096,1024]{1,0:T(8,128)(2,1)}) %all-gather.8.cloned.1.call-update) | async-done | bytes 8388624 | tf_op jit(solution)/shard_map/all_gather | solution.py:426
  267.8 20.7 %multiply_reduce_fusion = (f32[4096]{0:T(1024)}, f32[1024]{0:T(1024)S(1)}, f32[1024]{0:T(1024)S(1)}, f32[4096]{0:T(1024)}, f32[1024,4096]{1,0:T(8,128)}) fusion(f32[1024,4096]{1,0:T(8,128)} %get-tuple-element.447, f32[1024]{0:T(1024)S(1)} %get-tuple-element.485, f32[1024]{0:T(1024)S(1)} %get-tuple-element.484, f32[4096]{0:T(1024)S(1)} %copy-done.57, ...), kind=kOutput, calls=%fused_computation.7 | convolution fusion | flops 8627673088 | bytes 44105728 | tf_op jit(solution)/shard_map/dot_general | solution.py:23
  288.5 17.6 %fusion.5 = bf16[1024,4096]{1,0:T(8,128)(2,1)S(1)} fusion(f32[1024,4096]{1,0:T(8,128)} %get-tuple-element.493, f32[1024,4096]{1,0:T(8,128)} %get-tuple-element.492, f32[1024,4096]{1,0:T(8,128)} %get-tuple-element.447, f32[1024]{0:T(1024)S(1)} %get-tuple-element.496, f32[1024]{0:T(1024)S(1)} %get-tuple-element.497, f32[1024]{0:T(1024)S(1)} %get-tuple-element.485, ...), kind=kLoop, calls=%fused_computation.6 | loop fusion | flops 75497472 | bytes 58769408 | tf_op jit(solution)/shard_map/convert_element_type | solution.py:483
  320.6 12.3 %convolution_convert_fusion = bf16[1024,4096]{1,0:T(8,128)(2,1)} fusion(bf16[1024,4096]{1,0:T(8,128)(2,1)S(1)} %fusion.5, f32[1024,1024]{1,0:T(8,128)S(1)} %copy-done.3, f32[1024]{0:T(1024)S(1)} %copy-done.85, f32[1024]{0:T(1024)S(1)} %copy-done.63, f32[1024]{0:T(1024)S(1)} %add_rsqrt_fusion.1, f32[1024]{0:T(1024)S(1)} %broadcast_multiply_fusion.9), kind=kOutput, calls=%fused_computation.21 | convolution fusion | flops 8599371776 | bytes 20987904 | tf_op jit(solution)/shard_map/dot_general | solution.py:27
  356.5 12.8 %fusion.8 = f32[1024,1024]{1,0:T(8,128)S(1)} fusion(bf16[1024,4096]{1,0:T(8,128)(2,1)} %copy-done.12, bf16[1024,5120]{1,0:T(8,128)(2,1)} %all-gather.6.cloned.1.call-done), kind=kOutput, calls=%fused_computation.23 | convolution fusion | flops 8589934592 | bytes 20971520 | tf_op jit(solution)/shard_map/dot_general | solution.py:23
  402.6 44.8 %attend_back.1 = (bf16[2,512,1024]{2,1,0:T(8,128)(2,1)}, bf16[2,512,1024]{2,1,0:T(8,128)(2,1)}, bf16[2,512,1024]{2,1,0:T(8,128)(2,1)}, bf16[2,288,1024]{2,1,0:T(...) custom-call(s32[2,2]{1,0:T(2,128)} %slice.180.first_ref, ...), custom_call_target="tpu_custom_call" | custom-call | flops 55029268480 | bytes 53739520 | tf_op jit(solution)/shard_map/attend_back/pallas_call | solution.py:239
  470.3 67.0 %collective-permute-done.7 = bf16[2,288,1024]{2,1,0:T(8,128)(2,1)S(1)} collective-permute-done((bf16[2,288,1024]{2,1,0:T(8,128)(2,1)S(1)}, bf16[2,288,1024]{2,1,0:T(8,128)(2,1)S(1)}, u32[]{:S(2)}, u32[]{:S(2)}) %collective-permute-start.7) | collective-permute-done | bytes 1179680 | tf_op jit(solution)/shard_map/ppermute | solution.py:509
  573.0 6.1 fusion.42
  583.7 5.9 add_add_fusion
  590.1 7.2 %collective-permute-done.14 = bf16[256,2048]{1,0:T(8,128)(2,1)S(1)} collective-permute-done((bf16[256,2048]{1,0:T(8,128)(2,1)S(1)}, bf16[256,2048]{1,0:T(8,128)(2,1)S(1)}, u32[]{:S(2)}, u32[]{:S(2)}) %collective-permute-start.14) | collective-permute-done | bytes 1048608 | tf_op jit(solution)/shard_map/ppermute | solution.py:285
  608.4 14.7 %collective-permute-done.8 = bf16[2,512,1024]{2,1,0:T(8,128)(2,1)} collective-permute-done((bf16[2,512,1024]{2,1,0:T(8,128)(2,1)}, bf16[2,512,1024]{2,1,0:T(8,128)(2,1)}, u32[]{:S(2)}, u32[]{:S(2)}) %collective-permute-start.8) | collective-permute-done | bytes 2097184 | tf_op jit(solution)/shard_map/ppermute | solution.py:509
  630.0 21.6 %collective-permute-done.16 = f32[22544]{0:T(1024)S(1)} collective-permute-done((f32[22544]{0:T(1024)S(1)}, f32[22544]{0:T(1024)S(1)}, u32[]{:S(2)}, u32[]{:S(2)}) %collective-permute-start.16) | collective-permute-done | bytes 90208 | tf_op jit(solution)/shard_map/ppermute | solution.py:285
  658.8 10.0 %add_convert_fusion.1 = bf16[1024,1024]{1,0:T(8,128)(2,1)} fusion(f32[1024,1024]{1,0:T(8,128)S(1)} %copy-done.5, f32[1024]{0:T(1024)S(1)} %copy-done.86, bf16[1024,4096]{1,0:T(8,128)(2,1)S(1)} %bitcast.265, bf16[4096,1024]{1,0:T(8,128)(2,1)S(1)} %bitcast.341), kind=kOutput, calls=%fused_computation.67 | convolution fusion | flops 8593080320 | bytes 23072768 | tf_op jit(solution)/shard_map/dot_general | solution.py:19
  678.7 7.6 %collective-permute-done.21 = bf16[64,2048]{1,0:T(8,128)(2,1)S(1)} collective-permute-done((bf16[64,2048]{1,0:T(8,128)(2,1)S(1)}, bf16[64,2048]{1,0:T(8,128)(2,1)S(1)}, u32[]{:S(2)}, u32[]{:S(2)}) %collective-permute-start.21) | collective-permute-done | bytes 262176 | tf_op jit(solution)/shard_map/ppermute | solution.py:285
  (414 shorter events, 232.5 us)
Async XLA Ops:
  7.2 92.3 %all-gather.4.cloned.1.call-start = ((), (), s32[]{:S(2)}) async-start(), calls=%async_computation | async-start | bytes 6488064 | tf_op jit(solution)/shard_map/all_gather | solution.py:424
  9.0 180.3 %all-gather.6.cloned.1.call-start = ((), (), s32[]{:S(2)}) async-start(), calls=%async_computation.1 | async-start | bytes 10813440 | tf_op jit(solution)/shard_map/all_gather | solution.py:425
  10.8 257.0 %all-gather.8.cloned.1.call-start = ((), (), s32[]{:S(2)}) async-start(), calls=%async_computation.2 | async-start | bytes 8650752 | tf_op jit(solution)/shard_map/all_gather | solution.py:426
  12.2 41.0 %collective-permute-start = (bf16[2,288,1024]{2,1,0:T(8,128)(2,1)S(1)}, bf16[2,288,1024]{2,1,0:T(8,128)(2,1)}, u32[]{:S(2)}, u32[]{:S(2)}) collective-permute-start(bf16[2,288,1024]{2,1,0:T(8,128)(2,1)S(1)} %slice.182), channel_id=1, source_target_pairs={{0,1},{1,2},{2,3},{4,5},{5,6},{6,7},{8,9},{9,10},{10,11},{12,13},{... | collective-permute-start | bytes 3538952 | tf_op jit(solution)/shard_map/ppermute | solution.py:412
  53.2 43.2 %collective-permute-start.2 = (bf16[2,224,1024]{2,1,0:T(8,128)(2,1)}, bf16[2,224,1024]{2,1,0:T(8,128)(2,1)}, u32[]{:S(2)}, u32[]{:S(2)}) collective-permute-start(bf16[2,224,1024]{2,1,0:T(8,128)(2,1)} %slice.181), channel_id=1, source_target_pairs={{0,1},{1,2},{2,3},{4,5},{5,6},{6,7},{8,9},{9,10},{10,11},{12,13},{... | collective-permute-start | bytes 2752520 | tf_op jit(solution)/shard_map/ppermute | solution.py:412
  64.2 60.5 %collective-permute-start.1 = (bf16[2,288,1024]{2,1,0:T(8,128)(2,1)}, bf16[2,288,1024]{2,1,0:T(8,128)(2,1)S(1)}, u32[]{:S(2)}, u32[]{:S(2)}) collective-permute-start(bf16[2,288,1024]{2,1,0:T(8,128)(2,1)} %collective-permute-done), channel_id=1, source_target_pairs={{0,1},{1,2},{2,3},{4,5},{5,6},{6,7},{8,9},{9,10},{10,11},{12,13},{... | collective-permute-start | bytes 3538952 | tf_op jit(solution)/shard_map/ppermute | solution.py:412
  242.6 69.3 %collective-permute-start.3 = (bf16[2048,1024]{1,0:T(8,128)(2,1)}, bf16[2048,1024]{1,0:T(8,128)(2,1)}, u32[]{:S(2)}, u32[]{:S(2)}) collective-permute-start(bf16[2048,1024]{1,0:T(8,128)(2,1)} %bitcast.13), channel_id=1, source_target_pairs={{0,4},{4,0},{8,12},{12,8},{16,20},{20,16},{24,28},{28,24},{1,5},{5... | collective-permute-start | bytes 12582920 | tf_op jit(solution)/shard_map/ppermute | solution.py:285
  337.8 39.3 %collective-permute-start.4 = (bf16[512,4096]{1,0:T(8,128)(2,1)}, bf16[512,4096]{1,0:T(8,128)(2,1)}, u32[]{:S(2)}, u32[]{:S(2)}) collective-permute-start(bf16[512,4096]{1,0:T(8,128)(2,1)} %bitcast.18), channel_id=1, source_target_pairs={{0,4},{4,0},{8,12},{12,8},{16,20},{20,16},{24,28},{28,24},{1,5},{5... | collective-permute-start | bytes 12582920 | tf_op jit(solution)/shard_map/ppermute | solution.py:285
  355.1 92.3 %collective-permute-start.6 = (bf16[1024,1024]{1,0:T(8,128)(2,1)}, bf16[1024,1024]{1,0:T(8,128)(2,1)}, u32[]{:S(2)}, u32[]{:S(2)}) collective-permute-start(bf16[1024,1024]{1,0:T(8,128)(2,1)} %dynamic-slice_bitcast_fusion), channel_id=1, source_target_pairs={{0,16},{4,20},{8,24},{12,28},{16,0},{20,4},{24,8},{28,12},{1,17},{... | collective-permute-start | bytes 6291464 | tf_op jit(solution)/shard_map/ppermute | solution.py:285
  402.1 50.8 %collective-permute-start.5 = (bf16[256,4096]{1,0:T(8,128)(2,1)}, bf16[256,4096]{1,0:T(8,128)(2,1)}, u32[]{:S(2)}, u32[]{:S(2)}) collective-permute-start(bf16[256,4096]{1,0:T(8,128)(2,1)} %bitcast.21), channel_id=1, source_target_pairs={{0,8},{4,12},{8,0},{12,4},{16,24},{20,28},{24,16},{28,20},{1,9},{5... | collective-permute-start | bytes 6291464 | tf_op jit(solution)/shard_map/ppermute | solution.py:285
  451.1 98.6 %collective-permute-start.9 = (bf16[512,1024]{1,0:T(8,128)(2,1)S(1)}, bf16[512,1024]{1,0:T(8,128)(2,1)S(1)}, u32[]{:S(2)}, u32[]{:S(2)}) collective-permute-start(bf16[512,1024]{1,0:T(8,128)(2,1)S(1)} %dynamic-slice_bitcast_fusion.3), channel_id=1, source_target_pairs={{0,8},{4,12},{8,0},{12,4},{16,24},{20,28},{24,16},{28,20},{1,9},{5... | collective-permute-start | bytes 3145736 | tf_op jit(solution)/shard_map/ppermute | solution.py:285
  455.5 94.2 %collective-permute-start.10 = (bf16[128,4096]{1,0:T(8,128)(2,1)S(1)}, bf16[128,4096]{1,0:T(8,128)(2,1)}, u32[]{:S(2)}, u32[]{:S(2)}) collective-permute-start(bf16[128,4096]{1,0:T(8,128)(2,1)S(1)} %dynamic-slice_bitcast_fusion.2), channel_id=1, source_target_pairs={{0,16},{4,20},{8,24},{12,28},{16,0},{20,4},{24,8},{28,12},{1,17},{... | collective-permute-start | bytes 3145736 | tf_op jit(solution)/shard_map/ppermute | solution.py:285
  459.4 78.0 %collective-permute-start.7 = (bf16[2,288,1024]{2,1,0:T(8,128)(2,1)S(1)}, bf16[2,288,1024]{2,1,0:T(8,128)(2,1)S(1)}, u32[]{:S(2)}, u32[]{:S(2)}) collective-permute-start(bf16[2,288,1024]{2,1,0:T(8,128)(2,1)S(1)} %bitcast.348), channel_id=1, source_target_pairs={{1,0},{2,1},{3,2},{5,4},{6,5},{7,6},{9,8},{10,9},{11,10},{13,12},{... | collective-permute-start | bytes 3538952 | tf_op jit(solution)/shard_map/ppermute | solution.py:509
  551.8 14.5 %collective-permute-start.11 = (bf16[512,4096]{1,0:T(8,128)(2,1)S(1)}, bf16[512,4096]{1,0:T(8,128)(2,1)}, u32[]{:S(2)}, u32[]{:S(2)}) collective-permute-start(bf16[512,4096]{1,0:T(8,128)(2,1)S(1)} %pad_maximum_fusion), channel_id=1, source_target_pairs={{0,4},{4,0},{8,12},{12,8},{16,20},{20,16},{24,28},{28,24},{1,5},{5... | collective-permute-start | bytes 12582920 | tf_op jit(solution)/shard_map/ppermute | solution.py:285
  552.1 47.9 %collective-permute-start.12 = (bf16[512,1024]{1,0:T(8,128)(2,1)S(1)}, bf16[512,1024]{1,0:T(8,128)(2,1)}, u32[]{:S(2)}, u32[]{:S(2)}) collective-permute-start(bf16[512,1024]{1,0:T(8,128)(2,1)S(1)} %bitcast.321), channel_id=1, source_target_pairs={{0,1},{1,0},{2,3},{3,2},{4,5},{5,4},{6,7},{7,6},{8,9},{9,8},{10,11... | collective-permute-start | bytes 3145736 | tf_op jit(solution)/shard_map/ppermute | solution.py:285
  553.9 69.3 %collective-permute-start.8 = (bf16[2,512,1024]{2,1,0:T(8,128)(2,1)}, bf16[2,512,1024]{2,1,0:T(8,128)(2,1)}, u32[]{:S(2)}, u32[]{:S(2)}) collective-permute-start(bf16[2,512,1024]{2,1,0:T(8,128)(2,1)} %add_convert_fusion.2), channel_id=1, source_target_pairs={{1,0},{2,1},{3,2},{5,4},{6,5},{7,6},{9,8},{10,9},{11,10},{13,12},{... | collective-permute-start | bytes 6291464 | tf_op jit(solution)/shard_map/ppermute | solution.py:509
  570.9 27.7 %collective-permute-start.13 = (bf16[256,2048]{1,0:T(8,128)(2,1)S(1)}, bf16[256,2048]{1,0:T(8,128)(2,1)S(1)}, u32[]{:S(2)}, u32[]{:S(2)}) collective-permute-start(bf16[256,2048]{1,0:T(8,128)(2,1)S(1)} %bitcast.322), channel_id=1, source_target_pairs={{0,8},{4,12},{8,0},{12,4},{16,24},{20,28},{24,16},{28,20},{1,9},{5... | collective-permute-start | bytes 3145736 | tf_op jit(solution)/shard_map/ppermute | solution.py:285
  572.3 25.0 %collective-permute-start.14 = (bf16[256,2048]{1,0:T(8,128)(2,1)S(1)}, bf16[256,2048]{1,0:T(8,128)(2,1)S(1)}, u32[]{:S(2)}, u32[]{:S(2)}) collective-permute-start(bf16[256,2048]{1,0:T(8,128)(2,1)S(1)} %dynamic-slice_bitcast_fusion.1), channel_id=1, source_target_pairs={{0,16},{4,20},{8,24},{12,28},{16,0},{20,4},{24,8},{28,12},{1,17},{... | collective-permute-start | bytes 3145736 | tf_op jit(solution)/shard_map/ppermute | solution.py:285
  603.9 20.7 %collective-permute-start.15 = (f32[22544]{0:T(1024)S(1)}, f32[22544]{0:T(1024)S(1)}, u32[]{:S(2)}, u32[]{:S(2)}) collective-permute-start(f32[22544]{0:T(1024)S(1)} %concatenate.51), channel_id=1, source_target_pairs={{0,1},{1,0},{2,3},{3,2},{4,5},{5,4},{6,7},{7,6},{8,9},{9,8},{10,11... | collective-permute-start | bytes 270536 | tf_op jit(solution)/shard_map/ppermute | solution.py:285
  606.4 45.2 %collective-permute-start.17 = (bf16[128,2048]{1,0:T(8,128)(2,1)}, bf16[128,2048]{1,0:T(8,128)(2,1)S(1)}, u32[]{:S(2)}, u32[]{:S(2)}) collective-permute-start(bf16[128,2048]{1,0:T(8,128)(2,1)} %dynamic-slice_bitcast_fusion.6), channel_id=1, source_target_pairs={{0,8},{4,12},{8,0},{12,4},{16,24},{20,28},{24,16},{28,20},{1,9},{5... | collective-permute-start | bytes 1572872 | tf_op jit(solution)/shard_map/ppermute | solution.py:285
  607.1 44.5 %collective-permute-start.18 = (bf16[128,2048]{1,0:T(8,128)(2,1)}, bf16[128,2048]{1,0:T(8,128)(2,1)S(1)}, u32[]{:S(2)}, u32[]{:S(2)}) collective-permute-start(bf16[128,2048]{1,0:T(8,128)(2,1)} %dynamic-slice_bitcast_fusion.5), channel_id=1, source_target_pairs={{0,16},{4,20},{8,24},{12,28},{16,0},{20,4},{24,8},{28,12},{1,17},{... | collective-permute-start | bytes 1572872 | tf_op jit(solution)/shard_map/ppermute | solution.py:285
  623.2 52.5 %collective-permute-start.22 = (bf16[256,1024]{1,0:T(8,128)(2,1)}, bf16[256,1024]{1,0:T(8,128)(2,1)}, u32[]{:S(2)}, u32[]{:S(2)}) collective-permute-start(bf16[256,1024]{1,0:T(8,128)(2,1)} %dynamic-slice_bitcast_fusion.4), channel_id=1, source_target_pairs={{0,2},{1,3},{2,0},{3,1},{4,6},{5,7},{6,4},{7,5},{8,10},{9,11},{10,... | collective-permute-start | bytes 1572872 | tf_op jit(solution)/shard_map/ppermute | solution.py:285
  624.7 26.9 %collective-permute-start.16 = (f32[22544]{0:T(1024)S(1)}, f32[22544]{0:T(1024)S(1)}, u32[]{:S(2)}, u32[]{:S(2)}) collective-permute-start(f32[22544]{0:T(1024)S(1)} %add.468), channel_id=1, source_target_pairs={{0,2},{1,3},{2,0},{3,1},{4,6},{5,7},{6,4},{7,5},{8,10},{9,11},{10,... | collective-permute-start | bytes 270536 | tf_op jit(solution)/shard_map/ppermute | solution.py:285
  656.7 14.1 %collective-permute-start.20 = (bf16[128,2048]{1,0:T(8,128)(2,1)S(1)}, bf16[128,2048]{1,0:T(8,128)(2,1)S(1)}, u32[]{:S(2)}, u32[]{:S(2)}) collective-permute-start(bf16[128,2048]{1,0:T(8,128)(2,1)S(1)} %bitcast.327), channel_id=1, source_target_pairs={{0,1},{1,0},{2,3},{3,2},{4,5},{5,4},{6,7},{7,6},{8,9},{9,8},{10,11... | collective-permute-start | bytes 1572872 | tf_op jit(solution)/shard_map/ppermute | solution.py:285
  (101 other events, 912.6 us)
Sparse Core Ops, SparseCore 0:
  11.5 85.0 all-gather.3
  100.0 89.2 all-gather.5
  192.2 75.5 all-gather.7

commit v8 on v7

--- a/solution.py
+++ b/solution.py
@@ -454,7 +454,6 @@
     scaled, lse = attend(first, head_scale, query, keys, values, start, hops)
 
     scaled_low, *normed_pieces = together(flat(scaled), *normed_pieces)
-    picked = [pick_columns(piece, core) for piece in normed_pieces]
     branch = dot_nn(scaled_low, output_full) + output_bias
     hat_post, scale_post = moments(branch)
     middle = tokens + hat_post * post_gain + post_shift
@@ -476,6 +475,9 @@
     sums = query_key_sum, value_output_sum = RowSum(one_way), RowSum(other_way)
     sequence = Sequence(jnp.zeros((8, 128), jnp.float32))
     down_sum.send(dot_tn(mixed, grad_low), sequence)
+
+    picked = [sequence(*pick_columns(piece, core)) for piece in (*normed_pieces, scaled_low)]
+    *picked, picked_scaled = picked
 
     low = sequence(grad_low)
     grad_mixed = dot_nt(low, down_full)
@@ -521,7 +523,6 @@
         going = partial + jnp.pad(carried.astype(jnp.float32), ((0, 0), (missing, 0), (0, 0)))
         carried = lower(sequence(going.astype(jnp.bfloat16)))
 
-    picked_scaled = pick_columns(scaled_low, core)
     query_low, grad_branch, *pairs = sequence(query_low, grad_branch, *dkeys, *dvalues)
     dkeys, dvalues = pairs[: len(dkeys)], pairs[len(dkeys) :]
 
@@ -584,7 +585,7 @@
             jnp.sum(grad_mixed, 0),
         ]
     )
-    places = bits_of("seq") + bits_of("dp")
+    places = bits_of("dp") + bits_of("seq")
     vector = sequence(vector)
     vector_came = exchange(vector, *places.pop(0))
 

time: 702 us -> 676 us (0.963)
  waiting for transfers between devices: 236 us -> 209 us
    all_gather x1, waiting for transfers between devices: 25.7 us -> 9.83 us  [local(): lax.all_gather(jnp.concatenate([output_weight, up_weight], 1), BOTH, axis...]
    ppermute x20, waiting for transfers between devices: 42.5 us -> 30.7 us  [exchange(): lax.ppermute(array, axis, [(i, i ^ 1 << bit) for i in range(lax.axis_size...]
    unnamed x202 -> x206, local copies, waits for them, and re-layouts: 14.5 us -> 14.5 us
  transfers between devices with their start and end apart: 28 -> 28, of which waited for: 12 -> 11; matrix products, arithmetic and copies ran while one was open for 39% -> 40% of each run, Pallas kernels for 13% -> 13%
where the time goes in v8:
time: 676 us; the launch traced here: 671 us
  waiting for transfers between devices  209 us (31%)
  matrix products  164 us (24%)
  other arithmetic  97.9 us (14%)
  Pallas kernels  90.6 us (13%)
  local copies, waits for them, and re-layouts  52.7 us (8%)
  starting transfers between devices  41.6 us (6%)
  between operations  15.9 us (2%)
    ppermute x2, waiting for transfers between devices, local(): lower = lambda array: lax.ppermute(array, 'seq', downward)  83 us
    dot_general x10, matrix products, dot_nt(): lax.dot_general(a, b, (((1,), (1,)), ((), ())), preferred_element_type=jn...  68 us
    ppermute x3, waiting for transfers between devices, local(): shift = lambda array: lax.ppermute(array, 'seq', upward)  60.6 us
    dot_general x6, matrix products, dot_nn(): lax.dot_general(a, b, (((1,), (0,)), ((), ())), preferred_element_type=jn...  54.3 us
    pallas_call x1, Pallas kernels, attend_back(): pl.pallas_call(kernel, grid_spec=pltpu.PrefetchScalarGridSpec(num_scalar_...  44.8 us
    dot_general x18, matrix products, dot_tn(): lax.dot_general(a, b, (((0,), (0,)), ((), ())), preferred_element_type=jn...  41.3 us
    ppermute x20, waiting for transfers between devices, exchange(): lax.ppermute(array, axis, [(i, i ^ 1 << bit) for i in range(lax.axis_size...  30.7 us
    pallas_call x1, Pallas kernels, attend(): pl.pallas_call(kernel, grid_spec=pltpu.PrefetchScalarGridSpec(num_scalar_...  29.8 us
  transfers between devices with their start and end apart: 28, of which 11 were waited for; matrix products, arithmetic and copies ran while one was open for 40% of the time, Pallas kernels for 13%

profile of v8, /device:TPU:0, one launch (start us, length us, event | category | flops | bytes accessed | tf_op | source)
XLA Modules:
  0.0 671.3 jit_solution(6095072560609687397)
XLA Ops:
  12.2 6.0 collective-permute-start
  20.7 32.5 %collective-permute-done = bf16[2,288,1024]{2,1,0:T(8,128)(2,1)} collective-permute-done((bf16[2,288,1024]{2,1,0:T(8,128)(2,1)S(1)}, bf16[2,288,1024]{2,1,0:T(8,128)(2,1)}, u32[]{:S(2)}, u32[]{:S(2)}) %collective-permute-start) | collective-permute-done | bytes 1179680 | tf_op jit(solution)/shard_map/ppermute | solution.py:412
  53.2 6.3 collective-permute-start.2
  68.3 28.1 %collective-permute-done.2 = bf16[2,224,1024]{2,1,0:T(8,128)(2,1)} collective-permute-done((bf16[2,224,1024]{2,1,0:T(8,128)(2,1)}, bf16[2,224,1024]{2,1,0:T(8,128)(2,1)}, u32[]{:S(2)}, u32[]{:S(2)}) %collective-permute-start.2) | collective-permute-done | bytes 917536 | tf_op jit(solution)/shard_map/ppermute | solution.py:412
  99.5 9.4 %fusion.85 = f32[1024,3072]{1,0:T(8,128)S(1)} fusion(bf16[1024,1024]{1,0:T(8,128)(2,1)} %fusion.28.array_ref, bf16[1024,3072]{1,0:T(8,128)(2,1)} %all-gather.4.cloned.1.call-done), kind=kOutput, calls=%fused_computation.231 | convolution fusion | flops 6442450944 | bytes 20971520 | tf_op jit(solution)/shard_map/dot_general | solution.py:19
  133.7 29.8 %attend.1 = (bf16[2,512,1024]{2,1,0:T(8,128)(2,1)}, f32[2,4,4,512]{3,2,1,0:T(4,128)}) custom-call(s32[2,2]{1,0:T(2,128)} %slice.180.first_ref, f32[16]{0:T(128)} %scale_ref.3, bf16[2,512,1024]{2,1,0:T(8,128)(2,1)} %bitcast.314, bf16[2,512,1024]{2,1,0:T(8,128)(2,1)} %bitcast.308, bf16[2,512,1024]{2,1,0:T(8,128)(2,1)} %bitcast.310, ...), custom_call_target="tpu_custom_call" | custom-call | flops 33017561088 | bytes 32243712 | tf_op jit(solution)/shard_map/attend/pallas_call | solution.py:142
  179.4 9.8 %all-gather.6.cloned.1.call-done = bf16[1024,5120]{1,0:T(8,128)(2,1)} async-done(((bf16[32,5120]{1,0:T(8,128)(2,1)}), bf16[1024,5120]{1,0:T(8,128)(2,1)}) %all-gather.6.cloned.1.call-update) | async-done | bytes 10485776 | tf_op jit(solution)/shard_map/all_gather | solution.py:425
  199.2 20.7 %multiply_reduce_fusion.2 = (f32[1024]{0:T(1024)S(1)}, f32[1024]{0:T(1024)S(1)}, f32[1024,4096]{1,0:T(8,128)}, f32[1024,4096]{1,0:T(8,128)}) fusion(f32[4096]{0:T(1024)S(1)} %copy-done.80, bf16[1024,5120]{1,0:T(8,128)(2,1)} %all-gather.6.cloned.1.call-done, f32[1024,1024]{1,0:T(8,128)} %copy-done.2, f32[1024]{0:T(1024)S(1)} %copy-done.85, ...), kind=kOutput, calls=%fused_computation.12 | convolution fusion | flops 8628729856 | bytes 46178304 | tf_op jit(solution)/shard_map/dot_general | solution.py:19
  219.9 7.9 %add_convert_fusion = bf16[1024,4096]{1,0:T(8,128)(2,1)S(1)} fusion(f32[1024,4096]{1,0:T(8,128)} %get-tuple-element.471, f32[4096]{0:T(1024)S(1)} %copy-done.79, f32[1024]{0:T(1024)S(1)} %get-tuple-element.509, f32[4096]{0:T(1024)S(1)} %copy-done.57, f32[1024]{0:T(1024)S(1)} %get-tuple-element.508), kind=kLoop, calls=%fused_computation.10 | loop fusion | flops 20971520 | bytes 25206784 | tf_op jit(solution)/shard_map/convert_element_type | solution.py:469
  227.9 9.6 %convolution_convert_fusion.1 = bf16[4096,1024]{1,0:T(8,128)(2,1)S(1)} fusion(bf16[1024,4096]{1,0:T(8,128)(2,1)S(1)} %add_convert_fusion, bf16[1024,1024]{1,0:T(8,128)(2,1)S(1)} %bitcast.272), kind=kOutput, calls=%fused_computation.22 | convolution fusion | flops 8594128896 | bytes 18874368 | tf_op jit(solution)/shard_map/dot_general | solution.py:27
  243.0 24.8 %all-gather.8.cloned.1.call-done = bf16[4096,1024]{1,0:T(8,128)(2,1)} async-done(((bf16[128,1024]{1,0:T(8,128)(2,1)}), bf16[4096,1024]{1,0:T(8,128)(2,1)}) %all-gather.8.cloned.1.call-update) | async-done | bytes 8388624 | tf_op jit(solution)/shard_map/all_gather | solution.py:426
  267.8 20.7 %multiply_reduce_fusion = (f32[4096]{0:T(1024)}, f32[1024]{0:T(1024)S(1)}, f32[1024]{0:T(1024)S(1)}, f32[4096]{0:T(1024)}, f32[1024,4096]{1,0:T(8,128)}) fusion(f32[1024,4096]{1,0:T(8,128)} %get-tuple-element.471, f32[1024]{0:T(1024)S(1)} %get-tuple-element.509, f32[1024]{0:T(1024)S(1)} %get-tuple-element.508, f32[4096]{0:T(1024)S(1)} %copy-done.57, ...), kind=kOutput, calls=%fused_computation.7 | convolution fusion | flops 8627673088 | bytes 44105728 | tf_op jit(solution)/shard_map/dot_general | solution.py:23
  288.5 17.6 %fusion.5 = bf16[1024,4096]{1,0:T(8,128)(2,1)S(1)} fusion(f32[1024,4096]{1,0:T(8,128)} %get-tuple-element.517, f32[1024,4096]{1,0:T(8,128)} %get-tuple-element.516, f32[1024,4096]{1,0:T(8,128)} %get-tuple-element.471, f32[1024]{0:T(1024)S(1)} %get-tuple-element.520, f32[1024]{0:T(1024)S(1)} %get-tuple-element.521, f32[1024]{0:T(1024)S(1)} %get-tuple-element.509, ...), kind=kLoop, calls=%fused_computation.6 | loop fusion | flops 75497472 | bytes 58769408 | tf_op jit(solution)/shard_map/convert_element_type | solution.py:485
  320.6 12.3 %convolution_convert_fusion = bf16[1024,4096]{1,0:T(8,128)(2,1)} fusion(bf16[1024,4096]{1,0:T(8,128)(2,1)S(1)} %fusion.5, f32[1024,1024]{1,0:T(8,128)S(1)} %copy-done.3, f32[1024]{0:T(1024)S(1)} %copy-done.85, f32[1024]{0:T(1024)S(1)} %copy-done.63, f32[1024]{0:T(1024)S(1)} %add_rsqrt_fusion.1, f32[1024]{0:T(1024)S(1)} %broadcast_multiply_fusion.9), kind=kOutput, calls=%fused_computation.21 | convolution fusion | flops 8599371776 | bytes 20987904 | tf_op jit(solution)/shard_map/dot_general | solution.py:27
  340.6 12.9 %fusion.8 = f32[1024,1024]{1,0:T(8,128)S(1)} fusion(bf16[1024,4096]{1,0:T(8,128)(2,1)} %copy-done.12, bf16[1024,5120]{1,0:T(8,128)(2,1)} %all-gather.6.cloned.1.call-done), kind=kOutput, calls=%fused_computation.23 | convolution fusion | flops 8589934592 | bytes 20971520 | tf_op jit(solution)/shard_map/dot_general | solution.py:23
  384.0 44.8 %attend_back.1 = (bf16[2,512,1024]{2,1,0:T(8,128)(2,1)}, bf16[2,512,1024]{2,1,0:T(8,128)(2,1)}, bf16[2,512,1024]{2,1,0:T(8,128)(2,1)}, bf16[2,288,1024]{2,1,0:T(...) custom-call(s32[2,2]{1,0:T(2,128)} %slice.180.first_ref, ...), custom_call_target="tpu_custom_call" | custom-call | flops 55029268480 | bytes 53739520 | tf_op jit(solution)/shard_map/attend_back/pallas_call | solution.py:239
  451.7 66.8 %collective-permute-done.7 = bf16[2,288,1024]{2,1,0:T(8,128)(2,1)S(1)} collective-permute-done((bf16[2,288,1024]{2,1,0:T(8,128)(2,1)S(1)}, bf16[2,288,1024]{2,1,0:T(8,128)(2,1)S(1)}, u32[]{:S(2)}, u32[]{:S(2)}) %collective-permute-start.7) | collective-permute-done | bytes 1179680 | tf_op jit(solution)/shard_map/ppermute | solution.py:511
  555.3 6.1 fusion.42
  566.0 5.9 add_add_fusion
  572.4 6.2 collective-permute-done.14
  587.7 16.2 %collective-permute-done.8 = bf16[2,512,1024]{2,1,0:T(8,128)(2,1)} collective-permute-done((bf16[2,512,1024]{2,1,0:T(8,128)(2,1)}, bf16[2,512,1024]{2,1,0:T(8,128)(2,1)}, u32[]{:S(2)}, u32[]{:S(2)}) %collective-permute-start.8) | collective-permute-done | bytes 2097184 | tf_op jit(solution)/shard_map/ppermute | solution.py:511
  619.4 10.0 %add_convert_fusion.1 = bf16[1024,1024]{1,0:T(8,128)(2,1)} fusion(f32[1024,1024]{1,0:T(8,128)S(1)} %copy-done.5, f32[1024]{0:T(1024)S(1)} %copy-done.86, bf16[1024,4096]{1,0:T(8,128)(2,1)S(1)} %bitcast.267, bf16[4096,1024]{1,0:T(8,128)(2,1)S(1)} %bitcast.343), kind=kOutput, calls=%fused_computation.67 | convolution fusion | flops 8593080320 | bytes 23072768 | tf_op jit(solution)/shard_map/dot_general | solution.py:19
  629.4 12.5 %collective-permute-done.23 = f32[22544]{0:T(1024)S(1)} collective-permute-done((f32[22544]{0:T(1024)S(1)}, f32[22544]{0:T(1024)S(1)}, u32[]{:S(2)}, u32[]{:S(2)}) %collective-permute-start.23) | collective-permute-done | bytes 90208 | tf_op jit(solution)/shard_map/ppermute | solution.py:285
  645.1 9.3 %collective-permute-done.24 = f32[22544]{0:T(1024)S(1)} collective-permute-done((f32[22544]{0:T(1024)S(1)}, f32[22544]{0:T(1024)S(1)}, u32[]{:S(2)}, u32[]{:S(2)}) %collective-permute-start.24) | collective-permute-done | bytes 90208 | tf_op jit(solution)/shard_map/ppermute | solution.py:285
  (419 shorter events, 229.2 us)
Async XLA Ops:
  7.2 92.3 %all-gather.4.cloned.1.call-start = ((), (), s32[]{:S(2)}) async-start(), calls=%async_computation | async-start | bytes 6488064 | tf_op jit(solution)/shard_map/all_gather | solution.py:424
  9.0 180.2 %all-gather.6.cloned.1.call-start = ((), (), s32[]{:S(2)}) async-start(), calls=%async_computation.1 | async-start | bytes 10813440 | tf_op jit(solution)/shard_map/all_gather | solution.py:425
  10.8 257.0 %all-gather.8.cloned.1.call-start = ((), (), s32[]{:S(2)}) async-start(), calls=%async_computation.2 | async-start | bytes 8650752 | tf_op jit(solution)/shard_map/all_gather | solution.py:426
  12.2 40.9 %collective-permute-start = (bf16[2,288,1024]{2,1,0:T(8,128)(2,1)S(1)}, bf16[2,288,1024]{2,1,0:T(8,128)(2,1)}, u32[]{:S(2)}, u32[]{:S(2)}) collective-permute-start(bf16[2,288,1024]{2,1,0:T(8,128)(2,1)S(1)} %slice.182), channel_id=1, source_target_pairs={{0,1},{1,2},{2,3},{4,5},{5,6},{6,7},{8,9},{9,10},{10,11},{12,13},{... | collective-permute-start | bytes 3538952 | tf_op jit(solution)/shard_map/ppermute | solution.py:412
  53.2 43.2 %collective-permute-start.2 = (bf16[2,224,1024]{2,1,0:T(8,128)(2,1)}, bf16[2,224,1024]{2,1,0:T(8,128)(2,1)}, u32[]{:S(2)}, u32[]{:S(2)}) collective-permute-start(bf16[2,224,1024]{2,1,0:T(8,128)(2,1)} %slice.181), channel_id=1, source_target_pairs={{0,1},{1,2},{2,3},{4,5},{5,6},{6,7},{8,9},{9,10},{10,11},{12,13},{... | collective-permute-start | bytes 2752520 | tf_op jit(solution)/shard_map/ppermute | solution.py:412
  64.2 60.4 %collective-permute-start.1 = (bf16[2,288,1024]{2,1,0:T(8,128)(2,1)}, bf16[2,288,1024]{2,1,0:T(8,128)(2,1)S(1)}, u32[]{:S(2)}, u32[]{:S(2)}) collective-permute-start(bf16[2,288,1024]{2,1,0:T(8,128)(2,1)} %collective-permute-done), channel_id=1, source_target_pairs={{0,1},{1,2},{2,3},{4,5},{5,6},{6,7},{8,9},{9,10},{10,11},{12,13},{... | collective-permute-start | bytes 3538952 | tf_op jit(solution)/shard_map/ppermute | solution.py:412
  242.6 69.3 %collective-permute-start.3 = (bf16[2048,1024]{1,0:T(8,128)(2,1)}, bf16[2048,1024]{1,0:T(8,128)(2,1)}, u32[]{:S(2)}, u32[]{:S(2)}) collective-permute-start(bf16[2048,1024]{1,0:T(8,128)(2,1)} %bitcast.14), channel_id=1, source_target_pairs={{0,4},{4,0},{8,12},{12,8},{16,20},{20,16},{24,28},{28,24},{1,5},{5... | collective-permute-start | bytes 12582920 | tf_op jit(solution)/shard_map/ppermute | solution.py:285
  337.8 20.0 %collective-permute-start.4 = (bf16[512,4096]{1,0:T(8,128)(2,1)}, bf16[512,4096]{1,0:T(8,128)(2,1)}, u32[]{:S(2)}, u32[]{:S(2)}) collective-permute-start(bf16[512,4096]{1,0:T(8,128)(2,1)} %bitcast.19), channel_id=1, source_target_pairs={{0,4},{4,0},{8,12},{12,8},{16,20},{20,16},{24,28},{28,24},{1,5},{5... | collective-permute-start | bytes 12582920 | tf_op jit(solution)/shard_map/ppermute | solution.py:285
  339.1 89.7 %collective-permute-start.6 = (bf16[1024,1024]{1,0:T(8,128)(2,1)}, bf16[1024,1024]{1,0:T(8,128)(2,1)}, u32[]{:S(2)}, u32[]{:S(2)}) collective-permute-start(bf16[1024,1024]{1,0:T(8,128)(2,1)} %dynamic-slice_bitcast_fusion), channel_id=1, source_target_pairs={{0,16},{4,20},{8,24},{12,28},{16,0},{20,4},{24,8},{28,12},{1,17},{... | collective-permute-start | bytes 6291464 | tf_op jit(solution)/shard_map/ppermute | solution.py:285
  382.8 50.9 %collective-permute-start.5 = (bf16[256,4096]{1,0:T(8,128)(2,1)}, bf16[256,4096]{1,0:T(8,128)(2,1)}, u32[]{:S(2)}, u32[]{:S(2)}) collective-permute-start(bf16[256,4096]{1,0:T(8,128)(2,1)} %bitcast.22), channel_id=1, source_target_pairs={{0,8},{4,12},{8,0},{12,4},{16,24},{20,28},{24,16},{28,20},{1,9},{5... | collective-permute-start | bytes 6291464 | tf_op jit(solution)/shard_map/ppermute | solution.py:285
  432.5 98.3 %collective-permute-start.9 = (bf16[512,1024]{1,0:T(8,128)(2,1)S(1)}, bf16[512,1024]{1,0:T(8,128)(2,1)S(1)}, u32[]{:S(2)}, u32[]{:S(2)}) collective-permute-start(bf16[512,1024]{1,0:T(8,128)(2,1)S(1)} %dynamic-slice_bitcast_fusion.3), channel_id=1, source_target_pairs={{0,8},{4,12},{8,0},{12,4},{16,24},{20,28},{24,16},{28,20},{1,9},{5... | collective-permute-start | bytes 3145736 | tf_op jit(solution)/shard_map/ppermute | solution.py:285
  436.3 94.5 %collective-permute-start.10 = (bf16[128,4096]{1,0:T(8,128)(2,1)S(1)}, bf16[128,4096]{1,0:T(8,128)(2,1)}, u32[]{:S(2)}, u32[]{:S(2)}) collective-permute-start(bf16[128,4096]{1,0:T(8,128)(2,1)S(1)} %dynamic-slice_bitcast_fusion.2), channel_id=1, source_target_pairs={{0,16},{4,20},{8,24},{12,28},{16,0},{20,4},{24,8},{28,12},{1,17},{... | collective-permute-start | bytes 3145736 | tf_op jit(solution)/shard_map/ppermute | solution.py:285
  440.7 77.7 %collective-permute-start.7 = (bf16[2,288,1024]{2,1,0:T(8,128)(2,1)S(1)}, bf16[2,288,1024]{2,1,0:T(8,128)(2,1)S(1)}, u32[]{:S(2)}, u32[]{:S(2)}) collective-permute-start(bf16[2,288,1024]{2,1,0:T(8,128)(2,1)S(1)} %bitcast.350), channel_id=1, source_target_pairs={{1,0},{2,1},{3,2},{5,4},{6,5},{7,6},{9,8},{10,9},{11,10},{13,12},{... | collective-permute-start | bytes 3538952 | tf_op jit(solution)/shard_map/ppermute | solution.py:511
  533.2 48.0 %collective-permute-start.12 = (bf16[512,1024]{1,0:T(8,128)(2,1)S(1)}, bf16[512,1024]{1,0:T(8,128)(2,1)}, u32[]{:S(2)}, u32[]{:S(2)}) collective-permute-start(bf16[512,1024]{1,0:T(8,128)(2,1)S(1)} %bitcast.323), channel_id=1, source_target_pairs={{0,1},{1,0},{2,3},{3,2},{4,5},{5,4},{6,7},{7,6},{8,9},{9,8},{10,11... | collective-permute-start | bytes 3145736 | tf_op jit(solution)/shard_map/ppermute | solution.py:285
  535.0 68.9 %collective-permute-start.8 = (bf16[2,512,1024]{2,1,0:T(8,128)(2,1)}, bf16[2,512,1024]{2,1,0:T(8,128)(2,1)}, u32[]{:S(2)}, u32[]{:S(2)}) collective-permute-start(bf16[2,512,1024]{2,1,0:T(8,128)(2,1)} %add_convert_fusion.2), channel_id=1, source_target_pairs={{1,0},{2,1},{3,2},{5,4},{6,5},{7,6},{9,8},{10,9},{11,10},{13,12},{... | collective-permute-start | bytes 6291464 | tf_op jit(solution)/shard_map/ppermute | solution.py:511
  552.1 27.8 %collective-permute-start.13 = (bf16[256,2048]{1,0:T(8,128)(2,1)S(1)}, bf16[256,2048]{1,0:T(8,128)(2,1)S(1)}, u32[]{:S(2)}, u32[]{:S(2)}) collective-permute-start(bf16[256,2048]{1,0:T(8,128)(2,1)S(1)} %bitcast.324), channel_id=1, source_target_pairs={{0,8},{4,12},{8,0},{12,4},{16,24},{20,28},{24,16},{28,20},{1,9},{5... | collective-permute-start | bytes 3145736 | tf_op jit(solution)/shard_map/ppermute | solution.py:285
  553.6 25.0 %collective-permute-start.14 = (bf16[256,2048]{1,0:T(8,128)(2,1)S(1)}, bf16[256,2048]{1,0:T(8,128)(2,1)S(1)}, u32[]{:S(2)}, u32[]{:S(2)}) collective-permute-start(bf16[256,2048]{1,0:T(8,128)(2,1)S(1)} %dynamic-slice_bitcast_fusion.1), channel_id=1, source_target_pairs={{0,16},{4,20},{8,24},{12,28},{16,0},{20,4},{24,8},{28,12},{1,17},{... | collective-permute-start | bytes 3145736 | tf_op jit(solution)/shard_map/ppermute | solution.py:285
  585.2 19.4 %collective-permute-start.15 = (f32[22544]{0:T(1024)S(1)}, f32[22544]{0:T(1024)S(1)}, u32[]{:S(2)}, u32[]{:S(2)}) collective-permute-start(f32[22544]{0:T(1024)S(1)} %concatenate.51), channel_id=1, source_target_pairs={{0,4},{4,0},{8,12},{12,8},{16,20},{20,16},{24,28},{28,24},{1,5},{5... | collective-permute-start | bytes 270536 | tf_op jit(solution)/shard_map/ppermute | solution.py:285
  585.3 24.6 %collective-permute-start.17 = (bf16[128,2048]{1,0:T(8,128)(2,1)}, bf16[128,2048]{1,0:T(8,128)(2,1)S(1)}, u32[]{:S(2)}, u32[]{:S(2)}) collective-permute-start(bf16[128,2048]{1,0:T(8,128)(2,1)} %dynamic-slice_bitcast_fusion.6), channel_id=1, source_target_pairs={{0,8},{4,12},{8,0},{12,4},{16,24},{20,28},{24,16},{28,20},{1,9},{5... | collective-permute-start | bytes 1572872 | tf_op jit(solution)/shard_map/ppermute | solution.py:285
  586.0 23.9 %collective-permute-start.18 = (bf16[128,2048]{1,0:T(8,128)(2,1)}, bf16[128,2048]{1,0:T(8,128)(2,1)S(1)}, u32[]{:S(2)}, u32[]{:S(2)}) collective-permute-start(bf16[128,2048]{1,0:T(8,128)(2,1)} %dynamic-slice_bitcast_fusion.5), channel_id=1, source_target_pairs={{0,16},{4,20},{8,24},{12,28},{16,0},{20,4},{24,8},{28,12},{1,17},{... | collective-permute-start | bytes 1572872 | tf_op jit(solution)/shard_map/ppermute | solution.py:285
  603.9 50.6 %collective-permute-start.22 = (bf16[256,1024]{1,0:T(8,128)(2,1)}, bf16[256,1024]{1,0:T(8,128)(2,1)}, u32[]{:S(2)}, u32[]{:S(2)}) collective-permute-start(bf16[256,1024]{1,0:T(8,128)(2,1)} %dynamic-slice_bitcast_fusion.4), channel_id=1, source_target_pairs={{0,2},{1,3},{2,0},{3,1},{4,6},{5,7},{6,4},{7,5},{8,10},{9,11},{10,... | collective-permute-start | bytes 1572872 | tf_op jit(solution)/shard_map/ppermute | solution.py:285
  617.2 24.8 %collective-permute-start.20 = (bf16[128,2048]{1,0:T(8,128)(2,1)S(1)}, bf16[128,2048]{1,0:T(8,128)(2,1)S(1)}, u32[]{:S(2)}, u32[]{:S(2)}) collective-permute-start(bf16[128,2048]{1,0:T(8,128)(2,1)S(1)} %bitcast.329), channel_id=1, source_target_pairs={{0,1},{1,0},{2,3},{3,2},{4,5},{5,4},{6,7},{7,6},{8,9},{9,8},{10,11... | collective-permute-start | bytes 1572872 | tf_op jit(solution)/shard_map/ppermute | solution.py:285
  617.4 24.5 %collective-permute-start.23 = (f32[22544]{0:T(1024)S(1)}, f32[22544]{0:T(1024)S(1)}, u32[]{:S(2)}, u32[]{:S(2)}) collective-permute-start(f32[22544]{0:T(1024)S(1)} %add.472), channel_id=1, source_target_pairs={{0,1},{1,0},{2,3},{3,2},{4,5},{5,4},{6,7},{7,6},{8,9},{9,8},{10,11... | collective-permute-start | bytes 270536 | tf_op jit(solution)/shard_map/ppermute | solution.py:285
  642.2 17.7 %collective-permute-start.21 = (bf16[64,2048]{1,0:T(8,128)(2,1)S(1)}, bf16[64,2048]{1,0:T(8,128)(2,1)S(1)}, u32[]{:S(2)}, u32[]{:S(2)}) collective-permute-start(bf16[64,2048]{1,0:T(8,128)(2,1)S(1)} %dynamic-slice_bitcast_fusion.7), channel_id=1, source_target_pairs={{0,2},{1,3},{2,0},{3,1},{4,6},{5,7},{6,4},{7,5},{8,10},{9,11},{10,... | collective-permute-start | bytes 786440 | tf_op jit(solution)/shard_map/ppermute | solution.py:285
  (103 other events, 825.8 us)
Sparse Core Ops, SparseCore 0:
  11.5 85.0 all-gather.3
  100.0 89.2 all-gather.5
  192.2 75.5 all-gather.7
